TPU v7x, 32 devices: a whole 2x2x4 slice. The times are simulated.
32 devices in a mesh: dp: 8 (over z, x), bn: 4 (over y, core).
Axes of the slice: x: 2, y: 2, z: 4, core: 2. Of those that a mesh axis runs over, the one named last changes fastest.
Arguments:
- features: bfloat16 [128, 19, 19, 1024], P(('dp', 'bn')), may hold values from -8 to 8
- image_counts: int32 [32], P(('dp', 'bn')), may hold values from 2 to 4, as said below
- map_sides: int32 [128], P(('dp', 'bn')), may hold values from 13 to 19, as said below
- split_kernel: bfloat16 [1024, 1024], replicated, may hold values from -0.1875 to 0.1875
- split_gain: float32 [1024], replicated, may hold values from 0.5 to 1.5
- split_shift: float32 [1024], replicated, may hold values from -2 to 2
- inner_kernel: bfloat16 [512, 512], replicated, may hold values from -0.25 to 0.25
- inner_gain: float32 [512], replicated, may hold values from 0.5 to 1.5
- inner_shift: float32 [512], replicated, may hold values from -2 to 2
- spread_kernel: bfloat16 [3, 3, 512, 512], replicated, may hold values from -0.09375 to 0.09375
- spread_gain: float32 [512], replicated, may hold values from 0.5 to 1.5
- spread_shift: float32 [512], replicated, may hold values from -2 to 2
- transition_kernel: bfloat16 [512, 512], replicated, may hold values from -0.25 to 0.25
- transition_gain: float32 [512], replicated, may hold values from 0.5 to 1.5
- transition_shift: float32 [512], replicated, may hold values from -2 to 2
- output_kernel: bfloat16 [1024, 1024], replicated, may hold values from -0.1875 to 0.1875
- output_gain: float32 [1024], replicated, may hold values from 0.5 to 1.5
- output_shift: float32 [1024], replicated, may hold values from -2 to 2
- cotangent: float32 [128, 19, 19, 1024], P(('dp', 'bn')), may hold values from -6 to 6
Outputs:
- result_map: float32 [128, 19, 19, 1024], P(('dp', 'bn'))
- grad_features: float32 [128, 19, 19, 1024], P(('dp', 'bn'))
- grad_split_kernel: float32 [1024, 1024], replicated
- grad_split_gain: float32 [1024], replicated
- grad_split_shift: float32 [1024], replicated
- grad_inner_kernel: float32 [512, 512], replicated
- grad_inner_gain: float32 [512], replicated
- grad_inner_shift: float32 [512], replicated
- grad_spread_kernel: float32 [3, 3, 512, 512], replicated
- grad_spread_gain: float32 [512], replicated
- grad_spread_shift: float32 [512], replicated
- grad_transition_kernel: float32 [512, 512], replicated
- grad_transition_gain: float32 [512], replicated
- grad_transition_shift: float32 [512], replicated
- grad_output_kernel: float32 [1024, 1024], replicated
- grad_output_gain: float32 [1024], replicated
- grad_output_shift: float32 [1024], replicated
Inputs may be any that keep to these rules, and one draw needn't show every extreme that they name: `image_counts`: each device has at least 2 live slots; some device has all 4. `map_sides`: each slot's side is 19, 16 or 13; sides of slots that are not live are to be ignored.
All inputs are finite; a program needn't handle non-finite values.
Results may differ from a plain program's by a relative error of at most 0.0003.
Values sent between devices are 32-bit elements; how exact they have to be, the bound alone decides.
A program may use at most 192 MiB of HBM per device.

v0:
```python
import jax
import jax.numpy as jnp
from jax import lax
from jax.sharding import PartitionSpec as P

SLOTS = 4
MAP = 19


epsilon = 1e-05


def mish(value):
    return value * jnp.tanh(jax.nn.softplus(value))


def convolve(inputs, kernel):
    return lax.conv_general_dilated(
        inputs,
        kernel,
        (1, 1),
        ((1, 1), (1, 1)),
        dimension_numbers=("NHWC", "HWIO", "NHWC"),
        precision=lax.Precision.HIGHEST,
    )


def pointwise(inputs, kernel):
    return jnp.einsum("nhwc,cd->nhwd", inputs, kernel, precision=lax.Precision.HIGHEST)


def kernel_grad(inputs, grad_z):
    return jnp.einsum("nhwc,nhwd->cd", inputs, grad_z, precision=lax.Precision.HIGHEST)


def masks(count_list, side_list):
    image = jnp.arange(side_list.shape[0])
    live = image % SLOTS < count_list[image // SLOTS]
    places = jnp.arange(MAP)
    inside = places[None, :] < side_list[:, None]
    keep = live[:, None, None] & inside[:, :, None] & inside[:, None, :]
    return keep.astype(jnp.float32)[..., None]


def local_sums(z, mask):
    return (jnp.sum(z * mask, axis=(0, 1, 2)), jnp.sum(z * z * mask, axis=(0, 1, 2)))


def finish(z, gain, shift, mask, first_sum, second_sum, total):
    mean = first_sum / total
    square = second_sum / total
    inverse_std = lax.rsqrt(square - mean * mean + epsilon)
    scaled = (z - mean) * inverse_std
    before = gain * scaled + shift
    return (mish(before) * mask, (scaled, inverse_std, before))


def norm_forward(z, gain, shift, mask, total):
    first_sum, second_sum = local_sums(z, mask)
    first_sum, second_sum = lax.psum((first_sum, second_sum), "bn")
    return finish(z, gain, shift, mask, first_sum, second_sum, total)


def norm_backward(grad_act, kept, gain, mask, total):
    scaled, inverse_std, before = kept
    unused, mish_pull = jax.vjp(mish, before)
    grad_before = mish_pull(grad_act * mask)[0]
    local_shift = jnp.sum(grad_before, axis=(0, 1, 2))
    local_gain = jnp.sum(grad_before * scaled, axis=(0, 1, 2))
    sum_shift, sum_gain = lax.psum((local_shift, local_gain), "bn")
    grad_z = mask * gain * inverse_std * (grad_before - (sum_shift + scaled * sum_gain) / total)
    return (grad_z, local_gain, local_shift)


def settle(kernel_part, gain_part, shift_part):
    return (kernel_part, gain_part, shift_part)


def local(
    features,
    image_counts,
    map_sides,
    split_kernel,
    split_gain,
    split_shift,
    inner_kernel,
    inner_gain,
    inner_shift,
    spread_kernel,
    spread_gain,
    spread_shift,
    transition_kernel,
    transition_gain,
    transition_shift,
    output_kernel,
    output_gain,
    output_shift,
    cotangent,
):
    half = inner_kernel.shape[0]
    split_weight = split_kernel.astype(jnp.float32)
    inner_weight = inner_kernel.astype(jnp.float32)
    spread_weight = spread_kernel.astype(jnp.float32)
    transition_weight = transition_kernel.astype(jnp.float32)
    output_weight = output_kernel.astype(jnp.float32)
    mask = masks(image_counts, map_sides)
    masked = features.astype(jnp.float32) * mask
    split_z = pointwise(masked, split_weight)
    first_sum, second_sum = local_sums(split_z, mask)
    first_sum, second_sum, total = lax.psum((first_sum, second_sum, jnp.sum(mask)), "bn")
    split, split_kept = finish(split_z, split_gain, split_shift, mask, first_sum, second_sum, total)
    part = split[..., :half]
    main = split[..., half:]
    inner, inner_kept = norm_forward(
        pointwise(main, inner_weight), inner_gain, inner_shift, mask, total
    )
    branch, spread_kept = norm_forward(
        convolve(inner, spread_weight), spread_gain, spread_shift, mask, total
    )
    joined = main + branch
    trans, trans_kept = norm_forward(
        pointwise(joined, transition_weight), transition_gain, transition_shift, mask, total
    )
    stacked = jnp.concatenate([trans, part], axis=-1)
    result, output_kept = norm_forward(
        pointwise(stacked, output_weight), output_gain, output_shift, mask, total
    )
    grad_z, gain_part, shift_part = norm_backward(cotangent, output_kept, output_gain, mask, total)
    grad_stacked = pointwise(grad_z, output_weight.T)
    output_grads = settle(kernel_grad(stacked, grad_z), gain_part, shift_part)
    grad_trans = grad_stacked[..., :half]
    grad_part = grad_stacked[..., half:]
    grad_z, gain_part, shift_part = norm_backward(
        grad_trans, trans_kept, transition_gain, mask, total
    )
    grad_joined = pointwise(grad_z, transition_weight.T)
    transition_grads = settle(kernel_grad(joined, grad_z), gain_part, shift_part)
    grad_z, gain_part, shift_part = norm_backward(
        grad_joined, spread_kept, spread_gain, mask, total
    )
    unused, spread_pull = jax.vjp(convolve, inner, spread_weight)
    grad_inner, grad_spread = spread_pull(grad_z)
    spread_grads = settle(grad_spread, gain_part, shift_part)
    grad_z, gain_part, shift_part = norm_backward(grad_inner, inner_kept, inner_gain, mask, total)
    grad_main = grad_joined + pointwise(grad_z, inner_weight.T)
    inner_grads = settle(kernel_grad(main, grad_z), gain_part, shift_part)
    grad_split = jnp.concatenate([grad_part, grad_main], axis=-1)
    grad_z, gain_part, shift_part = norm_backward(grad_split, split_kept, split_gain, mask, total)
    grad_features = pointwise(grad_z, split_weight.T) * mask
    split_grads = settle(kernel_grad(masked, grad_z), gain_part, shift_part)
    summed = lax.psum(
        (
            split_grads[0],
            split_grads[1],
            split_grads[2],
            inner_grads[0],
            inner_grads[1],
            inner_grads[2],
            spread_grads[0],
            spread_grads[1],
            spread_grads[2],
            transition_grads[0],
            transition_grads[1],
            transition_grads[2],
            output_grads[0],
            output_grads[1],
            output_grads[2],
        ),
        ("dp", "bn"),
    )
    return (
        result,
        grad_features,
        summed[0],
        summed[1],
        summed[2],
        summed[3],
        summed[4],
        summed[5],
        summed[6],
        summed[7],
        summed[8],
        summed[9],
        summed[10],
        summed[11],
        summed[12],
        summed[13],
        summed[14],
    )


def solution(mesh):
    return jax.shard_map(
        local,
        mesh=mesh,
        in_specs=(
            P(("dp", "bn"), None, None, None),
            P(("dp", "bn")),
            P(("dp", "bn")),
            P(),
            P(),
            P(),
            P(),
            P(),
            P(),
            P(),
            P(),
            P(),
            P(),
            P(),
            P(),
            P(),
            P(),
            P(),
            P(("dp", "bn"), None, None, None),
        ),
        out_specs=(
            P(("dp", "bn"), None, None, None),
            P(("dp", "bn"), None, None, None),
            P(),
            P(),
            P(),
            P(),
            P(),
            P(),
            P(),
            P(),
            P(),
            P(),
            P(),
            P(),
            P(),
            P(),
            P(),
        ),
        check_vma=False,
    )
```

profile of v0, /device:TPU:0, one launch (start us, length us, event | category | flops | bytes accessed | tf_op | source)
XLA Modules:
  0.0 992.0 jit_solution(5745738842142313879)
XLA Ops:
  9.7 19.9 %multiply_reduce_fusion.5 = (f32[1024]{0:T(1024)S(1)}, f32[1024]{0:T(1024)S(1)}, f32[4,19,19,1024]{3,2,1,0:T(8,128)}, f32[4,19,19,1024]{3,2,1,0:T(8,128)}) fusion(f32[4,19,19]{2,1,0:T(8,128)S(1)} %and_convert_fusion, bf16[4,19,19,1024]{3,0,2,1:T(4,128)(2,1)} %param.21, bf16[1024,1024]{1,0:T(8,128)(2,1)S(1)} %copy-done), kind=kOutput, calls=%fused_computation.52 | convolution fusion | flops 18183030784 | bytes 16897680 | tf_op jit(solution)/shard_map/nhwc,cd->nhwd/dot_general | solution.py:29
  29.6 9.3 all-reduce.11
  39.5 7.8 fusion.14
  76.0 43.0 %fusion.109 = (f32[19,32,3,512]{3,1,2,0:T(8,128)S(1)}, f32[19,32,3,512]{3,1,2,0:T(8,128)}) fusion(bf16[3,3,512,512]{3,2,1,0:T(8,128)(2,1)} %param.30, f32[19,4,8,5,512]{4,1,3,2,0:T(4,128)} %select_maximum_fusion.1, pred[32,3]{0,1:T(4,128)(4,1)S(1)} %copy-done.70), kind=kOutput, calls=%fused_computation.176 | convolution fusion | flops 49830199296 | bytes 18415712 | tf_op jit(solution)/shard_map/conv_general_dilated | solution.py:18
  155.1 7.8 fusion.23
  198.3 14.4 %multiply_reduce_fusion.3 = (f32[1024]{0:T(1024)S(1)}, f32[1024]{0:T(1024)S(1)}, f32[4,19,19,1024]{3,2,1,0:T(8,128)}) fusion(f32[4,19,19]{2,1,0:T(8,128)S(1)} %and_convert_fusion, bf16[1024,1024]{1,0:T(8,128)(2,1)S(1)} %copy-done.66, f32[4,19,19,512]{3,2,1,0:T(8,128)S(1)} %copy-done.16, f32[4,19,19,512]{3,2,1,0:T(8,128)S(1)} %fusion.55), kind=kOutput, calls=%fused_computation.47 | convolution fusion | flops 18178594816 | bytes 13940368 | tf_op jit(solution)/shard_map/nhwc,cd->nhwd/dot_general | solution.py:29
  220.1 17.3 %fusion.100 = (f32[1024]{0:T(1024)S(1)}, f32[1024]{0:T(1024)S(1)}, f32[4,19,19,1024]{3,2,1,0:T(8,128)}, f32[4,19,19,1024]{3,2,1,0:T(8,128)}) fusion(f32[1024]{0:T(1024)S(1)} %get-tuple-element.159, f32[4,19,19,1024]{3,2,1,0:T(8,128)} %get-tuple-element.175, f32[1024]{0:T(1024)S(1)} %get-tuple-element.158, f32[1024]{0:T(1024)S(1)} %copy-done.64, ...), kind=kLoop, calls=%fused_computation.172 | loop fusion | flops 42878976 | bytes 23688848 | tf_op jit(solution)/shard_map/reduce_sum | solution.py:68
  250.6 13.9 %fusion.72 = f32[4,19,19,1024]{3,2,1,0:T(8,128)} fusion(f32[4,19,19,1024]{3,2,1,0:T(8,128)S(1)} %subtract_multiply_fusion.1, bf16[1024,1024]{1,0:T(8,128)(2,1)S(1)} %copy-done.67), kind=kOutput, calls=%fused_computation.135 | convolution fusion | flops 18169724928 | bytes 13926400 | tf_op jit(solution)/shard_map/nhwc,cd->nhwd/dot_general | solution.py:29
  264.5 28.9 %fusion.64 = f32[1024,1024]{1,0:T(8,128)} fusion(f32[4,19,19,1024]{3,2,1,0:T(8,128)S(1)} %subtract_multiply_fusion.1, f32[4,19,19,512]{3,2,1,0:T(8,128)S(1)} %copy-done.17, f32[4,19,19,512]{3,2,1,0:T(8,128)S(1)} %copy-done.21), kind=kOutput, calls=%fused_computation.131 | convolution fusion | flops 18171203584 | bytes 16023552 | tf_op jit(solution)/shard_map/nhwc,nhwd->cd/dot_general | solution.py:33
  319.4 9.4 fusion.102
  335.4 18.8 %fusion.85 = f32[512,512]{1,0:T(8,128)} fusion(f32[4,19,19,512]{3,2,1,0:T(8,128)} %copy-done.6, f32[4,19,19,512]{3,2,1,0:T(8,128)} %get-tuple-element.147, f32[4,19,19,512]{3,2,1,0:T(8,128)} %get-tuple-element.174, f32[]{:T(128)} %get-tuple-element.142, f32[512]{0:T(512)S(1)} %get-tuple-element.129, f32[512]{0:T(512)S(1)} %get-tuple-element.130, ...), kind=kOutput, calls=%fused_computation.143 | convolution fusion | flops 4549085184 | bytes 9936532 | tf_op jit(solution)/shard_map/nhwc,nhwd->cd/dot_general | solution.py:33
  354.3 10.6 %fusion.40 = (f32[512]{0:T(512)S(1)}, f32[512]{0:T(512)S(1)}, f32[4,19,19,512]{3,2,1,0:T(8,128)}, f32[4,19,19,512]{3,2,1,0:T(8,128)}) fusion(f32[4,19,19]{2,1,0:T(8,128)S(1)} %and_convert_fusion, bf16[512,512]{1,0:T(8,128)(2,1)S(1)} %copy-done.27, f32[19,4,24,512]{3,2,1,0:T(8,128)S(1)} %copy-done.23, f32[19,4,24,512]{3,2,1,0:T(8,128)S(1)} %copy-done.24, ...), kind=kOutput, calls=%fused_computation.85 | convolution fusion | flops 4566088704 | bytes 21493764 | tf_op jit(solution)/shard_map/nhwc,cd->nhwd/dot_general | solution.py:29
  397.8 34.3 %broadcast_select_fusion = f32[19,32,3,512]{3,1,2,0:T(8,128)S(1)} fusion(pred[32,3]{0,1:T(4,128)(4,1)S(1)} %copy-done.70, bf16[3,3,512,512]{3,2,1,0:T(8,128)(2,1)} %param.30, f32[19,4,8,5,512]{4,1,3,2,0:T(4,128)} %select_maximum_fusion), kind=kOutput, calls=%fused_computation.140 | convolution fusion | flops 49829265408 | bytes 14680160 | tf_op jit(solution)/shard_map/transpose(jvp())/conv_general_dilated | solution.py:18
  444.1 8.4 fusion.101
  459.2 11.2 %convolution_add_fusion = f32[4,19,19,512]{3,2,1,0:T(8,128)} fusion(f32[4,19,19,512]{3,2,1,0:T(8,128)} %get-tuple-element.176, bf16[512,512]{1,0:T(8,128)(2,1)S(1)} %copy-done.69, f32[4,19,19,512]{3,2,1,0:T(8,128)} %get-tuple-element.145, f32[4,19,19,512]{3,2,1,0:T(8,128)} %get-tuple-element.171, f32[512]{0:T(512)S(1)} %get-tuple-element.125, ...), kind=kOutput, calls=%fused_computation.139 | convolution fusion | flops 4549824512 | bytes 12369556 | tf_op jit(solution)/shard_map/nhwc,cd->nhwd/dot_general | solution.py:29
  470.4 10.2 %fusion.80 = f32[512,512]{1,0:T(8,128)} fusion(f32[4,19,19,512]{3,2,1,0:T(8,128)S(1)} %copy-done.15, f32[4,19,19,512]{3,2,1,0:T(8,128)S(1)} %copy-done.22, f32[4,19,19,512]{3,2,1,0:T(8,128)S(1)} %copy-done.2, f32[512]{0:T(512)S(1)} %get-tuple-element.125, f32[512]{0:T(512)S(1)} %get-tuple-element.126, f32[]{:T(128)} %get-tuple-element.142, ...), kind=kOutput, calls=%fused_computation.142 | convolution fusion | flops 4549085184 | bytes 9936532 | tf_op jit(solution)/shard_map/nhwc,nhwd->cd/dot_general | solution.py:33
  480.7 108.9 %fusion.56 = f32[3,3,512,512]{3,2,1,0:T(8,128)} fusion(f32[4,19,19,512]{3,2,1,0:T(8,128)S(1)} %copy-done.9, f32[4,19,19,512]{3,2,1,0:T(8,128)S(1)} %copy-done.19), kind=kOutput, calls=%fused_computation.127 | convolution fusion | flops 38063308800 | bytes 15351808 | tf_op jit(solution)/shard_map/transpose(jvp())/conv_general_dilated | solution.py:18
  589.7 12.9 %fusion.99 = (f32[1024]{0:T(1024)S(1)}, f32[1024]{0:T(1024)S(1)}, f32[4,19,19,1024]{3,2,1,0:T(8,128)}) fusion(f32[1024]{0:T(1024)S(1)} %copy-done.31, f32[4,19,19,1024]{3,2,1,0:T(8,128)} %get-tuple-element.170, f32[1024]{0:T(1024)S(1)} %copy-done.29, f32[1024]{0:T(1024)S(1)} %copy-done.55, f32[1024]{0:T(1024)S(1)} %copy-done.37, ...), kind=kLoop, calls=%fused_computation.171 | loop fusion | flops 41400320 | bytes 17774224 | tf_op jit(solution)/shard_map/reduce_sum | solution.py:68
  608.3 7.4 subtract_multiply_fusion
  618.7 28.9 %fusion.59 = f32[1024,1024]{1,0:T(8,128)} fusion(f32[4,19,19,1024]{3,2,1,0:T(8,128)S(1)} %subtract_multiply_fusion, f32[4,19,19,1024]{3,2,1,0:T(8,128)S(1)} %copy-done.71), kind=kOutput, calls=%fused_computation.130 | convolution fusion | flops 18169724928 | bytes 16023552 | tf_op jit(solution)/shard_map/nhwc,nhwd->cd/dot_general | solution.py:33
  647.7 10.0 %copy.115 = f32[4,19,19,1024]{3,0,2,1:T(4,128)} copy(f32[4,19,19,1024]{3,2,1,0:T(8,128)} %get-tuple-element.152) | data formatting | bytes 11829248
  657.7 14.8 %broadcast_multiply_fusion = f32[4,19,19,1024]{3,2,1,0:T(8,128)S(1)} fusion(f32[4,19,19]{2,1,0:T(8,128)S(1)} %copy-done.11, f32[4,19,19,1024]{3,2,1,0:T(8,128)} %copy-done.13, bf16[1024,1024]{1,0:T(8,128)(2,1)S(1)} %copy-done), kind=kOutput, calls=%fused_computation.126 | convolution fusion | flops 18171203584 | bytes 13932176 | tf_op jit(solution)/shard_map/nhwc,cd->nhwd/dot_general | solution.py:29
  679.6 42.0 %all-reduce = (f32[1024]{0:T(1024)}, f32[1024]{0:T(1024)}, f32[512]{0:T(512)}, f32[512]{0:T(512)}, f32[512]{0:T(512)}, /*index=5*/f32[512]{0:T(512)}, f32[512]{0...) all-reduce(f32[1024]{0:T(1024)S(1)} %get-tuple-element.93, ...), channel_id=1, replica_groups=mesh['dp'=8,'bn'=4] {'dp','bn'}, use_global_device_ids=true, to_apply=%region_43.46 | all-reduce | flops 7168 | bytes 57344 | tf_op jit(solution)/shard_map/psum | solution.py:151
  721.6 247.1 %all-reduce.14.cloned.1.call-done = (f32[1024,1024]{1,0:T(8,128)}, f32[512,512]{1,0:T(8,128)}, f32[3,3,512,512]{3,2,1,0:T(8,128)}, f32[512,512]{1,0:T(8,128)}, f32[1024,1024]{1,0:T(8,128)}) async-done(((f32[1024,1024]{1,0:T(8,128)}, f32[512,512]{1,0:T(8,128)}, f32[3,3,512,512]{3,2,1,0:T(8,128)}, f32[512,512]{1,0:T(8,128)}, f32[1024,1024]{1,0:T(8,128)}), (f32[1024,1024]{1,0:T(8,128)}, f32[512,512]{1,0:T(8,128)}, ...) | async-done | bytes 19922960 | tf_op jit(solution)/shard_map/psum | solution.py:151
  (203 shorter events, 238.4 us)
Async XLA Ops:
  7.2 961.4 %all-reduce.14.cloned.1.call-start = ((), (), s32[]{:S(2)}) async-start(), calls=%async_computation | async-start | bytes 39845888 | tf_op jit(solution)/shard_map/psum | solution.py:151
  9.0 461.4 %copy-start.10 = (f32[4,19,19]{2,1,0:T(8,128)}, f32[4,19,19]{2,1,0:T(8,128)S(1)}, u32[]{:S(2)}) copy-start(f32[4,19,19]{2,1,0:T(8,128)S(1)} %and_convert_fusion) | copy-start | bytes 17332
  9.7 29.8 %copy-start.36 = (f32[1024]{0:T(1024)S(1)}, f32[1024]{0:T(1024)}, u32[]{:S(2)}) copy-start(f32[1024]{0:T(1024)} %param.25) | copy-start | bytes 12292
  9.7 29.8 %copy-start.54 = (f32[1024]{0:T(1024)S(1)}, f32[1024]{0:T(1024)}, u32[]{:S(2)}) copy-start(f32[1024]{0:T(1024)} %param.26) | copy-start | bytes 12292
  198.3 14.4 %copy-start.20 = (f32[4,19,19,512]{3,2,1,0:T(8,128)}, f32[4,19,19,512]{3,2,1,0:T(8,128)S(1)}, u32[]{:S(2)}) copy-start(f32[4,19,19,512]{3,2,1,0:T(8,128)S(1)} %fusion.55) | copy-start | bytes 8871940
  198.3 21.8 %copy-start.56 = (f32[1024]{0:T(1024)S(1)}, f32[1024]{0:T(1024)}, u32[]{:S(2)}) copy-start(f32[1024]{0:T(1024)} %param.37) | copy-start | bytes 12292
  198.3 21.8 %copy-start.64 = (f32[1024]{0:T(1024)S(1)}, f32[1024]{0:T(1024)}, u32[]{:S(2)}) copy-start(f32[1024]{0:T(1024)} %param.38) | copy-start | bytes 12292
  264.5 28.9 %copy-start.3 = (f32[19,32,3,512]{3,1,2,0:T(8,128)S(1)}, f32[19,32,3,512]{3,1,2,0:T(8,128)}, u32[]{:S(2)}) copy-start(f32[19,32,3,512]{3,1,2,0:T(8,128)} %get-tuple-element.151) | copy-start | bytes 11206660
  328.8 25.4 %copy-start.46 = (f32[512]{0:T(512)}, f32[512]{0:T(512)S(1)}, u32[]{:S(2)}) copy-start(f32[512]{0:T(512)S(1)} %get-tuple-element.104) | copy-start | bytes 6148
  328.8 25.4 %copy-start.48 = (f32[512]{0:T(512)}, f32[512]{0:T(512)S(1)}, u32[]{:S(2)}) copy-start(f32[512]{0:T(512)S(1)} %get-tuple-element.105) | copy-start | bytes 6148
  335.4 18.8 %copy-start.4 = (f32[4,19,19,512]{3,2,1,0:T(8,128)S(1)}, f32[4,19,19,512]{3,2,1,0:T(8,128)}, u32[]{:S(2)}) copy-start(f32[4,19,19,512]{3,2,1,0:T(8,128)} %get-tuple-element.174) | copy-start | bytes 8871940
  335.4 18.8 %copy-start.23 = (f32[19,4,24,512]{3,2,1,0:T(8,128)S(1)}, f32[19,4,24,512]{3,2,1,0:T(8,128)}, u32[]{:S(2)}) copy-start(f32[19,4,24,512]{3,2,1,0:T(8,128)} %reshape.156) | copy-start | bytes 11206660
  335.4 18.8 %copy-start.24 = (f32[19,4,24,512]{3,2,1,0:T(8,128)S(1)}, f32[19,4,24,512]{3,2,1,0:T(8,128)}, u32[]{:S(2)}) copy-start(f32[19,4,24,512]{3,2,1,0:T(8,128)} %reshape.145) | copy-start | bytes 11206660
  335.4 18.8 %copy-start.25 = (f32[4,19,19,512]{3,2,1,0:T(8,128)S(1)}, f32[4,19,19,512]{3,2,1,0:T(8,128)}, u32[]{:S(2)}) copy-start(f32[4,19,19,512]{3,2,1,0:T(8,128)} %get-tuple-element.147) | copy-start | bytes 8871940
  444.1 15.0 %copy-start.69 = (bf16[512,512]{1,0:T(8,128)(2,1)S(1)}, bf16[512,512]{1,0:T(8,128)(2,1)}, u32[]{:S(2)}) copy-start(bf16[512,512]{1,0:T(8,128)(2,1)} %param.27) | copy-start | bytes 1572868
  452.5 17.8 %copy-start.50 = (f32[512]{0:T(512)}, f32[512]{0:T(512)S(1)}, u32[]{:S(2)}) copy-start(f32[512]{0:T(512)S(1)} %get-tuple-element.100) | copy-start | bytes 6148
  452.5 17.8 %copy-start.52 = (f32[512]{0:T(512)}, f32[512]{0:T(512)S(1)}, u32[]{:S(2)}) copy-start(f32[512]{0:T(512)S(1)} %get-tuple-element.101) | copy-start | bytes 6148
  480.6 109.0 %copy-start.7 = (f32[4,19,19,512]{3,2,1,0:T(8,128)S(1)}, f32[4,19,19,512]{3,2,1,0:T(8,128)}, u32[]{:S(2)}) copy-start(f32[4,19,19,512]{3,2,1,0:T(8,128)} %get-tuple-element.156) | copy-start | bytes 8871940
  480.6 109.0 %copy-start.11 = (f32[4,19,19]{2,1,0:T(8,128)S(1)}, f32[4,19,19]{2,1,0:T(8,128)}, u32[]{:S(2)}) copy-start(f32[4,19,19]{2,1,0:T(8,128)} %copy-done.10) | copy-start | bytes 17332
  480.6 109.0 %copy-start.18 = (f32[4,19,19,512]{3,2,1,0:T(8,128)S(1)}, f32[4,19,19,512]{3,2,1,0:T(8,128)}, u32[]{:S(2)}) copy-start(f32[4,19,19,512]{3,2,1,0:T(8,128)} %convolution_add_fusion) | copy-start | bytes 8871940
  480.6 109.0 %copy-start.29 = (f32[1024]{0:T(1024)S(1)}, f32[1024]{0:T(1024)}, u32[]{:S(2)}) copy-start(f32[1024]{0:T(1024)} %copy-done.28) | copy-start | bytes 12292
  480.6 109.0 %copy-start.31 = (f32[1024]{0:T(1024)S(1)}, f32[1024]{0:T(1024)}, u32[]{:S(2)}) copy-start(f32[1024]{0:T(1024)} %copy-done.30) | copy-start | bytes 12292
  480.6 109.0 %copy-start.37 = (f32[1024]{0:T(1024)S(1)}, f32[1024]{0:T(1024)}, u32[]{:S(2)}) copy-start(f32[1024]{0:T(1024)} %param.25) | copy-start | bytes 12292
  480.6 109.0 %copy-start.55 = (f32[1024]{0:T(1024)S(1)}, f32[1024]{0:T(1024)}, u32[]{:S(2)}) copy-start(f32[1024]{0:T(1024)} %param.26) | copy-start | bytes 12292
  (49 other events, 392.1 us)
Sparse Core Ops, SparseCore 0:
  647.8 320.8 all-reduce.13
where the time goes:
time: 998 us; the launch traced here: 992 us
  matrix products  369 us (37%)
  waiting for transfers between devices  247 us (25%)
  local copies, waits for them, and re-layouts  131 us (13%)
  other arithmetic  122 us (12%)
  blocking collectives  107 us (11%)
  between operations  16.3 us (2%)
    psum x1, waiting for transfers between devices, local(): lax.psum((split_grads[0], split_grads[1], split_grads[2], inner_grads[0],...  247 us
    conv_general_dilated x3, matrix products, convolve(): lax.conv_general_dilated(inputs, kernel, (1, 1), ((1, 1), (1, 1)), dimens...  186 us
    dot_general x8, matrix products, pointwise(): jnp.einsum('nhwc,cd->nhwd', inputs, kernel, precision=lax.Precision.HIGHEST)  95.4 us
    dot_general x4, matrix products, kernel_grad(): jnp.einsum('nhwc,nhwd->cd', inputs, grad_z, precision=lax.Precision.HIGHEST)  86.9 us
    reduce_sum x4, other arithmetic, norm_backward(): local_shift = jnp.sum(grad_before, axis=(0, 1, 2))  48 us
    psum x1, blocking collectives, local(): lax.psum((split_grads[0], split_grads[1], split_grads[2], inner_grads[0],...  42 us
    unnamed x153, local copies, waits for them, and re-layouts  40.6 us
    psum x5, blocking collectives, norm_backward(): sum_shift, sum_gain = lax.psum((local_shift, local_gain), 'bn')  30.5 us
  transfers between devices with their start and end apart: 1, of which 1 were waited for; matrix products, arithmetic and copies ran while one was open for 3% of the time, Pallas kernels for 0%

commit v1 on v0

v1 whole, which is shorter than its diff:
```python
import functools

import jax
import jax.numpy as jnp
from jax import lax
from jax.experimental import pallas as pl
from jax.experimental.pallas import tpu as pltpu
from jax.sharding import PartitionSpec as P

EPS = 1e-05
GUARD = 24
CHUNK = 16
F32 = jnp.float32
BF16 = jnp.bfloat16


def round_up(value, step):
    return -(-value // step) * step


def params(megabytes=56):
    return pltpu.CompilerParams(vmem_limit_bytes=megabytes * 1024 * 1024)


def whole(array):
    zeros = (0,) * len(array.shape)
    return pl.BlockSpec(array.shape, lambda *_: zeros, pipeline_mode=pl.Buffered(1))


def out_whole(shape):
    zeros = (0,) * len(shape)
    return pl.BlockSpec(shape, lambda *_: zeros)


def rows(pitch, width, column=0):
    return pl.BlockSpec((pitch, width), lambda i: (i, column))


def rows2(pitch, width):
    return pl.BlockSpec((2, pitch, width), lambda i: (0, i, 0))


def image(shape):
    return pl.BlockSpec((1,) + tuple(shape[1:]), lambda i: (i, 0, 0, 0))


def sds(shape, dtype=F32):
    return jax.ShapeDtypeStruct(tuple(shape), dtype)


def dot(left, right):
    return jnp.dot(left, right, preferred_element_type=F32)


def dot_t(left, right):
    return lax.dot_general(left, right, (((1,), (1,)), ((), ())), preferred_element_type=F32)


def split_store(ref, place, value):
    high = value.astype(BF16)
    ref[(0,) + place] = high
    ref[(1,) + place] = (value - high.astype(F32)).astype(BF16)


def moments(stats_ref, total, columns):
    mean = stats_ref[0:1, columns] / total
    square = stats_ref[1:2, columns] / total
    return mean, lax.rsqrt(square - mean * mean + EPS)


def mish(y):
    t = jnp.exp(jnp.minimum(y, 30.0))
    n = t * (t + 2.0)
    return y * (n / (n + 2.0))


def mish_slope(y):
    t = jnp.exp(jnp.minimum(y, 30.0))
    n = t * (t + 2.0)
    r = 1.0 / (n + 2.0)
    return n * r + y * (((4.0 * t) * (t + 1.0) * r) * r)


def fold(value):
    return jnp.sum(value.reshape(value.shape[0] // 8, 8, value.shape[1]), axis=0)


def over_rows(count, body, carry=None, unroll=2):
    def step(k, c):
        return body(pl.ds(pl.multiple_of(k * CHUNK, CHUNK), CHUNK), c)

    return lax.fori_loop(0, count // CHUNK, step, carry, unroll=unroll)


def column_blocks(width, block=512):
    return [slice(c, c + block) for c in range(0, width, block)]


def add_sums(sums_ref, columns, pieces):
    for k, piece in enumerate(pieces):
        sums_ref[k : k + 1, columns] += jnp.sum(piece, axis=0, keepdims=True)


def start_sums(sums_ref):
    @pl.when(pl.program_id(0) == 0)
    def _():
        sums_ref[...] = jnp.zeros_like(sums_ref)


def sum_squares(z_ref, sums_ref, mask_ref=None):
    for columns in column_blocks(z_ref.shape[1]):
        width = columns.stop - columns.start

        def body(r, carry):
            value = z_ref[r, columns]
            kept = value if mask_ref is None else value * mask_ref[r, 0:1]
            return (carry[0] + fold(kept), carry[1] + fold(kept * value))

        zero = jnp.zeros((8, width), F32)
        add_sums(sums_ref, columns, over_rows(z_ref.shape[0], body, (zero, zero)))


def product2(ref, place, weight):
    high = ref[(0,) + place]
    low = ref[(1,) + place]
    return dot(high, weight) + dot(low, weight)


def product2_t(ref, place, weight):
    high = ref[(0,) + place]
    low = ref[(1,) + place]
    return dot_t(high, weight) + dot_t(low, weight)


def compact(source_ref, scratch_ref):
    side = source_ref.shape[1]
    for y in range(side):
        scratch_ref[y * side : (y + 1) * side, :] = source_ref[0, y].astype(F32)
    scratch_ref[side * side :, :] = jnp.zeros((scratch_ref.shape[0] - side * side, scratch_ref.shape[1]), F32)


def spread_out(scratch_ref, target_ref):
    side = target_ref.shape[1]
    for y in range(side):
        target_ref[0, y] = scratch_ref[y * side : (y + 1) * side, :]


def split_kernel_body(features_ref, mask_ref, w_ref, x_ref, z_ref, sums_ref, scratch_ref):
    compact(features_ref, scratch_ref)

    def body(r, _):
        x_ref[r, :] = (scratch_ref[r, :] * mask_ref[r, 0:1]).astype(BF16)

    over_rows(x_ref.shape[0], body)
    z_ref[...] = dot(x_ref[...], w_ref[...])
    start_sums(sums_ref)
    sum_squares(z_ref, sums_ref)
    count = jnp.sum(mask_ref[...], axis=0, keepdims=True)
    sums_ref[2:3, 0:128] += count


def inner_body(z_ref, stats_ref, gain_ref, shift_ref, mask_ref, w_ref, part_ref, main_ref, main2_ref, zi_ref, sums_ref):
    total = stats_ref[2:3, 0:1]
    half = w_ref.shape[0]
    for index, columns in enumerate(column_blocks(2 * half, half)):
        mean, inverse = moments(stats_ref, total, columns)
        scale, shift = gain_ref[0:1, columns] * inverse, shift_ref[0:1, columns]

        def body(r, _):
            act = mish((z_ref[r, columns] - mean) * scale + shift) * mask_ref[r, 0:1]
            if index == 0:
                split_store(part_ref, (r,), act)
            else:
                main_ref[r, :] = act
                split_store(main2_ref, (r,), act)

        over_rows(z_ref.shape[0], body)
    zi_ref[...] = product2(main2_ref, (), w_ref[...])
    start_sums(sums_ref)
    sum_squares(zi_ref, sums_ref)


def taps(side):
    return [(dy * side + dx, dx) for dy in (-1, 0, 1) for dx in (-1, 0, 1)]


def spread_body(side, z_ref, total_ref, stats_ref, gain_ref, shift_ref, mask_ref, edge_ref, w_ref, inner_ref, zs_ref, sums_ref, padded_ref, pair_ref):
    total = total_ref[2:3, 0:1]
    pitch = z_ref.shape[0]
    columns = slice(None)
    mean, inverse = moments(stats_ref, total, columns)
    scale, shift = gain_ref[...] * inverse, shift_ref[...]
    padded_ref[0:GUARD, :] = jnp.zeros((GUARD, padded_ref.shape[1]), F32)
    padded_ref[GUARD + pitch :, :] = jnp.zeros((GUARD, padded_ref.shape[1]), F32)

    def body(r, _):
        act = mish((z_ref[r, :] - mean) * scale + shift) * mask_ref[r, 0:1]
        padded_ref[pl.ds(r.start + GUARD, CHUNK), :] = act
        split_store(inner_ref, (r,), act)

    over_rows(pitch, body)
    for tap, (move, dx) in enumerate(taps(side)):
        if move == 0:
            part = product2(inner_ref, (), w_ref[tap])
        else:
            moved = padded_ref[GUARD + move : GUARD + move + pitch, :]
            if dx:
                moved = moved * edge_ref[:, dx + 1 : dx + 2]
            split_store(pair_ref, (slice(None),), moved)
            part = product2(pair_ref, (), w_ref[tap])
        if tap == 0:
            zs_ref[...] = part
        else:
            zs_ref[...] += part
    start_sums(sums_ref)
    sum_squares(zs_ref, sums_ref, mask_ref)


def transition_body(z_ref, total_ref, stats_ref, gain_ref, shift_ref, mask_ref, main_ref, w_ref, joined_ref, zt_ref, sums_ref):
    total = total_ref[2:3, 0:1]
    mean, inverse = moments(stats_ref, total, slice(None))
    scale, shift = gain_ref[...] * inverse, shift_ref[...]

    def body(r, _):
        act = mish((z_ref[r, :] - mean) * scale + shift) * mask_ref[r, 0:1]
        split_store(joined_ref, (r,), act + main_ref[r, :])

    over_rows(z_ref.shape[0], body)
    zt_ref[...] = product2(joined_ref, (), w_ref[...])
    start_sums(sums_ref)
    sum_squares(zt_ref, sums_ref)


def output_body(z_ref, total_ref, stats_ref, gain_ref, shift_ref, mask_ref, part_ref, w_ref, trans_ref, zo_ref, sums_ref):
    total = total_ref[2:3, 0:1]
    mean, inverse = moments(stats_ref, total, slice(None))
    scale, shift = gain_ref[...] * inverse, shift_ref[...]
    half = z_ref.shape[1]

    def body(r, _):
        act = mish((z_ref[r, :] - mean) * scale + shift) * mask_ref[r, 0:1]
        split_store(trans_ref, (r,), act)

    over_rows(z_ref.shape[0], body)
    zo_ref[...] = product2(part_ref, (), w_ref[half:, :])
    zo_ref[...] += product2(trans_ref, (), w_ref[:half, :])
    start_sums(sums_ref)
    sum_squares(zo_ref, sums_ref)


def result_body(z_ref, total_ref, stats_ref, gain_ref, shift_ref, mask_ref, cotangent_ref, result_ref, dy_ref, sums_ref, scratch_ref):
    total = total_ref[2:3, 0:1]
    compact(cotangent_ref, scratch_ref)
    start_sums(sums_ref)
    for columns in column_blocks(z_ref.shape[1]):
        mean, inverse = moments(stats_ref, total, columns)
        gain, shift = gain_ref[0:1, columns], shift_ref[0:1, columns]

        def body(r, carry):
            mask = mask_ref[r, 0:1]
            scaled = (z_ref[r, columns] - mean) * inverse
            y = scaled * gain + shift
            t = jnp.exp(jnp.minimum(y, 30.0))
            n = t * (t + 2.0)
            inv = 1.0 / (n + 2.0)
            ratio = n * inv
            slope = ratio + y * (((4.0 * t) * (t + 1.0) * inv) * inv)
            dy = scratch_ref[r, columns] * mask * slope
            scratch_ref[r, columns] = y * ratio * mask
            dy_ref[r, columns] = dy
            return (carry[0] + fold(dy), carry[1] + fold(dy * scaled))

        zero = jnp.zeros((8, columns.stop - columns.start), F32)
        add_sums(sums_ref, columns, over_rows(z_ref.shape[0], body, (zero, zero)))
    spread_out(scratch_ref, result_ref)


def norm_slope(z_ref, grad, mask_ref, r, columns, mean, inverse, gain, shift):
    scaled = (z_ref[r, columns] - mean) * inverse
    dy = grad * mask_ref[r, 0:1] * mish_slope(scaled * gain + shift)
    return dy, (fold(dy), fold(dy * scaled))


def settle(dy, z, mask, mean, inverse, factor, first, second):
    scaled = (z - mean) * inverse
    return mask * factor * (dy - (first + scaled * second))


def output_back_body(dy_ref, zo_ref, so_ref, go_ref, qo_ref, total_ref, mask_ref, w_ref, zt_ref, st_ref, gt_ref, bt_ref, zp_ref, gp_ref, bp_ref, dz_ref, dyt_ref, dyp_ref, sums_ref, grad_ref):
    total = total_ref[2:3, 0:1]
    for columns in column_blocks(zo_ref.shape[1]):
        mean, inverse = moments(so_ref, total, columns)
        factor = go_ref[0:1, columns] * inverse
        first, second = qo_ref[0:1, columns] / total, qo_ref[1:2, columns] / total

        def body(r, _):
            dz = settle(dy_ref[r, columns], zo_ref[r, columns], mask_ref[r, 0:1], mean, inverse, factor, first, second)
            split_store(dz_ref, (r, columns), dz)

        over_rows(zo_ref.shape[0], body)
    grad_ref[...] = product2_t(dz_ref, (), w_ref[...])
    start_sums(sums_ref)
    half = zt_ref.shape[1]
    for index, (z_ref, s_ref, g_ref, b_ref, out_ref) in enumerate(((zt_ref, st_ref, gt_ref, bt_ref, dyt_ref), (zp_ref, total_ref, gp_ref, bp_ref, dyp_ref))):
        columns = slice(index * half, (index + 1) * half)
        own = slice(0, half)
        mean, inverse = moments(s_ref, total, own)
        gain, shift = g_ref[0:1, own], b_ref[0:1, own]

        def body(r, carry):
            dy, sums = norm_slope(z_ref, grad_ref[r, columns], mask_ref, r, own, mean, inverse, gain, shift)
            out_ref[r, :] = dy
            return (carry[0] + sums[0], carry[1] + sums[1])

        zero = jnp.zeros((8, half), F32)
        add_sums(sums_ref, columns, over_rows(zt_ref.shape[0], body, (zero, zero)))


def transition_back_body(dyt_ref, dyp_ref, zt_ref, st_ref, gt_ref, q_ref, total_ref, mask_ref, w_ref, zp_ref, gp_ref, zs_ref, ss_ref, gs_ref, bs_ref, dz_ref, dzp_ref, grad_ref, dys_ref, sums_ref):
    total = total_ref[2:3, 0:1]
    half = zt_ref.shape[1]
    own = slice(0, half)
    for index, (dy_ref, z_ref, s_ref, g_ref, out_ref) in enumerate(((dyt_ref, zt_ref, st_ref, gt_ref, dz_ref), (dyp_ref, zp_ref, total_ref, gp_ref, dzp_ref))):
        columns = slice(index * half, (index + 1) * half)
        mean, inverse = moments(s_ref, total, own)
        factor = g_ref[0:1, own] * inverse
        first, second = q_ref[0:1, columns] / total, q_ref[1:2, columns] / total

        def body(r, _):
            dz = settle(dy_ref[r, :], z_ref[r, :], mask_ref[r, 0:1], mean, inverse, factor, first, second)
            split_store(out_ref, (r,), dz)

        over_rows(zt_ref.shape[0], body)
    grad_ref[...] = product2_t(dz_ref, (), w_ref[...])
    start_sums(sums_ref)
    mean, inverse = moments(ss_ref, total, own)
    gain, shift = gs_ref[...], bs_ref[...]

    def tail(r, carry):
        dy, sums = norm_slope(zs_ref, grad_ref[r, :], mask_ref, r, own, mean, inverse, gain, shift)
        dys_ref[r, :] = dy
        return (carry[0] + sums[0], carry[1] + sums[1])

    zero = jnp.zeros((8, half), F32)
    add_sums(sums_ref, own, over_rows(zt_ref.shape[0], tail, (zero, zero)))


def spread_back_body(side, dy_ref, z_ref, s_ref, g_ref, q_ref, total_ref, mask_ref, edge_ref, w_ref, inner_ref, zi_ref, si_ref, gi_ref, bi_ref, dw_ref, dyi_ref, sums_ref, padded_ref, pair_ref, turned_ref, grad_ref):
    total = total_ref[2:3, 0:1]
    count, half = z_ref.shape
    tap = pl.program_id(0)

    @pl.when(tap == 0)
    def _():
        padded_ref[0:GUARD, :] = jnp.zeros((GUARD, half), F32)
        padded_ref[GUARD + count :, :] = jnp.zeros((GUARD, half), F32)
        mean, inverse = moments(s_ref, total, slice(None))
        factor = g_ref[...] * inverse
        first, second = q_ref[0:1, :] / total, q_ref[1:2, :] / total

        def body(r, _):
            dz = settle(dy_ref[r, :], z_ref[r, :], mask_ref[r, 0:1], mean, inverse, factor, first, second)
            padded_ref[pl.ds(r.start + GUARD, CHUNK), :] = dz

        over_rows(count, body)
        turned_ref[0:half, :] = inner_ref[0].T
        turned_ref[half:, :] = inner_ref[1].T
        grad_ref[...] = jnp.zeros_like(grad_ref)

    for index, (move, dx) in enumerate(taps(side)):

        @pl.when(tap == index)
        def _(move=move, dx=dx):
            moved = padded_ref[GUARD - move : GUARD - move + count, :]
            if dx:
                moved = moved * edge_ref[:, 1 - dx : 2 - dx]
            split_store(pair_ref, (slice(None),), moved)

    both = dot(turned_ref[...], pair_ref[0])
    dw_ref[0] = both[0:half] + both[half:] + dot(turned_ref[0:half, :], pair_ref[1])
    grad_ref[...] += product2_t(pair_ref, (), w_ref[0])

    @pl.when(tap == pl.num_programs(0) - 1)
    def _():
        sums_ref[...] = jnp.zeros_like(sums_ref)
        own = slice(0, half)
        mean, inverse = moments(si_ref, total, own)
        gain, shift = gi_ref[...], bi_ref[...]

        def tail(r, carry):
            dy, sums = norm_slope(zi_ref, grad_ref[r, :], mask_ref, r, own, mean, inverse, gain, shift)
            dyi_ref[r, :] = dy
            return (carry[0] + sums[0], carry[1] + sums[1])

        zero = jnp.zeros((8, half), F32)
        add_sums(sums_ref, own, over_rows(count, tail, (zero, zero)))


def inner_back_body(dy_ref, zi_ref, si_ref, gi_ref, q_ref, total_ref, mask_ref, w_ref, joined_ref, zm_ref, gm_ref, bm_ref, dz_ref, dym_ref, sums_ref, grad_ref):
    total = total_ref[2:3, 0:1]
    half = zi_ref.shape[1]
    own = slice(0, half)
    upper = slice(half, 2 * half)
    mean, inverse = moments(si_ref, total, own)
    factor = gi_ref[...] * inverse
    first, second = q_ref[0:1, :] / total, q_ref[1:2, :] / total

    def body(r, _):
        dz = settle(dy_ref[r, :], zi_ref[r, :], mask_ref[r, 0:1], mean, inverse, factor, first, second)
        split_store(dz_ref, (r,), dz)

    over_rows(zi_ref.shape[0], body)
    grad_ref[...] = product2_t(dz_ref, (), w_ref[...])
    start_sums(sums_ref)
    mean, inverse = moments(total_ref, total, upper)
    gain, shift = gm_ref[0:1, upper], bm_ref[0:1, upper]

    def tail(r, carry):
        dy, sums = norm_slope(zm_ref, grad_ref[r, :] + joined_ref[r, :], mask_ref, r, own, mean, inverse, gain, shift)
        dym_ref[r, :] = dy
        return (carry[0] + sums[0], carry[1] + sums[1])

    zero = jnp.zeros((8, half), F32)
    add_sums(sums_ref, own, over_rows(zi_ref.shape[0], tail, (zero, zero)))


def split_back_body(dy_ref, zm_ref, q_ref, total_ref, g_ref, mask_ref, dzp_ref, w_ref, dz_ref, grad_ref, scratch_ref):
    total = total_ref[2:3, 0:1]
    half = zm_ref.shape[1]
    upper = slice(half, 2 * half)
    mean, inverse = moments(total_ref, total, upper)
    factor = g_ref[0:1, upper] * inverse
    first, second = q_ref[0:1, :] / total, q_ref[1:2, :] / total

    def body(r, _):
        dz = settle(dy_ref[r, :], zm_ref[r, :], mask_ref[r, 0:1], mean, inverse, factor, first, second)
        split_store(dz_ref, (r,), dz)

    over_rows(zm_ref.shape[0], body)
    scratch_ref[...] = product2_t(dzp_ref, (), w_ref[:, :half])
    scratch_ref[...] += product2_t(dz_ref, (), w_ref[:, half:])
    spread_out(scratch_ref, grad_ref)


def weight_body(x_ref, dz_ref, dw_ref):
    turned = x_ref[0].T
    value = dot(turned, dz_ref[0]) + dot(turned, dz_ref[1])
    if x_ref.shape[0] == 2:
        value += dot(x_ref[1].T, dz_ref[0])
    dw_ref[...] = value


def weight_grad(x, dz, block=256):
    parts, count, width = x.shape
    wide = dz.shape[2]
    return pl.pallas_call(
        weight_body,
        grid=(width // block,),
        in_specs=[pl.BlockSpec((parts, count, block), lambda i: (0, 0, i)), whole(dz)],
        out_specs=pl.BlockSpec((block, wide), lambda i: (i, 0)),
        out_shape=sds((width, wide)),
        compiler_params=params(),
    )(x, dz)


def local(
    features, image_counts, map_sides,
    split_kernel, split_gain, split_shift, inner_kernel, inner_gain, inner_shift,
    spread_kernel, spread_gain, spread_shift, transition_kernel, transition_gain, transition_shift,
    output_kernel, output_gain, output_shift, cotangent,
):
    slots, side, _, full = features.shape
    half = inner_kernel.shape[0]
    pitch = round_up(side * side, 128)
    count = slots * pitch
    grid = (slots,)
    row = jnp.arange(pitch)
    y, x = row // side, row % side
    live = jnp.arange(slots) < image_counts[0]
    keep = live[:, None] & (y[None, :] < map_sides[:, None]) & (x[None, :] < map_sides[:, None])
    mask = jnp.broadcast_to(keep.astype(F32).reshape(count, 1), (count, 128))
    lane = jnp.arange(128)[None, :]
    edges = jnp.where(lane == 0, (x > 0)[:, None], jnp.where(lane == 2, (x < side - 1)[:, None], True)).astype(F32)
    edges = jnp.tile(edges, (slots, 1))
    (split_gain, split_shift, inner_gain, inner_shift, spread_gain, spread_shift, transition_gain, transition_shift, output_gain, output_shift) = (
        item.reshape(1, -1)
        for item in (split_gain, split_shift, inner_gain, inner_shift, spread_gain, spread_shift, transition_gain, transition_shift, output_gain, output_shift)
    )
    spread_weight = spread_kernel.reshape(9, half, half)

    def group(sums):
        return lax.psum(sums, "bn")

    sums_full, sums_half = out_whole((8, full)), out_whole((8, half))
    r_half, r_full, r_mask = rows(pitch, half), rows(pitch, full), rows(pitch, 128)
    pair_half, pair_full = rows2(pitch, half), rows2(pitch, full)

    def call(body, ins, outs, scratch=(), steps=grid):
        return pl.pallas_call(
            body,
            grid=steps,
            in_specs=[spec for _, spec in ins],
            out_specs=[spec for _, spec in outs],
            out_shape=[shape for shape, _ in outs],
            scratch_shapes=list(scratch),
            compiler_params=params(),
        )(*[array for array, _ in ins])

    def fixed(array):
        return (array, whole(array))

    x0, z_split, s_split = call(
        split_kernel_body,
        [(features, image(features.shape)), (mask, r_mask), fixed(split_kernel)],
        [(sds((count, full), BF16), r_full), (sds((count, full)), r_full), (sds((8, full)), sums_full)],
        [pltpu.VMEM((pitch, full), F32)],
    )
    s_split = group(s_split)
    part2, main, main2, z_inner, s_inner = call(
        inner_body,
        [(z_split, r_full), fixed(s_split), fixed(split_gain), fixed(split_shift), (mask, r_mask), fixed(inner_kernel)],
        [
            (sds((2, count, half), BF16), pair_half), (sds((count, half)), r_half), (sds((2, count, half), BF16), pair_half),
            (sds((count, half)), r_half), (sds((8, half)), sums_half),
        ],
    )
    s_inner = group(s_inner)
    inner2, z_spread, s_spread = call(
        functools.partial(spread_body, side),
        [(z_inner, r_half), fixed(s_split), fixed(s_inner), fixed(inner_gain), fixed(inner_shift), (mask, r_mask), (edges, r_mask), fixed(spread_weight)],
        [(sds((2, count, half), BF16), pair_half), (sds((count, half)), r_half), (sds((8, half)), sums_half)],
        [pltpu.VMEM((pitch + 2 * GUARD, half), F32), pltpu.VMEM((2, pitch, half), BF16)],
    )
    s_spread = group(s_spread)
    joined2, z_trans, s_trans = call(
        transition_body,
        [(z_spread, r_half), fixed(s_split), fixed(s_spread), fixed(spread_gain), fixed(spread_shift), (mask, r_mask), (main, r_half), fixed(transition_kernel)],
        [(sds((2, count, half), BF16), pair_half), (sds((count, half)), r_half), (sds((8, half)), sums_half)],
    )
    s_trans = group(s_trans)
    trans2, z_out, s_out = call(
        output_body,
        [(z_trans, r_half), fixed(s_split), fixed(s_trans), fixed(transition_gain), fixed(transition_shift), (mask, r_mask), (part2, pair_half), fixed(output_kernel)],
        [(sds((2, count, half), BF16), pair_half), (sds((count, full)), r_full), (sds((8, full)), sums_full)],
    )
    s_out = group(s_out)
    result, dy_out, q_out = call(
        result_body,
        [(z_out, r_full), fixed(s_split), fixed(s_out), fixed(output_gain), fixed(output_shift), (mask, r_mask), (cotangent, image(cotangent.shape))],
        [(sds(cotangent.shape), image(cotangent.shape)), (sds((count, full)), r_full), (sds((8, full)), sums_full)],
        [pltpu.VMEM((pitch, full), F32)],
    )
    own_out = q_out
    q_out = group(q_out)
    dz_out, dy_trans, dy_part, q_mid = call(
        output_back_body,
        [
            (dy_out, r_full), (z_out, r_full), fixed(s_out), fixed(output_gain), fixed(q_out), fixed(s_split), (mask, r_mask), fixed(output_kernel),
            (z_trans, r_half), fixed(s_trans), fixed(transition_gain), fixed(transition_shift), (z_split, rows(pitch, half, 0)), fixed(split_gain), fixed(split_shift),
        ],
        [(sds((2, count, full), BF16), pair_full), (sds((count, half)), r_half), (sds((count, half)), r_half), (sds((8, full)), sums_full)],
        [pltpu.VMEM((pitch, full), F32)],
    )
    own_mid = q_mid
    q_mid = group(q_mid)
    grad_output = jnp.concatenate([weight_grad(trans2, dz_out), weight_grad(part2, dz_out)], axis=0)
    dz_trans, dz_part, grad_joined, dy_spread, q_spread = call(
        transition_back_body,
        [
            (dy_trans, r_half), (dy_part, r_half), (z_trans, r_half), fixed(s_trans), fixed(transition_gain), fixed(q_mid), fixed(s_split), (mask, r_mask), fixed(transition_kernel),
            (z_split, rows(pitch, half, 0)), fixed(split_gain), (z_spread, r_half), fixed(s_spread), fixed(spread_gain), fixed(spread_shift),
        ],
        [
            (sds((2, count, half), BF16), pair_half), (sds((2, count, half), BF16), pair_half), (sds((count, half)), r_half),
            (sds((count, half)), r_half), (sds((8, half)), sums_half),
        ],
    )
    own_spread = q_spread
    q_spread = group(q_spread)
    grad_transition = weight_grad(joined2, dz_trans)
    grad_part = weight_grad(x0[None], dz_part)
    tap_spec = pl.BlockSpec((1, half, half), lambda i: (i, 0, 0))
    grad_spread, dy_inner, q_inner = call(
        functools.partial(spread_back_body, side),
        [
            fixed(dy_spread), fixed(z_spread), fixed(s_spread), fixed(spread_gain), fixed(q_spread), fixed(s_split), fixed(mask), fixed(edges), (spread_weight, tap_spec),
            fixed(inner2), fixed(z_inner), fixed(s_inner), fixed(inner_gain), fixed(inner_shift),
        ],
        [(sds((9, half, half)), tap_spec), (sds((count, half)), out_whole((count, half))), (sds((8, half)), sums_half)],
        [pltpu.VMEM((count + 2 * GUARD, half), F32), pltpu.VMEM((2, count, half), BF16), pltpu.VMEM((2 * half, count), BF16), pltpu.VMEM((count, half), F32)],
        (9,),
    )
    own_inner = q_inner
    q_inner = group(q_inner)
    dz_inner, dy_main, q_main = call(
        inner_back_body,
        [
            (dy_inner, r_half), (z_inner, r_half), fixed(s_inner), fixed(inner_gain), fixed(q_inner), fixed(s_split), (mask, r_mask), fixed(inner_kernel),
            (grad_joined, r_half), (z_split, rows(pitch, half, 1)), fixed(split_gain), fixed(split_shift),
        ],
        [(sds((2, count, half), BF16), pair_half), (sds((count, half)), r_half), (sds((8, half)), sums_half)],
        [pltpu.VMEM((pitch, half), F32)],
    )
    own_main = q_main
    q_main = group(q_main)
    grad_inner = weight_grad(main2, dz_inner)
    dz_main, grad_features = call(
        split_back_body,
        [(dy_main, r_half), (z_split, rows(pitch, half, 1)), fixed(q_main), fixed(s_split), fixed(split_gain), (mask, r_mask), (dz_part, pair_half), fixed(split_kernel)],
        [(sds((2, count, half), BF16), pair_half), (sds(cotangent.shape), image(cotangent.shape))],
        [pltpu.VMEM((pitch, full), F32)],
    )
    grad_main = weight_grad(x0[None], dz_main)
    grad_split = jnp.concatenate([grad_part, grad_main], axis=1)
    small = jnp.concatenate([own_mid[0:2, half:], own_main[0:2], own_inner[0:2], own_spread[0:2], own_mid[0:2, :half], own_out[0:2]], axis=1)
    grad_split, grad_inner, grad_spread, grad_transition, grad_output, small = lax.psum(
        (grad_split, grad_inner, grad_spread, grad_transition, grad_output, small), ("dp", "bn")
    )
    cuts = [0, full, full + half, full + 2 * half, full + 3 * half, 2 * full + 3 * half]
    shifts = [small[0, a:b] for a, b in zip(cuts[:-1], cuts[1:])]
    gains = [small[1, a:b] for a, b in zip(cuts[:-1], cuts[1:])]
    return (
        result, grad_features,
        grad_split, gains[0], shifts[0], grad_inner, gains[1], shifts[1],
        grad_spread.reshape(3, 3, half, half), gains[2], shifts[2], grad_transition, gains[3], shifts[3], grad_output, gains[4], shifts[4],
    )


def solution(mesh):
    shard, copy = P(("dp", "bn")), P()
    return jax.shard_map(
        local,
        mesh=mesh,
        in_specs=(shard, shard, shard) + (copy,) * 15 + (shard,),
        out_specs=(shard, shard) + (copy,) * 15,
        check_vma=False,
    )
```

time: 998 us -> 789 us (0.79)
  matrix products: 369 us -> 0 us
  Pallas kernels: 0 us -> 288 us
  other arithmetic: 122 us -> 5.99 us
  local copies, waits for them, and re-layouts: 131 us -> 56.4 us
  blocking collectives: 107 us -> 159 us
    pallas_call x0 -> x17, Pallas kernels: none -> 288 us  [the longest x11 242 us: call(): pl.pallas_call(body, grid=steps, in_specs=[spec for _, spec in ins], out_...]
    conv_general_dilated x3 -> x0, matrix products: 186 us -> none  [convolve(): lax.conv_general_dilated(inputs, kernel, (1, 1), ((1, 1), (1, 1)), dimens...]
    dot_general x12 -> x0, matrix products: 182 us -> none  [the longest x8 95.4 us: pointwise(): jnp.einsum('nhwc,cd->nhwd', inputs, kernel, precision=lax.Precision.HIGHEST)]
    reduce_sum x6 -> x0, other arithmetic: 52.3 us -> none  [the longest x4 48 us: norm_backward(): local_shift = jnp.sum(grad_before, axis=(0, 1, 2))]
    psum x11, blocking collectives: 107 us -> 159 us  [the longest x10 116 us: group(): return lax.psum(sums, 'bn')]
    mul x8 -> x0, other arithmetic: 47.2 us -> none  [the longest x4 21 us: finish(): return (mish(before) * mask, (scaled, inverse_std, before))]
    mul x8 -> x0, local copies, waits for them, and re-layouts: 37.7 us -> none  [the longest x2 11.9 us: finish(): scaled = (z - mean) * inverse_std]
    conv_general_dilated x6 -> x0, local copies, waits for them, and re-layouts: 27.2 us -> none  [convolve(): lax.conv_general_dilated(inputs, kernel, (1, 1), ((1, 1), (1, 1)), dimens...]
where the time goes in v1:
time: 789 us; the launch traced here: 779 us
  Pallas kernels  288 us (37%)
  waiting for transfers between devices  255 us (32%)
  blocking collectives  159 us (20%)
  local copies, waits for them, and re-layouts  56.4 us (7%)
  between operations  15 us (2%)
    psum x1, waiting for transfers between devices, local(): lax.psum((grad_split, grad_inner, grad_spread, grad_transition, grad_outp...  255 us
    pallas_call x11, Pallas kernels, call(): pl.pallas_call(body, grid=steps, in_specs=[spec for _, spec in ins], out_...  242 us
    psum x10, blocking collectives, group(): return lax.psum(sums, 'bn')  116 us
    unnamed x30, local copies, waits for them, and re-layouts  52.4 us
    pallas_call x6, Pallas kernels, weight_grad(): pl.pallas_call(weight_body, grid=(width // block,), in_specs=[pl.BlockSpe...  46.1 us
    psum x1, blocking collectives, local(): lax.psum((grad_split, grad_inner, grad_spread, grad_transition, grad_outp...  42.3 us
  transfers between devices with their start and end apart: 1, of which 1 were waited for; matrix products, arithmetic and copies ran while one was open for 3% of the time, Pallas kernels for 0%

profile of v1, /device:TPU:0, one launch (start us, length us, event | category | flops | bytes accessed | tf_op | source)
XLA Modules:
  0.0 779.1 jit_solution(13098132990951760707)
XLA Ops:
  14.6 13.1 %shard_map.314 = (bf16[1536,1024]{1,0:T(8,128)(2,1)}, f32[1536,1024]{1,0:T(8,128)}, f32[8,1024]{1,0:T(8,128)}) custom-call(bf16[4,19,19,1024]{3,2,1,0:T(8,128)(2,1)} %copy.36.features_ref, f32[1536,128]{1,0:T(8,128)} %broadcast_in_dim.61.mask_ref, bf16[1024,1024]{1,0:T(8,128)(2,1)} %w_ref.15), custom_call_target="tpu_custom_call" | custom-call | tf_op jit(solution)/shard_map/pallas_call | solution.py:499
  27.7 14.1 %psum.112.stats_ref.total_ref = f32[8,1024]{1,0:T(8,128)} all-reduce(f32[8,1024]{1,0:T(8,128)} %get-tuple-element.55), channel_id=1, replica_groups=mesh['dp'=8,'bn'=4] {'bn'}, use_global_device_ids=true, to_apply=%region_0.1 | all-reduce | flops 8192 | bytes 65536 | tf_op jit(solution)/shard_map/psum | solution.py:492
  51.1 14.7 %shard_map.315 = (bf16[2,1536,512]{2,1,0:T(8,128)(2,1)}, f32[1536,512]{1,0:T(8,128)}, bf16[2,1536,512]{2,1,0:T(8,128)(2,1)}, f32[1536,512]{1,0:T(8,128)}, f32[8,512]{1,0:T(8,128)}) custom-call(f32[1536,1024]{1,0:T(8,128)} %get-tuple-element.54.z_ref.zp_ref.zm_ref, f32[8,1024]{1,0:T(8,128)} %psum.112.stats_ref.total_ref, f32[1,1024]{1,0:T(1,128)} %bitcast.33, ...), custom_call_target="tpu_custom_call" | custom-call | tf_op jit(solution)/shard_map/pallas_call | solution.py:499
  65.7 11.3 %psum.113.stats_ref.si_ref = f32[8,512]{1,0:T(8,128)} all-reduce(f32[8,512]{1,0:T(8,128)} %get-tuple-element.57), channel_id=1, replica_groups=mesh['dp'=8,'bn'=4] {'bn'}, use_global_device_ids=true, to_apply=%region_1.2 | all-reduce | flops 4096 | bytes 32768 | tf_op jit(solution)/shard_map/psum | solution.py:492
  78.2 27.9 %shard_map.316 = (bf16[2,1536,512]{2,1,0:T(8,128)(2,1)}, f32[1536,512]{1,0:T(8,128)}, f32[8,512]{1,0:T(8,128)}) custom-call(f32[1536,512]{1,0:T(8,128)} %get-tuple-element.56.z_ref.zi_ref, f32[8,1024]{1,0:T(8,128)} %psum.112.stats_ref.total_ref, f32[8,512]{1,0:T(8,128)} %psum.113.stats_ref.si_ref, f32[1,512]{1,0:T(1,128)} %bitcast.44, f32[1,512]{1,0:T(1,128)} %bitcast.54, ...), custom_call_target="tpu_custom_call" | custom-call | tf_op jit(solution)/shard_map/pallas_call | solution.py:499
  106.1 11.3 %psum.114.stats_ref.ss_ref.s_ref = f32[8,512]{1,0:T(8,128)} all-reduce(f32[8,512]{1,0:T(8,128)} %get-tuple-element.59), channel_id=1, replica_groups=mesh['dp'=8,'bn'=4] {'bn'}, use_global_device_ids=true, to_apply=%region_2.3 | all-reduce | flops 4096 | bytes 32768 | tf_op jit(solution)/shard_map/psum | solution.py:492
  117.4 10.4 %shard_map.317 = (bf16[2,1536,512]{2,1,0:T(8,128)(2,1)}, f32[1536,512]{1,0:T(8,128)}, f32[8,512]{1,0:T(8,128)}) custom-call(f32[1536,512]{1,0:T(8,128)} %get-tuple-element.58.z_ref.zs_ref, f32[8,1024]{1,0:T(8,128)} %psum.112.stats_ref.total_ref, f32[8,512]{1,0:T(8,128)} %psum.114.stats_ref.ss_ref.s_ref, f32[1,512]{1,0:T(1,128)} %bitcast.41, ...), custom_call_target="tpu_custom_call" | custom-call | tf_op jit(solution)/shard_map/pallas_call | solution.py:499
  127.8 11.5 %psum.115.stats_ref.st_ref = f32[8,512]{1,0:T(8,128)} all-reduce(f32[8,512]{1,0:T(8,128)} %get-tuple-element.62), channel_id=1, replica_groups=mesh['dp'=8,'bn'=4] {'bn'}, use_global_device_ids=true, to_apply=%region_3.4 | all-reduce | flops 4096 | bytes 32768 | tf_op jit(solution)/shard_map/psum | solution.py:492
  139.3 16.5 %shard_map.318 = (bf16[2,1536,512]{2,1,0:T(8,128)(2,1)}, f32[1536,1024]{1,0:T(8,128)}, f32[8,1024]{1,0:T(8,128)}) custom-call(f32[1536,512]{1,0:T(8,128)} %get-tuple-element.61.z_ref.zt_ref, f32[8,1024]{1,0:T(8,128)} %psum.112.stats_ref.total_ref, f32[8,512]{1,0:T(8,128)} %psum.115.stats_ref.st_ref, f32[1,512]{1,0:T(1,128)} %bitcast.47, f32[1,512]{1,0:T(1,128)} %bitcast.56, ...), custom_call_target="tpu_custom_call" | custom-call | tf_op jit(solution)/shard_map/pallas_call | solution.py:499
  155.8 11.5 %psum.116.stats_ref.so_ref = f32[8,1024]{1,0:T(8,128)} all-reduce(f32[8,1024]{1,0:T(8,128)} %get-tuple-element.65), channel_id=1, replica_groups=mesh['dp'=8,'bn'=4] {'bn'}, use_global_device_ids=true, to_apply=%region_4.5 | all-reduce | flops 8192 | bytes 65536 | tf_op jit(solution)/shard_map/psum | solution.py:492
  167.2 14.5 %shard_map.319 = (f32[4,19,19,1024]{3,2,1,0:T(8,128)}, f32[1536,1024]{1,0:T(8,128)}, f32[8,1024]{1,0:T(8,128)}) custom-call(f32[1536,1024]{1,0:T(8,128)} %get-tuple-element.64.z_ref.zo_ref, f32[8,1024]{1,0:T(8,128)} %psum.112.stats_ref.total_ref, f32[8,1024]{1,0:T(8,128)} %psum.116.stats_ref.so_ref, f32[1,1024]{1,0:T(1,128)} %bitcast.50, ...), custom_call_target="tpu_custom_call" | custom-call | tf_op jit(solution)/shard_map/pallas_call | solution.py:499
  181.8 11.5 %psum.117.qo_ref = f32[8,1024]{1,0:T(8,128)} all-reduce(f32[8,1024]{1,0:T(8,128)} %get-tuple-element.68), channel_id=1, replica_groups=mesh['dp'=8,'bn'=4] {'bn'}, use_global_device_ids=true, to_apply=%region_5.6 | all-reduce | flops 8192 | bytes 65536 | tf_op jit(solution)/shard_map/psum | solution.py:492
  193.2 29.5 %shard_map.320 = (bf16[2,1536,1024]{2,1,0:T(8,128)(2,1)}, f32[1536,512]{1,0:T(8,128)}, f32[1536,512]{1,0:T(8,128)}, f32[8,1024]{1,0:T(8,128)}) custom-call(f32[1536,1024]{1,0:T(8,128)} %get-tuple-element.67.dy_ref, f32[1536,1024]{1,0:T(8,128)} %get-tuple-element.64.z_ref.zo_ref, f32[8,1024]{1,0:T(8,128)} %psum.116.stats_ref.so_ref, f32[1,1024]{1,0:T(1,128)} %bitcast.51, ...), custom_call_target="tpu_custom_call" | custom-call | tf_op jit(solution)/shard_map/pallas_call | solution.py:499
  241.9 10.8 %psum.118.q_ref = f32[8,1024]{1,0:T(8,128)} all-reduce(f32[8,1024]{1,0:T(8,128)S(1)} %copy-done.7), channel_id=1, replica_groups=mesh['dp'=8,'bn'=4] {'bn'}, use_global_device_ids=true, to_apply=%region_6.7 | all-reduce | flops 8192 | bytes 65536 | tf_op jit(solution)/shard_map/psum | solution.py:492
  252.7 19.5 %shard_map.321 = (bf16[2,1536,512]{2,1,0:T(8,128)(2,1)}, bf16[2,1536,512]{2,1,0:T(8,128)(2,1)}, f32[1536,512]{1,0:T(8,128)}, f32[1536,512]{1,0:T(8,128)}, f32[8,512]{1,0:T(8,128)}) custom-call(f32[1536,512]{1,0:T(8,128)} %get-tuple-element.69.dyt_ref, f32[1536,512]{1,0:T(8,128)} %get-tuple-element.70.dyp_ref, f32[1536,512]{1,0:T(8,128)} %get-tuple-element.61.z_ref.zt_ref, ...), custom_call_target="tpu_custom_call" | custom-call | tf_op jit(solution)/shard_map/pallas_call | solution.py:499
  272.2 11.8 %psum.119.q_ref = f32[8,512]{1,0:T(8,128)} all-reduce(f32[8,512]{1,0:T(8,128)} %get-tuple-element.73), channel_id=1, replica_groups=mesh['dp'=8,'bn'=4] {'bn'}, use_global_device_ids=true, to_apply=%region_7.8 | all-reduce | flops 4096 | bytes 32768 | tf_op jit(solution)/shard_map/psum | solution.py:492
  284.0 65.1 %shard_map.322 = (f32[9,512,512]{2,1,0:T(8,128)}, f32[1536,512]{1,0:T(8,128)}, f32[8,512]{1,0:T(8,128)}) custom-call(f32[1536,512]{1,0:T(8,128)} %get-tuple-element.72.dy_ref, f32[1536,512]{1,0:T(8,128)} %get-tuple-element.58.z_ref.zs_ref, f32[8,512]{1,0:T(8,128)} %psum.114.stats_ref.ss_ref.s_ref, f32[1,512]{1,0:T(1,128)} %bitcast.43, ...), custom_call_target="tpu_custom_call" | custom-call | tf_op jit(solution)/shard_map/pallas_call | solution.py:499
  349.1 11.3 %psum.120.q_ref = f32[8,512]{1,0:T(8,128)} all-reduce(f32[8,512]{1,0:T(8,128)} %get-tuple-element.76), channel_id=1, replica_groups=mesh['dp'=8,'bn'=4] {'bn'}, use_global_device_ids=true, to_apply=%region_8.9 | all-reduce | flops 4096 | bytes 32768 | tf_op jit(solution)/shard_map/psum | solution.py:492
  360.3 14.9 %shard_map.323 = (bf16[2,1536,512]{2,1,0:T(8,128)(2,1)}, f32[1536,512]{1,0:T(8,128)}, f32[8,512]{1,0:T(8,128)}) custom-call(f32[1536,512]{1,0:T(8,128)} %get-tuple-element.75.dy_ref, f32[1536,512]{1,0:T(8,128)} %get-tuple-element.56.z_ref.zi_ref, f32[8,512]{1,0:T(8,128)} %psum.113.stats_ref.si_ref, f32[1,512]{1,0:T(1,128)} %bitcast.46, ...), custom_call_target="tpu_custom_call" | custom-call | tf_op jit(solution)/shard_map/pallas_call | solution.py:499
  375.3 11.2 %psum.121.q_ref = f32[8,512]{1,0:T(8,128)} all-reduce(f32[8,512]{1,0:T(8,128)} %get-tuple-element.79), channel_id=1, replica_groups=mesh['dp'=8,'bn'=4] {'bn'}, use_global_device_ids=true, to_apply=%region_9.10 | all-reduce | flops 4096 | bytes 32768 | tf_op jit(solution)/shard_map/psum | solution.py:492
  393.9 16.0 %shard_map.324 = (bf16[2,1536,512]{2,1,0:T(8,128)(2,1)}, f32[4,19,19,1024]{3,2,1,0:T(8,128)}) custom-call(f32[1536,512]{1,0:T(8,128)} %get-tuple-element.78.dy_ref, f32[1536,1024]{1,0:T(8,128)} %get-tuple-element.54.z_ref.zp_ref.zm_ref, f32[8,512]{1,0:T(8,128)} %psum.121.q_ref, f32[8,1024]{1,0:T(8,128)} %psum.112.stats_ref.total_ref, f32[1,1024]{1,0:T(1,128)} %bitcast.37, ...), custom_call_target="tpu_custom_call" | custom-call | tf_op jit(solution)/shard_map/pallas_call | solution.py:499
  444.6 10.1 %copy.39 = f32[4,19,19,1024]{3,0,2,1:T(4,128)} copy(f32[4,19,19,1024]{3,2,1,0:T(8,128)} %get-tuple-element.92) | data formatting | bytes 11829248
  457.7 42.3 %psum.123 = f32[2,3584]{1,0:T(2,128)S(1)} all-reduce(f32[2,3584]{1,0:T(2,128)S(1)} %constant_dynamic-update-slice_fusion), channel_id=1, replica_groups=mesh['dp'=8,'bn'=4] {'dp','bn'}, use_global_device_ids=true, to_apply=%region_11.12 | all-reduce | flops 7168 | bytes 57344 | tf_op jit(solution)/shard_map/psum | solution.py:616
  501.2 254.8 %all-reduce.3.cloned.1.call-done = (f32[1024,1024]{1,0:T(8,128)}, f32[512,512]{1,0:T(8,128)}, f32[3,3,512,512]{3,2,1,0:T(8,128)}, f32[512,512]{1,0:T(8,128)}, f32[1024,1024]{1,0:T(8,128)}) async-done(((f32[1024,1024]{1,0:T(8,128)}, f32[512,512]{1,0:T(8,128)}, f32[3,3,512,512]{3,2,1,0:T(8,128)}, f32[512,512]{1,0:T(8,128)}, f32[1024,1024]{1,0:T(8,128)}), (f32[1024,1024]{1,0:T(8,128)}, f32[512,512]{1,0:T(8,128)}, ...) | async-done | bytes 19922960 | tf_op jit(solution)/shard_map/psum | solution.py:616
  (51 shorter events, 98.5 us)
Async XLA Ops:
  7.2 748.8 %all-reduce.3.cloned.1.call-start = ((), (), s32[]{:S(2)}) async-start(), calls=%async_computation | async-start | bytes 39845888 | tf_op jit(solution)/shard_map/psum | solution.py:616
  232.3 9.6 %copy-start.7 = (f32[8,1024]{1,0:T(8,128)S(1)}, f32[8,1024]{1,0:T(8,128)}, u32[]{:S(2)}) copy-start(f32[8,1024]{1,0:T(8,128)} %get-tuple-element.71) | copy-start | bytes 98308
  409.9 7.5 copy-start.1
  409.9 7.5 copy-start.2
  426.0 6.1 copy-start.3
  426.0 6.1 copy-start.4
  756.0 7.7 copy-start
  763.8 4.8 copy-start.6
  763.8 6.3 copy-start.5
Sparse Core Ops, SparseCore 0:
  434.7 321.2 all-reduce.2

commit v2 on v1

--- a/solution.py
+++ b/solution.py
@@ -8,8 +8,10 @@
 from jax.sharding import PartitionSpec as P
 
 EPS = 1e-05
-GUARD = 24
+GUARD = 80
 CHUNK = 16
+TILES = 4
+MESH = pl.DeviceIdType.MESH
 F32 = jnp.float32
 BF16 = jnp.bfloat16
 
@@ -40,8 +42,8 @@
     return pl.BlockSpec((2, pitch, width), lambda i: (0, i, 0))
 
 
-def image(shape):
-    return pl.BlockSpec((1,) + tuple(shape[1:]), lambda i: (i, 0, 0, 0))
+def pixels(pitch, shape):
+    return pl.BlockSpec((pitch // shape[1],) + tuple(shape[1:]), lambda i: (i, 0, 0))
 
 
 def sds(shape, dtype=F32):
@@ -133,23 +135,22 @@
 
 
 def compact(source_ref, scratch_ref):
-    side = source_ref.shape[1]
-    for y in range(side):
-        scratch_ref[y * side : (y + 1) * side, :] = source_ref[0, y].astype(F32)
-    scratch_ref[side * side :, :] = jnp.zeros((scratch_ref.shape[0] - side * side, scratch_ref.shape[1]), F32)
+    places, slots, _ = source_ref.shape
+    for p in range(places):
+        scratch_ref[p * slots : (p + 1) * slots, :] = source_ref[p].astype(F32)
 
 
 def spread_out(scratch_ref, target_ref):
-    side = target_ref.shape[1]
-    for y in range(side):
-        target_ref[0, y] = scratch_ref[y * side : (y + 1) * side, :]
+    places, slots, _ = target_ref.shape
+    for p in range(places):
+        target_ref[p] = scratch_ref[p * slots : (p + 1) * slots, :]
 
 
 def split_kernel_body(features_ref, mask_ref, w_ref, x_ref, z_ref, sums_ref, scratch_ref):
     compact(features_ref, scratch_ref)
 
     def body(r, _):
-        x_ref[r, :] = (scratch_ref[r, :] * mask_ref[r, 0:1]).astype(BF16)
+        x_ref[r, :] = jnp.where(mask_ref[r, 0:1] > 0.0, scratch_ref[r, :], 0.0).astype(BF16)
 
     over_rows(x_ref.shape[0], body)
     z_ref[...] = dot(x_ref[...], w_ref[...])
@@ -180,40 +181,49 @@
     sum_squares(zi_ref, sums_ref)
 
 
-def taps(side):
-    return [(dy * side + dx, dx) for dy in (-1, 0, 1) for dx in (-1, 0, 1)]
-
-
-def spread_body(side, z_ref, total_ref, stats_ref, gain_ref, shift_ref, mask_ref, edge_ref, w_ref, inner_ref, zs_ref, sums_ref, padded_ref, pair_ref):
-    total = total_ref[2:3, 0:1]
-    pitch = z_ref.shape[0]
-    columns = slice(None)
-    mean, inverse = moments(stats_ref, total, columns)
-    scale, shift = gain_ref[...] * inverse, shift_ref[...]
-    padded_ref[0:GUARD, :] = jnp.zeros((GUARD, padded_ref.shape[1]), F32)
-    padded_ref[GUARD + pitch :, :] = jnp.zeros((GUARD, padded_ref.shape[1]), F32)
-
-    def body(r, _):
-        act = mish((z_ref[r, :] - mean) * scale + shift) * mask_ref[r, 0:1]
-        padded_ref[pl.ds(r.start + GUARD, CHUNK), :] = act
-        split_store(inner_ref, (r,), act)
-
-    over_rows(pitch, body)
-    for tap, (move, dx) in enumerate(taps(side)):
-        if move == 0:
-            part = product2(inner_ref, (), w_ref[tap])
-        else:
-            moved = padded_ref[GUARD + move : GUARD + move + pitch, :]
+def taps(side, slots):
+    return [((dy * side + dx) * slots, dx) for dy in (-1, 0, 1) for dx in (-1, 0, 1)]
+
+
+def move_rows(padded_ref, edge_ref, pair_ref, side, slots, sign):
+    count = pair_ref.shape[1]
+    for index, (move, dx) in enumerate(taps(side, slots)):
+
+        @pl.when(pl.program_id(0) == index)
+        def _(move=sign * move, dx=sign * dx):
+            moved = padded_ref[GUARD + move : GUARD + move + count, :]
             if dx:
                 moved = moved * edge_ref[:, dx + 1 : dx + 2]
             split_store(pair_ref, (slice(None),), moved)
-            part = product2(pair_ref, (), w_ref[tap])
-        if tap == 0:
-            zs_ref[...] = part
-        else:
-            zs_ref[...] += part
-    start_sums(sums_ref)
-    sum_squares(zs_ref, sums_ref, mask_ref)
+
+
+def spread_body(side, slots, z_ref, total_ref, stats_ref, gain_ref, shift_ref, mask_ref, edge_ref, w_ref, inner_ref, zs_ref, sums_ref, padded_ref, pair_ref):
+    total = total_ref[2:3, 0:1]
+    count = z_ref.shape[0]
+    tap = pl.program_id(0)
+
+    @pl.when(tap == 0)
+    def _():
+        mean, inverse = moments(stats_ref, total, slice(None))
+        scale, shift = gain_ref[...] * inverse, shift_ref[...]
+        padded_ref[0:GUARD, :] = jnp.zeros((GUARD, padded_ref.shape[1]), F32)
+        padded_ref[GUARD + count :, :] = jnp.zeros((GUARD, padded_ref.shape[1]), F32)
+
+        def body(r, _):
+            act = mish((z_ref[r, :] - mean) * scale + shift) * mask_ref[r, 0:1]
+            padded_ref[pl.ds(r.start + GUARD, CHUNK), :] = act
+            split_store(inner_ref, (r,), act)
+
+        over_rows(count, body)
+        zs_ref[...] = jnp.zeros_like(zs_ref)
+
+    move_rows(padded_ref, edge_ref, pair_ref, side, slots, 1)
+    zs_ref[...] += product2(pair_ref, (), w_ref[0])
+
+    @pl.when(tap == pl.num_programs(0) - 1)
+    def _():
+        sums_ref[...] = jnp.zeros_like(sums_ref)
+        sum_squares(zs_ref, sums_ref, mask_ref)
 
 
 def transition_body(z_ref, total_ref, stats_ref, gain_ref, shift_ref, mask_ref, main_ref, w_ref, joined_ref, zt_ref, sums_ref):
@@ -265,7 +275,7 @@
             inv = 1.0 / (n + 2.0)
             ratio = n * inv
             slope = ratio + y * (((4.0 * t) * (t + 1.0) * inv) * inv)
-            dy = scratch_ref[r, columns] * mask * slope
+            dy = jnp.where(mask > 0.0, scratch_ref[r, columns], 0.0) * slope
             scratch_ref[r, columns] = y * ratio * mask
             dy_ref[r, columns] = dy
             return (carry[0] + fold(dy), carry[1] + fold(dy * scaled))
@@ -345,7 +355,7 @@
     add_sums(sums_ref, own, over_rows(zt_ref.shape[0], tail, (zero, zero)))
 
 
-def spread_back_body(side, dy_ref, z_ref, s_ref, g_ref, q_ref, total_ref, mask_ref, edge_ref, w_ref, inner_ref, zi_ref, si_ref, gi_ref, bi_ref, dw_ref, dyi_ref, sums_ref, padded_ref, pair_ref, turned_ref, grad_ref):
+def spread_back_body(side, slots, dy_ref, z_ref, s_ref, g_ref, q_ref, total_ref, mask_ref, edge_ref, w_ref, zi_ref, si_ref, gi_ref, bi_ref, moved_ref, dyi_ref, sums_ref, padded_ref, grad_ref):
     total = total_ref[2:3, 0:1]
     count, half = z_ref.shape
     tap = pl.program_id(0)
@@ -363,22 +373,10 @@
             padded_ref[pl.ds(r.start + GUARD, CHUNK), :] = dz
 
         over_rows(count, body)
-        turned_ref[0:half, :] = inner_ref[0].T
-        turned_ref[half:, :] = inner_ref[1].T
         grad_ref[...] = jnp.zeros_like(grad_ref)
 
-    for index, (move, dx) in enumerate(taps(side)):
-
-        @pl.when(tap == index)
-        def _(move=move, dx=dx):
-            moved = padded_ref[GUARD - move : GUARD - move + count, :]
-            if dx:
-                moved = moved * edge_ref[:, 1 - dx : 2 - dx]
-            split_store(pair_ref, (slice(None),), moved)
-
-    both = dot(turned_ref[...], pair_ref[0])
-    dw_ref[0] = both[0:half] + both[half:] + dot(turned_ref[0:half, :], pair_ref[1])
-    grad_ref[...] += product2_t(pair_ref, (), w_ref[0])
+    move_rows(padded_ref, edge_ref, moved_ref.at[0], side, slots, -1)
+    grad_ref[...] += product2_t(moved_ref.at[0], (), w_ref[0])
 
     @pl.when(tap == pl.num_programs(0) - 1)
     def _():
@@ -463,7 +461,263 @@
     )(x, dz)
 
 
+LAG = 8
+KEPT = 6
+
+
+def reduce_body(jobs, left_count, right_count, *refs):
+    lefts, rights = refs[:left_count], refs[left_count : left_count + right_count]
+    refs = refs[left_count + right_count :]
+    outs = refs[:5]
+    (x_ref, z_ref, turned_ref, own_ref, r0_ref, half_ref, r1_ref, quarter_ref, r2_ref, eighth_ref, r3_ref, full_ref, load_sem, store_sem) = refs[5:19]
+    sems = refs[19:]
+    block = own_ref.shape[1]
+    mid = block // 2
+    dp, bn = lax.axis_index("dp"), lax.axis_index("bn")
+    z, x, y, core = dp // 2, dp % 2, bn // 2, bn % 2
+
+    def at(new_z, new_x, new_y, new_core):
+        return {"dp": new_z * 2 + new_x, "bn": new_y * 2 + new_core}
+
+    to_core, to_x, to_y = at(z, x, y, 1 - core), at(z, 1 - x, y, core), at(z, x, 1 - y, core)
+    depth = [(z + k) % 4 for k in (1, 2, 3)]
+    to_z = [at(new_z, x, y, core) for new_z in depth]
+    columns = (pl.ds(0, mid), pl.ds(mid, mid))
+
+    def part(start, size):
+        return pl.ds(pl.multiple_of(start, size), size)
+
+    def far(stage, k, slot, source, target, peer):
+        send, recv = sems[2 * stage], sems[2 * stage + 1]
+        return pltpu.make_async_remote_copy(
+            src_ref=source, dst_ref=target, send_sem=send.at[k, slot], recv_sem=recv.at[k, slot], device_id=peer, device_id_type=MESH
+        )
+
+    first = (x, y)
+    second = (y, x)
+    sides = (to_x, to_y)
+
+    def copies(stage, c):
+        slot, keep = c % 2, c % KEPT
+        base = core * (block // 2)
+        if stage == 0:
+            return [far(0, 0, slot, own_ref.at[slot, part((1 - core) * (block // 2), block // 2)], r0_ref.at[slot], to_core)]
+        if stage == 1:
+            return [
+                far(1, k, slot, half_ref.at[slot, part((1 - first[k]) * (block // 4), block // 4), columns[k]], r1_ref.at[slot, :, columns[k]], sides[k])
+                for k in (0, 1)
+            ]
+        if stage == 2:
+            return [
+                far(2, k, slot, quarter_ref.at[slot, part((1 - second[k]) * (block // 8), block // 8), columns[k]], r2_ref.at[slot, :, columns[k]], sides[1 - k])
+                for k in (0, 1)
+            ]
+        if stage == 3:
+            return [
+                far(3, k, slot, eighth_ref.at[slot, part(depth[k] * (block // 32), block // 32)], r3_ref.at[slot, k], to_z[k]) for k in (0, 1, 2)
+            ]
+        made = []
+        for k in (0, 1):
+            eighth = base + first[k] * (block // 4) + second[k] * (block // 8)
+            if stage == 4:
+                spot = full_ref.at[keep, part(eighth + z * (block // 32), block // 32), columns[k]]
+                made += [far(4, 3 * k + d, slot, spot, spot, to_z[d]) for d in (0, 1, 2)]
+            elif stage == 5:
+                spot = full_ref.at[keep, part(eighth, block // 8), columns[k]]
+                made.append(far(5, k, slot, spot, spot, sides[1 - k]))
+            elif stage == 6:
+                spot = full_ref.at[keep, part(base + first[k] * (block // 4), block // 4), columns[k]]
+                made.append(far(6, k, slot, spot, spot, sides[k]))
+        if stage == 7:
+            spot = full_ref.at[keep, part(base, block // 2)]
+            made.append(far(7, 0, slot, spot, spot, to_core))
+        return made
+
+    def begin(stage, c):
+        for copy in copies(stage, c):
+            copy.start()
+
+    def finish(stage, c):
+        for copy in copies(stage, c):
+            copy.wait()
+
+    def load(j):
+        (left, left_columns, parts), (right, right_columns), _ = jobs[j]
+        slot = j % 2
+        return [
+            pltpu.make_async_copy(lefts[left].at[0:parts, :, left_columns], x_ref.at[slot, 0:parts], load_sem.at[slot, 0]),
+            pltpu.make_async_copy(rights[right].at[(slice(None),) * (len(rights[right].shape) - 2) + (slice(None), right_columns)] if right_columns is not None else rights[right[0]].at[right[1]], z_ref.at[slot], load_sem.at[slot, 1]),
+        ]
+
+    def store(j):
+        out, spot = jobs[j][2]
+        return pltpu.make_async_copy(full_ref.at[j % KEPT], outs[out].at[spot], store_sem.at[j % KEPT])
+
+    for copy in load(0):
+        copy.start()
+    barrier = pltpu.get_barrier_semaphore()
+    peers = [to_core, to_x, to_y] + to_z
+    for peer in peers:
+        pl.semaphore_signal(barrier, inc=1, device_id=peer, device_id_type=MESH)
+    pl.semaphore_wait(barrier, len(peers))
+    total = len(jobs)
+
+    @pl.loop(0, total + LAG + 1)
+    def _(t):
+        for j in range(total):
+
+            @pl.when(t == j + LAG + 1)
+            def _(j=j):
+                store(j).wait()
+
+        def stage(number, lag):
+            def wrap(body):
+                c = t - lag
+                pl.when(jnp.logical_and(c >= 0, c < total))(lambda: body(c))
+
+            return wrap
+
+        @stage(7, 8)
+        def _(c):
+            finish(7, c)
+
+        for j in range(total):
+
+            @pl.when(t == j + LAG)
+            def _(j=j):
+                store(j).start()
+
+        for number in (6, 5, 4):
+
+            @stage(number, number + 1)
+            def _(c, number=number):
+                finish(number, c)
+                begin(number + 1, c)
+
+        @stage(3, 4)
+        def _(c):
+            finish(3, c)
+            slot, keep = c % 2, c % KEPT
+            value = eighth_ref[slot, part(z * (block // 32), block // 32), :]
+            for k in (0, 1, 2):
+                value = value + r3_ref[slot, k]
+            for k in (0, 1):
+                row = core * (block // 2) + first[k] * (block // 4) + second[k] * (block // 8) + z * (block // 32)
+                full_ref[keep, part(row, block // 32), k * mid : (k + 1) * mid] = value[:, k * mid : (k + 1) * mid]
+            begin(4, c)
+
+        @stage(2, 3)
+        def _(c):
+            finish(2, c)
+            slot = c % 2
+            for k in (0, 1):
+                eighth_ref[slot, :, columns[k]] = quarter_ref[slot, part(second[k] * (block // 8), block // 8), columns[k]] + r2_ref[slot, :, columns[k]]
+            begin(3, c)
+
+        @stage(1, 2)
+        def _(c):
+            finish(1, c)
+            slot = c % 2
+            for k in (0, 1):
+                quarter_ref[slot, :, columns[k]] = half_ref[slot, part(first[k] * (block // 4), block // 4), columns[k]] + r1_ref[slot, :, columns[k]]
+            begin(2, c)
+
+        @stage(0, 1)
+        def _(c):
+            finish(0, c)
+            slot = c % 2
+            half_ref[slot] = own_ref[slot, part(core * (block // 2), block // 2), :] + r0_ref[slot]
+            begin(1, c)
+
+        for j in range(total):
+
+            @pl.when(t == j)
+            def _(j=j):
+                for copy in load(j):
+                    copy.wait()
+                if j + 1 < total:
+                    for copy in load(j + 1):
+                        copy.start()
+
+        exact = functools.reduce(jnp.logical_or, [t == j for j in range(total) if jobs[j][0][2] == 1])
+
+        @stage(None, 0)
+        def _(c):
+            slot = c % 2
+            turned_ref[...] = x_ref[slot, 0].T
+            own_ref[slot] = dot(turned_ref[...], z_ref[slot, 0]) + dot(turned_ref[...], z_ref[slot, 1])
+
+            @pl.when(jnp.logical_not(exact))
+            def _():
+                turned_ref[...] = x_ref[slot, 1].T
+                own_ref[slot] += dot(turned_ref[...], z_ref[slot, 0])
+
+            begin(0, c)
+
+
+def reduce_call(jobs, lefts, rights, shapes, count, block):
+    hbm = pl.BlockSpec(memory_space=pl.ANY)
+    vmem = pltpu.VMEM
+    scratch = [
+        vmem((2, 2, count, block), BF16), vmem((2, 2, count, block), BF16), vmem((block, count), BF16),
+        vmem((2, block, block), F32), vmem((2, block // 2, block), F32), vmem((2, block // 2, block), F32),
+        vmem((2, block // 4, block), F32), vmem((2, block // 4, block), F32), vmem((2, block // 8, block), F32), vmem((2, block // 8, block), F32),
+        vmem((2, 3, block // 32, block), F32), vmem((KEPT, block, block), F32),
+        pltpu.SemaphoreType.DMA((2, 2)), pltpu.SemaphoreType.DMA((KEPT,)),
+    ]
+    for width in (1, 2, 2, 3, 6, 2, 2, 1):
+        scratch += [pltpu.SemaphoreType.DMA((width, 2)), pltpu.SemaphoreType.DMA((width, 2))]
+    return pl.pallas_call(
+        functools.partial(reduce_body, jobs, len(lefts), len(rights)),
+        in_specs=[hbm] * (len(lefts) + len(rights)),
+        out_specs=[hbm] * len(shapes),
+        out_shape=[sds(shape) for shape in shapes],
+        scratch_shapes=scratch,
+        compiler_params=pltpu.CompilerParams(collective_id=3, has_side_effects=True, vmem_limit_bytes=56 * 1024 * 1024),
+    )(*lefts, *rights)
+
+
+def gather_sums_body(axis, sums_ref, out_ref, slots_ref, send_sem, recv_sem):
+    members = slots_ref.shape[0]
+    me = lax.axis_index(axis)
+    peers = [lax.rem(me + k, members) for k in range(1, members)]
+    barrier = pltpu.get_barrier_semaphore()
+    for peer in peers:
+        pl.semaphore_signal(barrier, inc=1, device_id={axis: peer}, device_id_type=MESH)
+    pl.semaphore_wait(barrier, members - 1)
+    copies = [
+        pltpu.make_async_remote_copy(
+            src_ref=sums_ref, dst_ref=slots_ref.at[me], send_sem=send_sem.at[k], recv_sem=recv_sem.at[k], device_id={axis: peer}, device_id_type=MESH
+        )
+        for k, peer in enumerate(peers)
+    ]
+    for copy in copies:
+        copy.start()
+    slots_ref[me] = sums_ref[...]
+    for copy in copies:
+        copy.wait()
+    value = slots_ref[0]
+    for k in range(1, members):
+        value = value + slots_ref[k]
+    out_ref[...] = value
+
+
+def gather_sums(sums, members, collective, axis="bn"):
+    if members == 1:
+        return sums
+    spec = pl.BlockSpec(memory_space=pltpu.VMEM)
+    return pl.pallas_call(
+        functools.partial(gather_sums_body, axis),
+        in_specs=[spec],
+        out_specs=spec,
+        out_shape=sds(sums.shape),
+        scratch_shapes=[pltpu.VMEM((members,) + sums.shape, F32), pltpu.SemaphoreType.DMA((members - 1,)), pltpu.SemaphoreType.DMA((members - 1,))],
+        compiler_params=pltpu.CompilerParams(collective_id=collective, has_side_effects=True),
+    )(sums)
+
+
 def local(
+    shape,
     features, image_counts, map_sides,
     split_kernel, split_gain, split_shift, inner_kernel, inner_gain, inner_shift,
     spread_kernel, spread_gain, spread_shift, transition_kernel, transition_gain, transition_shift,
@@ -471,17 +725,19 @@
 ):
     slots, side, _, full = features.shape
     half = inner_kernel.shape[0]
-    pitch = round_up(side * side, 128)
-    count = slots * pitch
-    grid = (slots,)
-    row = jnp.arange(pitch)
-    y, x = row // side, row % side
-    live = jnp.arange(slots) < image_counts[0]
-    keep = live[:, None] & (y[None, :] < map_sides[:, None]) & (x[None, :] < map_sides[:, None])
-    mask = jnp.broadcast_to(keep.astype(F32).reshape(count, 1), (count, 128))
+    pitch = round_up(-(-slots * side * side // TILES), 16)
+    count = TILES * pitch
+    grid = (TILES,)
+    row = jnp.arange(count)
+    slot, place = row % slots, row // slots
+    y, x = place // side, place % side
+    sides = map_sides[slot]
+    keep = (slot < image_counts[0]) & (y < sides) & (x < sides) & (place < side * side)
+    mask = jnp.broadcast_to(keep.astype(F32)[:, None], (count, 128))
     lane = jnp.arange(128)[None, :]
     edges = jnp.where(lane == 0, (x > 0)[:, None], jnp.where(lane == 2, (x < side - 1)[:, None], True)).astype(F32)
-    edges = jnp.tile(edges, (slots, 1))
+    features = features.transpose(1, 2, 0, 3).reshape(side * side, slots, full)
+    cotangent = cotangent.transpose(1, 2, 0, 3).reshape(side * side, slots, full)
     (split_gain, split_shift, inner_gain, inner_shift, spread_gain, spread_shift, transition_gain, transition_shift, output_gain, output_shift) = (
         item.reshape(1, -1)
         for item in (split_gain, split_shift, inner_gain, inner_shift, spread_gain, spread_shift, transition_gain, transition_shift, output_gain, output_shift)
@@ -489,7 +745,7 @@
     spread_weight = spread_kernel.reshape(9, half, half)
 
     def group(sums):
-        return lax.psum(sums, "bn")
+        return gather_sums(sums, shape[1], 1 if sums.shape[1] == full else 2)
 
     sums_full, sums_half = out_whole((8, full)), out_whole((8, half))
     r_half, r_full, r_mask = rows(pitch, half), rows(pitch, full), rows(pitch, 128)
@@ -511,7 +767,7 @@
 
     x0, z_split, s_split = call(
         split_kernel_body,
-        [(features, image(features.shape)), (mask, r_mask), fixed(split_kernel)],
+        [(features, pixels(pitch, features.shape)), (mask, r_mask), fixed(split_kernel)],
         [(sds((count, full), BF16), r_full), (sds((count, full)), r_full), (sds((8, full)), sums_full)],
         [pltpu.VMEM((pitch, full), F32)],
     )
@@ -525,11 +781,13 @@
         ],
     )
     s_inner = group(s_inner)
+    tap_spec = pl.BlockSpec((1, half, half), lambda i: (i, 0, 0))
     inner2, z_spread, s_spread = call(
-        functools.partial(spread_body, side),
-        [(z_inner, r_half), fixed(s_split), fixed(s_inner), fixed(inner_gain), fixed(inner_shift), (mask, r_mask), (edges, r_mask), fixed(spread_weight)],
-        [(sds((2, count, half), BF16), pair_half), (sds((count, half)), r_half), (sds((8, half)), sums_half)],
-        [pltpu.VMEM((pitch + 2 * GUARD, half), F32), pltpu.VMEM((2, pitch, half), BF16)],
+        functools.partial(spread_body, side, slots),
+        [fixed(z_inner), fixed(s_split), fixed(s_inner), fixed(inner_gain), fixed(inner_shift), fixed(mask), fixed(edges), (spread_weight, tap_spec)],
+        [(sds((2, count, half), BF16), out_whole((2, count, half))), (sds((count, half)), out_whole((count, half))), (sds((8, half)), sums_half)],
+        [pltpu.VMEM((count + 2 * GUARD, half), F32), pltpu.VMEM((2, count, half), BF16)],
+        (9,),
     )
     s_spread = group(s_spread)
     joined2, z_trans, s_trans = call(
@@ -546,11 +804,10 @@
     s_out = group(s_out)
     result, dy_out, q_out = call(
         result_body,
-        [(z_out, r_full), fixed(s_split), fixed(s_out), fixed(output_gain), fixed(output_shift), (mask, r_mask), (cotangent, image(cotangent.shape))],
-        [(sds(cotangent.shape), image(cotangent.shape)), (sds((count, full)), r_full), (sds((8, full)), sums_full)],
+        [(z_out, r_full), fixed(s_split), fixed(s_out), fixed(output_gain), fixed(output_shift), (mask, r_mask), (cotangent, pixels(pitch, cotangent.shape))],
+        [(sds(cotangent.shape), pixels(pitch, cotangent.shape)), (sds((count, full)), r_full), (sds((8, full)), sums_full)],
         [pltpu.VMEM((pitch, full), F32)],
     )
-    own_out = q_out
     q_out = group(q_out)
     dz_out, dy_trans, dy_part, q_mid = call(
         output_back_body,
@@ -561,9 +818,7 @@
         [(sds((2, count, full), BF16), pair_full), (sds((count, half)), r_half), (sds((count, half)), r_half), (sds((8, full)), sums_full)],
         [pltpu.VMEM((pitch, full), F32)],
     )
-    own_mid = q_mid
     q_mid = group(q_mid)
-    grad_output = jnp.concatenate([weight_grad(trans2, dz_out), weight_grad(part2, dz_out)], axis=0)
     dz_trans, dz_part, grad_joined, dy_spread, q_spread = call(
         transition_back_body,
         [
@@ -575,22 +830,18 @@
             (sds((count, half)), r_half), (sds((8, half)), sums_half),
         ],
     )
-    own_spread = q_spread
     q_spread = group(q_spread)
-    grad_transition = weight_grad(joined2, dz_trans)
-    grad_part = weight_grad(x0[None], dz_part)
-    tap_spec = pl.BlockSpec((1, half, half), lambda i: (i, 0, 0))
-    grad_spread, dy_inner, q_inner = call(
-        functools.partial(spread_back_body, side),
+    moved_spec = pl.BlockSpec((1, 2, count, half), lambda i: (i, 0, 0, 0))
+    moved, dy_inner, q_inner = call(
+        functools.partial(spread_back_body, side, slots),
         [
             fixed(dy_spread), fixed(z_spread), fixed(s_spread), fixed(spread_gain), fixed(q_spread), fixed(s_split), fixed(mask), fixed(edges), (spread_weight, tap_spec),
-            fixed(inner2), fixed(z_inner), fixed(s_inner), fixed(inner_gain), fixed(inner_shift),
+            fixed(z_inner), fixed(s_inner), fixed(inner_gain), fixed(inner_shift),
         ],
-        [(sds((9, half, half)), tap_spec), (sds((count, half)), out_whole((count, half))), (sds((8, half)), sums_half)],
-        [pltpu.VMEM((count + 2 * GUARD, half), F32), pltpu.VMEM((2, count, half), BF16), pltpu.VMEM((2 * half, count), BF16), pltpu.VMEM((count, half), F32)],
+        [(sds((9, 2, count, half), BF16), moved_spec), (sds((count, half)), out_whole((count, half))), (sds((8, half)), sums_half)],
+        [pltpu.VMEM((count + 2 * GUARD, half), F32), pltpu.VMEM((count, half), F32)],
         (9,),
     )
-    own_inner = q_inner
     q_inner = group(q_inner)
     dz_inner, dy_main, q_main = call(
         inner_back_body,
@@ -601,24 +852,42 @@
         [(sds((2, count, half), BF16), pair_half), (sds((count, half)), r_half), (sds((8, half)), sums_half)],
         [pltpu.VMEM((pitch, half), F32)],
     )
-    own_main = q_main
     q_main = group(q_main)
-    grad_inner = weight_grad(main2, dz_inner)
     dz_main, grad_features = call(
         split_back_body,
         [(dy_main, r_half), (z_split, rows(pitch, half, 1)), fixed(q_main), fixed(s_split), fixed(split_gain), (mask, r_mask), (dz_part, pair_half), fixed(split_kernel)],
-        [(sds((2, count, half), BF16), pair_half), (sds(cotangent.shape), image(cotangent.shape))],
+        [(sds((2, count, half), BF16), pair_half), (sds(cotangent.shape), pixels(pitch, cotangent.shape))],
         [pltpu.VMEM((pitch, full), F32)],
     )
-    grad_main = weight_grad(x0[None], dz_main)
-    grad_split = jnp.concatenate([grad_part, grad_main], axis=1)
-    small = jnp.concatenate([own_mid[0:2, half:], own_main[0:2], own_inner[0:2], own_spread[0:2], own_mid[0:2, :half], own_out[0:2]], axis=1)
-    grad_split, grad_inner, grad_spread, grad_transition, grad_output, small = lax.psum(
-        (grad_split, grad_inner, grad_spread, grad_transition, grad_output, small), ("dp", "bn")
-    )
+    small = jnp.concatenate([q_mid[0:2, half:], q_main[0:2], q_inner[0:2], q_spread[0:2], q_mid[0:2, :half], q_out[0:2]], axis=1)
+    if shape == (8, 4):
+        low, high = slice(0, half), slice(half, full)
+        every = slice(None)
+        lefts = [trans2, part2, joined2, x0[None], inner2, main2]
+        rights = [dz_out, dz_trans, dz_part, moved, dz_inner, dz_main]
+        jobs = [((0, every, 2), (0, low), (4, (low, low))), ((0, every, 2), (0, high), (4, (low, high)))]
+        jobs += [((1, every, 2), (0, low), (4, (high, low))), ((1, every, 2), (0, high), (4, (high, high)))]
+        jobs += [((2, every, 2), (1, every), (3, (every, every)))]
+        jobs += [((3, low, 1), (2, every), (0, (low, low))), ((3, high, 1), (2, every), (0, (high, low)))]
+        jobs += [((4, every, 2), ((3, tap), None), (2, (tap,))) for tap in range(9)]
+        jobs += [((5, every, 2), (4, every), (1, (every, every)))]
+        jobs += [((3, low, 1), (5, every), (0, (low, high))), ((3, high, 1), (5, every), (0, (high, high)))]
+        shapes = [(full, full), (half, half), (9, half, half), (half, half), (full, full)]
+        grad_split, grad_inner, grad_spread, grad_transition, grad_output = reduce_call(jobs, lefts, rights, shapes, count, half)
+        small = gather_sums(jnp.pad(small, ((0, 6), (0, 0))), shape[0], 4, "dp")
+    else:
+        grad_output = jnp.concatenate([weight_grad(trans2, dz_out), weight_grad(part2, dz_out)], axis=0)
+        grad_transition, grad_inner = weight_grad(joined2, dz_trans), weight_grad(main2, dz_inner)
+        grad_split = jnp.concatenate([weight_grad(x0[None], dz_part), weight_grad(x0[None], dz_main)], axis=1)
+        grad_spread = jnp.stack([weight_grad(inner2, moved[tap]) for tap in range(9)])
+        grad_split, grad_inner, grad_spread, grad_transition, grad_output = lax.psum(
+            (grad_split, grad_inner, grad_spread, grad_transition, grad_output), ("dp", "bn")
+        )
+        small = lax.psum(small, "dp")
     cuts = [0, full, full + half, full + 2 * half, full + 3 * half, 2 * full + 3 * half]
     shifts = [small[0, a:b] for a, b in zip(cuts[:-1], cuts[1:])]
     gains = [small[1, a:b] for a, b in zip(cuts[:-1], cuts[1:])]
+    result, grad_features = (item.reshape(side, side, slots, full).transpose(2, 0, 1, 3) for item in (result, grad_features))
     return (
         result, grad_features,
         grad_split, gains[0], shifts[0], grad_inner, gains[1], shifts[1],
@@ -629,7 +898,7 @@
 def solution(mesh):
     shard, copy = P(("dp", "bn")), P()
     return jax.shard_map(
-        local,
+        functools.partial(local, (mesh.shape["dp"], mesh.shape["bn"])),
         mesh=mesh,
         in_specs=(shard, shard, shard) + (copy,) * 15 + (shard,),
         out_specs=(shard, shard) + (copy,) * 15,

time: 789 us -> 510 us (0.65)
  waiting for transfers between devices: 255 us -> 0 us
  Pallas kernels: 288 us -> 474 us
  blocking collectives: 159 us -> 0 us
  local copies, waits for them, and re-layouts: 56.4 us -> 25.6 us
  between operations: 15 us -> 1.46 us
    psum x1 -> x0, waiting for transfers between devices: 255 us -> none  [local(): lax.psum((grad_split, grad_inner, grad_spread, grad_transition, grad_outp...]
    pallas_call x6 -> x12, Pallas kernels: 46.1 us -> 257 us  [the longest x1 183 us: reduce_call(): pl.pallas_call(functools.partial(reduce_body, jobs, len(lefts), len(right...]
    psum x11 -> x0, blocking collectives: 159 us -> none  [the longest x10 116 us: group(): return lax.psum(sums, 'bn')]
    unnamed x30 -> x18, local copies, waits for them, and re-layouts: 52.4 us -> 18.8 us
    pallas_call x11, Pallas kernels: 242 us -> 217 us  [call(): pl.pallas_call(body, grid=steps, in_specs=[spec for _, spec in ins], out_...]
  transfers between devices with their start and end apart: 1 -> 0, of which waited for: 1 -> 0; matrix products, arithmetic and copies ran while one was open for 3% -> 0% of each run, Pallas kernels for 0% -> 0%
where the time goes in v2:
time: 510 us; the launch traced here: 506 us
  Pallas kernels  474 us (93%)
  local copies, waits for them, and re-layouts  25.6 us (5%)
    pallas_call x11, Pallas kernels, call(): pl.pallas_call(body, grid=steps, in_specs=[spec for _, spec in ins], out_...  217 us
    pallas_call x1, Pallas kernels, reduce_call(): pl.pallas_call(functools.partial(reduce_body, jobs, len(lefts), len(right...  183 us
    pallas_call x11, Pallas kernels, gather_sums(): pl.pallas_call(functools.partial(gather_sums_body, axis), in_specs=[spec]...  74.6 us
    unnamed x18, local copies, waits for them, and re-layouts  18.8 us

profile of v2, /device:TPU:0, one launch (start us, length us, event | category | flops | bytes accessed | tf_op | source)
XLA Modules:
  0.0 505.6 jit_solution(431373777076110870)
XLA Ops:
  8.2 12.7 %shard_map.314 = (bf16[1472,1024]{1,0:T(8,128)(2,1)}, f32[1472,1024]{1,0:T(8,128)}, f32[8,1024]{1,0:T(8,128)}) custom-call(bf16[361,4,1024]{2,1,0:T(4,128)(2,1)} %bitcast.46, f32[1472,128]{1,0:T(8,128)} %broadcast_in_dim.57.mask_ref, bf16[1024,1024]{1,0:T(8,128)(2,1)} %w_ref.15), custom_call_target="tpu_custom_call" | custom-call | tf_op jit(solution)/shard_map/pallas_call | solution.py:755
  21.0 6.7 %shard_map.315.stats_ref.total_ref = f32[8,1024]{1,0:T(8,128)} custom-call(f32[8,1024]{1,0:T(8,128)} %get-tuple-element.60.sums_ref), custom_call_target="tpu_custom_call" | custom-call | tf_op jit(solution)/shard_map/pallas_call | solution.py:709
  27.6 14.1 %shard_map.316 = (bf16[2,1472,512]{2,1,0:T(8,128)(2,1)}, f32[1472,512]{1,0:T(8,128)}, bf16[2,1472,512]{2,1,0:T(8,128)(2,1)}, f32[1472,512]{1,0:T(8,128)}, f32[8,512]{1,0:T(8,128)}) custom-call(f32[1472,1024]{1,0:T(8,128)} %get-tuple-element.59.z_ref.zp_ref.zm_ref, f32[8,1024]{1,0:T(8,128)} %shard_map.315.stats_ref.total_ref, f32[1,1024]{1,0:T(1,128)} %bitcast.47, ...), custom_call_target="tpu_custom_call" | custom-call | tf_op jit(solution)/shard_map/pallas_call | solution.py:755
  41.8 5.1 %shard_map.317.stats_ref.si_ref = f32[8,512]{1,0:T(8,128)} custom-call(f32[8,512]{1,0:T(8,128)} %get-tuple-element.62.sums_ref), custom_call_target="tpu_custom_call" | custom-call | tf_op jit(solution)/shard_map/pallas_call | solution.py:709
  46.9 34.9 %shard_map.318 = (bf16[2,1472,512]{2,1,0:T(8,128)(2,1)}, f32[1472,512]{1,0:T(8,128)}, f32[8,512]{1,0:T(8,128)}) custom-call(f32[1472,512]{1,0:T(8,128)} %get-tuple-element.61.z_ref.zi_ref, f32[8,1024]{1,0:T(8,128)} %shard_map.315.stats_ref.total_ref, f32[8,512]{1,0:T(8,128)} %shard_map.317.stats_ref.si_ref, f32[1,512]{1,0:T(1,128)} %bitcast.61, ...), custom_call_target="tpu_custom_call" | custom-call | tf_op jit(solution)/shard_map/pallas_call | solution.py:755
  81.8 5.1 %shard_map.319.stats_ref.ss_ref.s_ref = f32[8,512]{1,0:T(8,128)} custom-call(f32[8,512]{1,0:T(8,128)} %get-tuple-element.64.sums_ref), custom_call_target="tpu_custom_call" | custom-call | tf_op jit(solution)/shard_map/pallas_call | solution.py:709
  86.9 10.1 %shard_map.320 = (bf16[2,1472,512]{2,1,0:T(8,128)(2,1)}, f32[1472,512]{1,0:T(8,128)}, f32[8,512]{1,0:T(8,128)}) custom-call(f32[1472,512]{1,0:T(8,128)} %get-tuple-element.63.z_ref.zs_ref, f32[8,1024]{1,0:T(8,128)} %shard_map.315.stats_ref.total_ref, f32[8,512]{1,0:T(8,128)} %shard_map.319.stats_ref.ss_ref.s_ref, f32[1,512]{1,0:T(1,128)} %bitcast.58, ...), custom_call_target="tpu_custom_call" | custom-call | tf_op jit(solution)/shard_map/pallas_call | solution.py:755
  97.0 5.1 %shard_map.321.stats_ref.st_ref = f32[8,512]{1,0:T(8,128)} custom-call(f32[8,512]{1,0:T(8,128)} %get-tuple-element.67.sums_ref), custom_call_target="tpu_custom_call" | custom-call | tf_op jit(solution)/shard_map/pallas_call | solution.py:709
  102.1 15.8 %shard_map.322 = (bf16[2,1472,512]{2,1,0:T(8,128)(2,1)}, f32[1472,1024]{1,0:T(8,128)}, f32[8,1024]{1,0:T(8,128)}) custom-call(f32[1472,512]{1,0:T(8,128)} %get-tuple-element.66.z_ref.zt_ref, f32[8,1024]{1,0:T(8,128)} %shard_map.315.stats_ref.total_ref, f32[8,512]{1,0:T(8,128)} %shard_map.321.stats_ref.st_ref, f32[1,512]{1,0:T(1,128)} %bitcast.55, ...), custom_call_target="tpu_custom_call" | custom-call | tf_op jit(solution)/shard_map/pallas_call | solution.py:755
  117.9 5.6 %shard_map.323.stats_ref.so_ref = f32[8,1024]{1,0:T(8,128)} custom-call(f32[8,1024]{1,0:T(8,128)} %get-tuple-element.70.sums_ref), custom_call_target="tpu_custom_call" | custom-call | tf_op jit(solution)/shard_map/pallas_call | solution.py:709
  123.5 14.1 %shard_map.324 = (f32[361,4,1024]{2,1,0:T(4,128)}, f32[1472,1024]{1,0:T(8,128)}, f32[8,1024]{1,0:T(8,128)}) custom-call(f32[1472,1024]{1,0:T(8,128)} %get-tuple-element.69.z_ref.zo_ref, f32[8,1024]{1,0:T(8,128)} %shard_map.315.stats_ref.total_ref, f32[8,1024]{1,0:T(8,128)} %shard_map.323.stats_ref.so_ref, f32[1,1024]{1,0:T(1,128)} %bitcast.64, ...), custom_call_target="tpu_custom_call" | custom-call | tf_op jit(solution)/shard_map/pallas_call | solution.py:755
  137.6 5.6 %shard_map.325.qo_ref = f32[8,1024]{1,0:T(8,128)} custom-call(f32[8,1024]{1,0:T(8,128)} %get-tuple-element.73.sums_ref), custom_call_target="tpu_custom_call" | custom-call | tf_op jit(solution)/shard_map/pallas_call | solution.py:709
  143.2 28.8 %shard_map.326 = (bf16[2,1472,1024]{2,1,0:T(8,128)(2,1)}, f32[1472,512]{1,0:T(8,128)}, f32[1472,512]{1,0:T(8,128)}, f32[8,1024]{1,0:T(8,128)}) custom-call(f32[1472,1024]{1,0:T(8,128)} %get-tuple-element.72.dy_ref, f32[1472,1024]{1,0:T(8,128)} %get-tuple-element.69.z_ref.zo_ref, f32[8,1024]{1,0:T(8,128)} %shard_map.323.stats_ref.so_ref, f32[1,1024]{1,0:T(1,128)} %bitcast.65, ...), custom_call_target="tpu_custom_call" | custom-call | tf_op jit(solution)/shard_map/pallas_call | solution.py:755
  172.0 5.5 %shard_map.327.q_ref = f32[8,1024]{1,0:T(8,128)} custom-call(f32[8,1024]{1,0:T(8,128)} %get-tuple-element.76.sums_ref), custom_call_target="tpu_custom_call" | custom-call | tf_op jit(solution)/shard_map/pallas_call | solution.py:709
  178.2 18.9 %shard_map.328 = (bf16[2,1472,512]{2,1,0:T(8,128)(2,1)}, bf16[2,1472,512]{2,1,0:T(8,128)(2,1)}, f32[1472,512]{1,0:T(8,128)}, f32[1472,512]{1,0:T(8,128)}, f32[8,512]{1,0:T(8,128)}) custom-call(f32[1472,512]{1,0:T(8,128)} %get-tuple-element.74.dyt_ref, f32[1472,512]{1,0:T(8,128)} %get-tuple-element.75.dyp_ref, f32[1472,512]{1,0:T(8,128)} %get-tuple-element.66.z_ref.zt_ref, ...), custom_call_target="tpu_custom_call" | custom-call | tf_op jit(solution)/shard_map/pallas_call | solution.py:755
  197.2 5.1 %shard_map.329.q_ref = f32[8,512]{1,0:T(8,128)} custom-call(f32[8,512]{1,0:T(8,128)} %get-tuple-element.78.sums_ref), custom_call_target="tpu_custom_call" | custom-call | tf_op jit(solution)/shard_map/pallas_call | solution.py:709
  202.3 37.4 %shard_map.330 = (bf16[9,2,1472,512]{3,2,1,0:T(8,128)(2,1)}, f32[1472,512]{1,0:T(8,128)}, f32[8,512]{1,0:T(8,128)}) custom-call(f32[1472,512]{1,0:T(8,128)} %get-tuple-element.77.dy_ref, f32[1472,512]{1,0:T(8,128)} %get-tuple-element.63.z_ref.zs_ref, f32[8,512]{1,0:T(8,128)} %shard_map.319.stats_ref.ss_ref.s_ref, f32[1,512]{1,0:T(1,128)} %bitcast.60, ...), custom_call_target="tpu_custom_call" | custom-call | tf_op jit(solution)/shard_map/pallas_call | solution.py:755
  239.7 5.1 %shard_map.331.q_ref = f32[8,512]{1,0:T(8,128)} custom-call(f32[8,512]{1,0:T(8,128)} %get-tuple-element.80.sums_ref), custom_call_target="tpu_custom_call" | custom-call | tf_op jit(solution)/shard_map/pallas_call | solution.py:709
  244.8 14.3 %shard_map.332 = (bf16[2,1472,512]{2,1,0:T(8,128)(2,1)}, f32[1472,512]{1,0:T(8,128)}, f32[8,512]{1,0:T(8,128)}) custom-call(f32[1472,512]{1,0:T(8,128)} %get-tuple-element.79.dy_ref, f32[1472,512]{1,0:T(8,128)} %get-tuple-element.61.z_ref.zi_ref, f32[8,512]{1,0:T(8,128)} %shard_map.317.stats_ref.si_ref, f32[1,512]{1,0:T(1,128)} %bitcast.63, ...), custom_call_target="tpu_custom_call" | custom-call | tf_op jit(solution)/shard_map/pallas_call | solution.py:755
  259.2 5.1 %shard_map.333.q_ref = f32[8,512]{1,0:T(8,128)} custom-call(f32[8,512]{1,0:T(8,128)} %get-tuple-element.83.sums_ref), custom_call_target="tpu_custom_call" | custom-call | tf_op jit(solution)/shard_map/pallas_call | solution.py:709
  264.3 15.6 %shard_map.334 = (bf16[2,1472,512]{2,1,0:T(8,128)(2,1)}, f32[361,4,1024]{2,1,0:T(4,128)}) custom-call(f32[1472,512]{1,0:T(8,128)} %get-tuple-element.82.dy_ref, f32[1472,1024]{1,0:T(8,128)} %get-tuple-element.59.z_ref.zp_ref.zm_ref, f32[8,512]{1,0:T(8,128)} %shard_map.333.q_ref, f32[8,1024]{1,0:T(8,128)} %shard_map.315.stats_ref.total_ref, ...), custom_call_target="tpu_custom_call" | custom-call | tf_op jit(solution)/shard_map/pallas_call | solution.py:755
  283.6 182.8 %shard_map.335 = (f32[1024,1024]{1,0:T(8,128)}, f32[512,512]{1,0:T(8,128)}, f32[9,512,512]{2,1,0:T(8,128)}, f32[512,512]{1,0:T(8,128)}, f32[1024,1024]{1,0:T(8,128)}) custom-call(bf16[2,1472,512]{2,1,0:T(8,128)(2,1)} %get-tuple-element.86.refs_0_, bf16[2,1472,512]{2,1,0:T(8,128)(2,1)} %get-tuple-element.68.part_ref.refs_1_, ...), custom_call_target="tpu_custom_call" | custom-call | tf_op jit(solution)/shard_map/pallas_call | solution.py:670
  467.1 20.5 %shard_map.336 = f32[8,3584]{1,0:T(8,128)} custom-call(f32[8,3584]{1,0:T(8,128)} %pad.4.sums_ref), custom_call_target="tpu_custom_call" | custom-call | tf_op jit(solution)/shard_map/pallas_call | solution.py:709
  490.5 5.1 %copy.47 = f32[1024,1024]{1,0:T(8,128)} copy(f32[1024,1024]{1,0:T(8,128)} %get-tuple-element.138) | data formatting | bytes 8388608
  (28 shorter events, 25.0 us)
Async XLA Ops:
  487.5 8.0 %copy-start.3 = (f32[512,512]{1,0:T(8,128)S(1)}, f32[512,512]{1,0:T(8,128)}, u32[]{:S(2)}) copy-start(f32[512,512]{1,0:T(8,128)} %get-tuple-element.141) | copy-start | bytes 3145732
  490.5 6.8 %copy-start = (f32[9,512,512]{2,1,0:T(8,128)S(1)}, f32[9,512,512]{2,1,0:T(8,128)}, u32[]{:S(2)}) copy-start(f32[9,512,512]{2,1,0:T(8,128)} %get-tuple-element.98) | copy-start | bytes 28311556
  497.3 4.8 copy-start.2
  497.3 6.3 %copy-start.1 = (f32[1024,1024]{1,0:T(8,128)S(1)}, f32[1024,1024]{1,0:T(8,128)}, u32[]{:S(2)}) copy-start(f32[1024,1024]{1,0:T(8,128)} %get-tuple-element.150) | copy-start | bytes 12582916

commit v3 on v2

--- a/solution.py
+++ b/solution.py
@@ -465,12 +465,19 @@
 KEPT = 6
 
 
-def reduce_body(jobs, left_count, right_count, *refs):
-    lefts, rights = refs[:left_count], refs[left_count : left_count + right_count]
-    refs = refs[left_count + right_count :]
-    outs = refs[:5]
-    (x_ref, z_ref, turned_ref, own_ref, r0_ref, half_ref, r1_ref, quarter_ref, r2_ref, eighth_ref, r3_ref, full_ref, load_sem, store_sem) = refs[5:19]
-    sems = refs[19:]
+def reduce_body(jobs, side, slots, *refs):
+    lefts, rights, refs = refs[:6], refs[6:9], refs[9:]
+    (dys_hbm, zs_hbm, zi_hbm, gj_hbm, zm_hbm, ws_hbm), refs = refs[:6], refs[6:]
+    (s_split, s_spread, g_spread, q_spread, s_inner, g_inner, b_inner, g_split, b_split, q_out, q_mid, mask_ref, edge_ref, wi_ref, w_ref), refs = refs[:15], refs[15:]
+    outs, features_hbm, vectors_ref, refs = refs[:5], refs[5], refs[6], refs[7:]
+    (x_ref, z_ref, turned_ref, own_ref, r0_ref, half_ref, r1_ref, quarter_ref, r2_ref, eighth_ref, r3_ref, full_ref, load_sem, store_sem) = refs[:14]
+    (padded_ref, grad_ref, page_ref, tile_ref, zm_ref, pair_ref, part_ref, wide_ref, staged_ref, tap_ref, sums_ref, shared_ref, small_ref, spread_ref) = refs[14:28]
+    (page_sem, tap_sem, part_sem, staged_sem, sum_send, sum_recv, small_send, small_recv) = refs[28:36]
+    sems = refs[36:]
+    count, half = grad_ref.shape
+    pitch = tile_ref.shape[1]
+    tiles = count // pitch
+    stats_total = s_split[2:3, 0:1]
     block = own_ref.shape[1]
     mid = block // 2
     dp, bn = lax.axis_index("dp"), lax.axis_index("bn")
@@ -482,6 +489,8 @@
     to_core, to_x, to_y = at(z, x, y, 1 - core), at(z, 1 - x, y, core), at(z, x, 1 - y, core)
     depth = [(z + k) % 4 for k in (1, 2, 3)]
     to_z = [at(new_z, x, y, core) for new_z in depth]
+    to_far = [at(new_z, 1 - x, y, core) for new_z in depth]
+    to_diagonal = at(z, x, 1 - y, 1 - core)
     columns = (pl.ds(0, mid), pl.ds(mid, mid))
 
     def part(start, size):
@@ -542,24 +551,229 @@
             copy.wait()
 
     def load(j):
-        (left, left_columns, parts), (right, right_columns), _ = jobs[j]
+        (left, left_columns, parts), right, _ = jobs[j]
         slot = j % 2
-        return [
-            pltpu.make_async_copy(lefts[left].at[0:parts, :, left_columns], x_ref.at[slot, 0:parts], load_sem.at[slot, 0]),
-            pltpu.make_async_copy(rights[right].at[(slice(None),) * (len(rights[right].shape) - 2) + (slice(None), right_columns)] if right_columns is not None else rights[right[0]].at[right[1]], z_ref.at[slot], load_sem.at[slot, 1]),
-        ]
+        made = [pltpu.make_async_copy(lefts[left].at[0:parts, :, left_columns], x_ref.at[slot, 0:parts], load_sem.at[slot, 0])]
+        if right == "pair":
+            made.append(pltpu.make_async_copy(pair_ref, z_ref.at[slot], load_sem.at[slot, 1]))
+        elif right is not None:
+            made.append(pltpu.make_async_copy(rights[right[0]].at[:, :, right[1]], z_ref.at[slot], load_sem.at[slot, 1]))
+        return made
 
     def store(j):
         out, spot = jobs[j][2]
         return pltpu.make_async_copy(full_ref.at[j % KEPT], outs[out].at[spot], store_sem.at[j % KEPT])
 
+
+    everything = slice(None)
+
+    def page(source, target, k):
+        return pltpu.make_async_copy(source, target, page_sem.at[k])
+
+    def tap_load(tap):
+        return pltpu.make_async_copy(ws_hbm.at[tap], tap_ref.at[tap % 2], tap_sem.at[tap % 2])
+
+    upper = slice(half, 2 * half)
+    load_dy, load_zs = page(dys_hbm, grad_ref, 0), page(zs_hbm, page_ref, 1)
+    load_zi, load_zm = page(zi_hbm, page_ref, 1), page(zm_hbm.at[:, upper], zm_ref, 2)
+
+    def joined_load(k):
+        return pltpu.make_async_copy(gj_hbm.at[k * pitch : (k + 1) * pitch], tile_ref.at[k % 2], part_sem.at[0, k % 2])
+
+    def part_load(k):
+        return pltpu.make_async_copy(rights[2].at[:, k * pitch : (k + 1) * pitch], part_ref.at[k % 2], part_sem.at[1, k % 2])
+
+    places = staged_ref.shape[0]
+
+    def staged_store(k):
+        size = min(places, features_hbm.shape[0] - k * places)
+        return pltpu.make_async_copy(staged_ref.at[0:size], features_hbm.at[k * places : k * places + size], staged_sem)
+
+    group = [at(z, x, y, 1 - core), at(z, x, 1 - y, core), to_diagonal]
+
+    def sum_copies(which):
+        return [
+            pltpu.make_async_remote_copy(
+                src_ref=sums_ref.at[which], dst_ref=shared_ref.at[which, bn], send_sem=sum_send.at[which, k], recv_sem=sum_recv.at[which, k], device_id=peer, device_id_type=MESH
+            )
+            for k, peer in enumerate(group)
+        ]
+
+    def sum_start(which):
+        for copy in sum_copies(which):
+            copy.start()
+        shared_ref[which, bn] = sums_ref[which]
+
+    def sum_finish(which):
+        for copy in sum_copies(which):
+            copy.wait()
+        value = shared_ref[which, 0]
+        for k in range(1, shared_ref.shape[1]):
+            value = value + shared_ref[which, k]
+        sums_ref[which] = value
+
+    everyone = [to_x] + to_z + to_far
+
+    def small_copies():
+        return [
+            pltpu.make_async_remote_copy(
+                src_ref=small_ref, dst_ref=spread_ref.at[dp], send_sem=small_send.at[k], recv_sem=small_recv.at[k], device_id=peer, device_id_type=MESH
+            )
+            for k, peer in enumerate(everyone)
+        ]
+
+    def prepare():
+        load_dy.wait()
+        load_zs.wait()
+        padded_ref[0:GUARD, :] = jnp.zeros((GUARD, half), F32)
+        padded_ref[GUARD + count :, :] = jnp.zeros((GUARD, half), F32)
+        mean, inverse = moments(s_spread, stats_total, everything)
+        factor = g_spread[...] * inverse
+        first_sum, second_sum = q_spread[0:1, :] / stats_total, q_spread[1:2, :] / stats_total
+
+        def body(r, _):
+            dz = settle(grad_ref[r, :], page_ref[r, :], mask_ref[r, 0:1], mean, inverse, factor, first_sum, second_sum)
+            padded_ref[pl.ds(r.start + GUARD, CHUNK), :] = dz
+
+        over_rows(count, body)
+        load_zi.start()
+        load_zm.start()
+
+    def tap_work(tap):
+        move, dx = taps(side, slots)[tap]
+        slot = tap % 2
+        moved = padded_ref[GUARD - move : GUARD - move + count, :]
+        if dx:
+            moved = moved * edge_ref[:, 1 - dx : 2 - dx]
+        high = moved.astype(BF16)
+        z_ref[slot, 0] = high
+        z_ref[slot, 1] = (moved - high.astype(F32)).astype(BF16)
+        tap_load(tap).wait()
+        if tap < 8:
+            tap_load(tap + 1).start()
+
+    def tap_gradient(slot):
+        grad_ref[...] += dot_t(z_ref[slot, 0], tap_ref[slot]) + dot_t(z_ref[slot, 1], tap_ref[slot])
+
+    def inner_slope():
+        load_zi.wait()
+        joined_load(0).start()
+        joined_load(1).start()
+        mean, inverse = moments(s_inner, stats_total, everything)
+        gain, shift = g_inner[...], b_inner[...]
+
+        def tail(r, carry):
+            dy, sums = norm_slope(page_ref, grad_ref[r, :], mask_ref, r, everything, mean, inverse, gain, shift)
+            grad_ref[r, :] = dy
+            return (carry[0] + sums[0], carry[1] + sums[1])
+
+        zero = jnp.zeros((8, half), F32)
+        sums_ref[...] = jnp.zeros_like(sums_ref)
+        add_sums(sums_ref.at[0], everything, over_rows(count, tail, (zero, zero)))
+        sum_start(0)
+
+    def shifted(k):
+        return lambda r: pl.ds(pl.multiple_of(r.start + k * pitch, CHUNK), CHUNK)
+
+    def inner_tile(k):
+        mean, inverse = moments(s_inner, stats_total, everything)
+        factor = g_inner[...] * inverse
+        first_sum, second_sum = sums_ref[0, 0:1, :] / stats_total, sums_ref[0, 1:2, :] / stats_total
+        here = shifted(k)
+
+        def body(r, _):
+            q = here(r)
+            dz = settle(grad_ref[q, :], page_ref[q, :], mask_ref[q, 0:1], mean, inverse, factor, first_sum, second_sum)
+            split_store(pair_ref, (q,), dz)
+
+        over_rows(pitch, body)
+        rows_k = slice(k * pitch, (k + 1) * pitch)
+        wide_ref[:, 0:half] = product2_t(pair_ref, (rows_k,), wi_ref[...])
+        joined_load(k).wait()
+        mean, inverse = moments(s_split, stats_total, upper)
+        gain, shift = g_split[0:1, upper], b_split[0:1, upper]
+
+        def tail(r, carry):
+            q = here(r)
+            dy, sums = norm_slope(zm_ref, wide_ref[r, 0:half] + tile_ref[k % 2, r, :], mask_ref, q, everything, mean, inverse, gain, shift)
+            grad_ref[q, :] = dy
+            return (carry[0] + sums[0], carry[1] + sums[1])
+
+        zero = jnp.zeros((8, half), F32)
+        add_sums(sums_ref.at[1], everything, over_rows(pitch, tail, (zero, zero)))
+        if k + 2 < tiles:
+            joined_load(k + 2).start()
+
+    def small_start():
+        pieces = [
+            (q_mid, slice(half, 2 * half)), (sums_ref.at[1], everything), (sums_ref.at[0], everything), (q_spread, everything),
+            (q_mid, slice(0, half)), (q_out, slice(0, half)), (q_out, slice(half, 2 * half)),
+        ]
+        small_ref[...] = jnp.zeros_like(small_ref)
+        for k, (ref, columns_k) in enumerate(pieces):
+            small_ref[k : k + 1, :] = ref[0:1, columns_k]
+            small_ref[8 + k : 9 + k, :] = ref[1:2, columns_k]
+        for copy in small_copies():
+            copy.start()
+        spread_ref[dp] = small_ref[...]
+
+    def small_finish():
+        for copy in small_copies():
+            copy.wait()
+        value = spread_ref[0]
+        for k in range(1, spread_ref.shape[0]):
+            value = value + spread_ref[k]
+        vectors_ref[...] = value
+
+    def split_tile(k):
+        mean, inverse = moments(s_split, stats_total, upper)
+        factor = g_split[0:1, upper] * inverse
+        first_sum, second_sum = sums_ref[1, 0:1, :] / stats_total, sums_ref[1, 1:2, :] / stats_total
+        here = shifted(k)
+
+        def body(r, _):
+            q = here(r)
+            dz = settle(grad_ref[q, :], zm_ref[q, :], mask_ref[q, 0:1], mean, inverse, factor, first_sum, second_sum)
+            split_store(pair_ref, (q,), dz)
+
+        over_rows(pitch, body)
+        part_load(k).wait()
+        wide_ref[...] = dot_t(part_ref[k % 2, 0], w_ref[:, 0:half]) + dot_t(part_ref[k % 2, 1], w_ref[:, 0:half])
+        wide_ref[...] += product2_t(pair_ref, (slice(k * pitch, (k + 1) * pitch),), w_ref[:, half:])
+        if k + 2 < tiles:
+            part_load(k + 2).start()
+        if k:
+            staged_store(k - 1).wait()
+        spread_out(wide_ref, staged_ref)
+        staged_store(k).start()
+
+    def first_parts():
+        part_load(0).start()
+        part_load(1).start()
+
+    hosted = {
+        9: [inner_slope],
+        10: [lambda: (load_zm.wait(), sum_finish(0)), functools.partial(inner_tile, 0), functools.partial(inner_tile, 1)],
+        11: [functools.partial(inner_tile, 2), functools.partial(inner_tile, 3), lambda: sum_start(1)],
+        12: [lambda: sum_finish(1), small_start, first_parts],
+        14: [functools.partial(split_tile, 0), functools.partial(split_tile, 1)],
+        15: [functools.partial(split_tile, 2), functools.partial(split_tile, 3)],
+        16: [lambda: staged_store(3).wait()],
+        18: [small_finish],
+    }
+
+    load_dy.start()
+    load_zs.start()
+    tap_load(0).start()
     for copy in load(0):
         copy.start()
     barrier = pltpu.get_barrier_semaphore()
-    peers = [to_core, to_x, to_y] + to_z
+    peers = [to_core, to_x, to_y] + to_z + to_far + [to_diagonal]
     for peer in peers:
         pl.semaphore_signal(barrier, inc=1, device_id=peer, device_id_type=MESH)
     pl.semaphore_wait(barrier, len(peers))
+    prepare()
+    grad_ref[...] = jnp.zeros_like(grad_ref)
     total = len(jobs)
 
     @pl.loop(0, total + LAG + 1)
@@ -635,9 +849,17 @@
             def _(j=j):
                 for copy in load(j):
                     copy.wait()
+                for task in hosted.get(j, ()):
+                    task()
                 if j + 1 < total:
                     for copy in load(j + 1):
                         copy.start()
+                if j < 9:
+                    tap_work(j)
+
+        @pl.when(t < 9)
+        def _():
+            tap_gradient(t % 2)
 
         exact = functools.reduce(jnp.logical_or, [t == j for j in range(total) if jobs[j][0][2] == 1])
 
@@ -655,26 +877,33 @@
             begin(0, c)
 
 
-def reduce_call(jobs, lefts, rights, shapes, count, block):
-    hbm = pl.BlockSpec(memory_space=pl.ANY)
-    vmem = pltpu.VMEM
+def reduce_call(jobs, lefts, rights, hosted, constants, shapes, side, slots, pixel_shape):
+    hbm, vmem_spec = pl.BlockSpec(memory_space=pl.ANY), pl.BlockSpec(memory_space=pltpu.VMEM)
+    vmem, dma = pltpu.VMEM, pltpu.SemaphoreType.DMA
+    count, block = hosted[0].shape
+    pitch = count // TILES
     scratch = [
         vmem((2, 2, count, block), BF16), vmem((2, 2, count, block), BF16), vmem((block, count), BF16),
         vmem((2, block, block), F32), vmem((2, block // 2, block), F32), vmem((2, block // 2, block), F32),
         vmem((2, block // 4, block), F32), vmem((2, block // 4, block), F32), vmem((2, block // 8, block), F32), vmem((2, block // 8, block), F32),
         vmem((2, 3, block // 32, block), F32), vmem((KEPT, block, block), F32),
-        pltpu.SemaphoreType.DMA((2, 2)), pltpu.SemaphoreType.DMA((KEPT,)),
+        dma((2, 2)), dma((KEPT,)),
+        vmem((count + 2 * GUARD, block), F32), vmem((count, block), F32), vmem((count, block), F32), vmem((2, pitch, block), F32),
+        vmem((count, block), F32), vmem((2, count, block), BF16), vmem((2, 2, pitch, block), BF16), vmem((pitch, 2 * block), F32),
+        vmem((pitch // slots, slots, 2 * block), F32), vmem((2, block, block), BF16), vmem((2, 8, block), F32), vmem((2, 4, 8, block), F32),
+        vmem((16, block), F32), vmem((8, 16, block), F32),
+        dma((3,)), dma((2,)), dma((2, 2)), dma(()), dma((2, 3)), dma((2, 3)), dma((7,)), dma((7,)),
     ]
     for width in (1, 2, 2, 3, 6, 2, 2, 1):
-        scratch += [pltpu.SemaphoreType.DMA((width, 2)), pltpu.SemaphoreType.DMA((width, 2))]
+        scratch += [dma((width, 2)), dma((width, 2))]
     return pl.pallas_call(
-        functools.partial(reduce_body, jobs, len(lefts), len(rights)),
-        in_specs=[hbm] * (len(lefts) + len(rights)),
-        out_specs=[hbm] * len(shapes),
-        out_shape=[sds(shape) for shape in shapes],
+        functools.partial(reduce_body, jobs, side, slots),
+        in_specs=[hbm] * (len(lefts) + len(rights) + len(hosted)) + [vmem_spec] * len(constants),
+        out_specs=[hbm] * (len(shapes) + 1) + [vmem_spec],
+        out_shape=[sds(shape) for shape in shapes] + [sds(pixel_shape), sds((16, block))],
         scratch_shapes=scratch,
-        compiler_params=pltpu.CompilerParams(collective_id=3, has_side_effects=True, vmem_limit_bytes=56 * 1024 * 1024),
-    )(*lefts, *rights)
+        compiler_params=pltpu.CompilerParams(collective_id=3, has_side_effects=True, vmem_limit_bytes=60 * 1024 * 1024),
+    )(*lefts, *rights, *hosted, *constants)
 
 
 def gather_sums_body(axis, sums_ref, out_ref, slots_ref, send_sem, recv_sem):
@@ -831,51 +1060,58 @@
         ],
     )
     q_spread = group(q_spread)
-    moved_spec = pl.BlockSpec((1, 2, count, half), lambda i: (i, 0, 0, 0))
-    moved, dy_inner, q_inner = call(
-        functools.partial(spread_back_body, side, slots),
-        [
-            fixed(dy_spread), fixed(z_spread), fixed(s_spread), fixed(spread_gain), fixed(q_spread), fixed(s_split), fixed(mask), fixed(edges), (spread_weight, tap_spec),
-            fixed(z_inner), fixed(s_inner), fixed(inner_gain), fixed(inner_shift),
-        ],
-        [(sds((9, 2, count, half), BF16), moved_spec), (sds((count, half)), out_whole((count, half))), (sds((8, half)), sums_half)],
-        [pltpu.VMEM((count + 2 * GUARD, half), F32), pltpu.VMEM((count, half), F32)],
-        (9,),
-    )
-    q_inner = group(q_inner)
-    dz_inner, dy_main, q_main = call(
-        inner_back_body,
-        [
-            (dy_inner, r_half), (z_inner, r_half), fixed(s_inner), fixed(inner_gain), fixed(q_inner), fixed(s_split), (mask, r_mask), fixed(inner_kernel),
-            (grad_joined, r_half), (z_split, rows(pitch, half, 1)), fixed(split_gain), fixed(split_shift),
-        ],
-        [(sds((2, count, half), BF16), pair_half), (sds((count, half)), r_half), (sds((8, half)), sums_half)],
-        [pltpu.VMEM((pitch, half), F32)],
-    )
-    q_main = group(q_main)
-    dz_main, grad_features = call(
-        split_back_body,
-        [(dy_main, r_half), (z_split, rows(pitch, half, 1)), fixed(q_main), fixed(s_split), fixed(split_gain), (mask, r_mask), (dz_part, pair_half), fixed(split_kernel)],
-        [(sds((2, count, half), BF16), pair_half), (sds(cotangent.shape), pixels(pitch, cotangent.shape))],
-        [pltpu.VMEM((pitch, full), F32)],
-    )
-    small = jnp.concatenate([q_mid[0:2, half:], q_main[0:2], q_inner[0:2], q_spread[0:2], q_mid[0:2, :half], q_out[0:2]], axis=1)
     if shape == (8, 4):
         low, high = slice(0, half), slice(half, full)
         every = slice(None)
-        lefts = [trans2, part2, joined2, x0[None], inner2, main2]
-        rights = [dz_out, dz_trans, dz_part, moved, dz_inner, dz_main]
-        jobs = [((0, every, 2), (0, low), (4, (low, low))), ((0, every, 2), (0, high), (4, (low, high)))]
+        jobs = [((4, every, 2), None, (2, (tap,))) for tap in range(9)]
+        jobs += [((0, every, 2), (0, low), (4, (low, low))), ((0, every, 2), (0, high), (4, (low, high)))]
         jobs += [((1, every, 2), (0, low), (4, (high, low))), ((1, every, 2), (0, high), (4, (high, high)))]
-        jobs += [((2, every, 2), (1, every), (3, (every, every)))]
+        jobs += [((5, every, 2), "pair", (1, (every, every))), ((2, every, 2), (1, every), (3, (every, every)))]
         jobs += [((3, low, 1), (2, every), (0, (low, low))), ((3, high, 1), (2, every), (0, (high, low)))]
-        jobs += [((4, every, 2), ((3, tap), None), (2, (tap,))) for tap in range(9)]
-        jobs += [((5, every, 2), (4, every), (1, (every, every)))]
-        jobs += [((3, low, 1), (5, every), (0, (low, high))), ((3, high, 1), (5, every), (0, (high, high)))]
-        shapes = [(full, full), (half, half), (9, half, half), (half, half), (full, full)]
-        grad_split, grad_inner, grad_spread, grad_transition, grad_output = reduce_call(jobs, lefts, rights, shapes, count, half)
-        small = gather_sums(jnp.pad(small, ((0, 6), (0, 0))), shape[0], 4, "dp")
+        jobs += [((3, low, 1), "pair", (0, (low, high))), ((3, high, 1), "pair", (0, (high, high)))]
+        grad_split, grad_inner, grad_spread, grad_transition, grad_output, grad_features, vectors = reduce_call(
+            jobs,
+            [trans2, part2, joined2, x0[None], inner2, main2],
+            [dz_out, dz_trans, dz_part],
+            [dy_spread, z_spread, z_inner, grad_joined, z_split, spread_weight],
+            [
+                s_split, s_spread, spread_gain, q_spread, s_inner, inner_gain, inner_shift, split_gain, split_shift, q_out, q_mid,
+                mask, edges, inner_kernel, split_kernel,
+            ],
+            [(full, full), (half, half), (9, half, half), (half, half), (full, full)],
+            side, slots, cotangent.shape,
+        )
+        small = vectors.reshape(2, 8 * half)
     else:
+        moved_spec = pl.BlockSpec((1, 2, count, half), lambda i: (i, 0, 0, 0))
+        moved, dy_inner, q_inner = call(
+            functools.partial(spread_back_body, side, slots),
+            [
+                fixed(dy_spread), fixed(z_spread), fixed(s_spread), fixed(spread_gain), fixed(q_spread), fixed(s_split), fixed(mask), fixed(edges), (spread_weight, tap_spec),
+                fixed(z_inner), fixed(s_inner), fixed(inner_gain), fixed(inner_shift),
+            ],
+            [(sds((9, 2, count, half), BF16), moved_spec), (sds((count, half)), out_whole((count, half))), (sds((8, half)), sums_half)],
+            [pltpu.VMEM((count + 2 * GUARD, half), F32), pltpu.VMEM((count, half), F32)],
+            (9,),
+        )
+        q_inner = group(q_inner)
+        dz_inner, dy_main, q_main = call(
+            inner_back_body,
+            [
+                (dy_inner, r_half), (z_inner, r_half), fixed(s_inner), fixed(inner_gain), fixed(q_inner), fixed(s_split), (mask, r_mask), fixed(inner_kernel),
+                (grad_joined, r_half), (z_split, rows(pitch, half, 1)), fixed(split_gain), fixed(split_shift),
+            ],
+            [(sds((2, count, half), BF16), pair_half), (sds((count, half)), r_half), (sds((8, half)), sums_half)],
+            [pltpu.VMEM((pitch, half), F32)],
+        )
+        q_main = group(q_main)
+        dz_main, grad_features = call(
+            split_back_body,
+            [(dy_main, r_half), (z_split, rows(pitch, half, 1)), fixed(q_main), fixed(s_split), fixed(split_gain), (mask, r_mask), (dz_part, pair_half), fixed(split_kernel)],
+            [(sds((2, count, half), BF16), pair_half), (sds(cotangent.shape), pixels(pitch, cotangent.shape))],
+            [pltpu.VMEM((pitch, full), F32)],
+        )
+        small = jnp.concatenate([q_mid[0:2, half:], q_main[0:2], q_inner[0:2], q_spread[0:2], q_mid[0:2, :half], q_out[0:2]], axis=1)
         grad_output = jnp.concatenate([weight_grad(trans2, dz_out), weight_grad(part2, dz_out)], axis=0)
         grad_transition, grad_inner = weight_grad(joined2, dz_trans), weight_grad(main2, dz_inner)
         grad_split = jnp.concatenate([weight_grad(x0[None], dz_part), weight_grad(x0[None], dz_main)], axis=1)

time: 510 us -> 437 us (0.86)
  Pallas kernels: 474 us -> 405 us
    pallas_call x11 -> x8, Pallas kernels: 217 us -> 150 us  [call(): pl.pallas_call(body, grid=steps, in_specs=[spec for _, spec in ins], out_...]
    pallas_call x11 -> x8, Pallas kernels: 74.6 us -> 43.8 us  [gather_sums(): pl.pallas_call(functools.partial(gather_sums_body, axis), in_specs=[spec]...]
    pallas_call x1, Pallas kernels: 183 us -> 212 us  [reduce_call(): pl.pallas_call(functools.partial(reduce_body, jobs, side, slots), in_spec...]
where the time goes in v3:
time: 437 us; the launch traced here: 436 us
  Pallas kernels  405 us (93%)
  local copies, waits for them, and re-layouts  25.6 us (6%)
  other arithmetic  4.38 us (1%)
    pallas_call x1, Pallas kernels, reduce_call(): pl.pallas_call(functools.partial(reduce_body, jobs, side, slots), in_spec...  212 us
    pallas_call x8, Pallas kernels, call(): pl.pallas_call(body, grid=steps, in_specs=[spec for _, spec in ins], out_...  150 us
    pallas_call x8, Pallas kernels, gather_sums(): pl.pallas_call(functools.partial(gather_sums_body, axis), in_specs=[spec]...  43.8 us
    unnamed x18, local copies, waits for them, and re-layouts  21.1 us

profile of v3, /device:TPU:0, one launch (start us, length us, event | category | flops | bytes accessed | tf_op | source)
XLA Modules:
  0.0 436.5 jit_solution(5358574983211056906)
XLA Ops:
  1.3 1.4 fusion.23
  2.7 2.6 fusion.20
  6.5 1.7 select_convert_fusion.edge_ref.refs_27_
  8.2 12.7 %shard_map.314 = (bf16[1472,1024]{1,0:T(8,128)(2,1)}, f32[1472,1024]{1,0:T(8,128)}, f32[8,1024]{1,0:T(8,128)}) custom-call(bf16[361,4,1024]{2,1,0:T(4,128)(2,1)} %bitcast.49, f32[1472,128]{1,0:T(8,128)} %broadcast_in_dim.57.mask_ref.refs_26_, bf16[1024,1024]{1,0:T(8,128)(2,1)} %refs_29_.1), custom_call_target="tpu_custom_call" | custom-call | tf_op jit(solution)/shard_map/pallas_call | solution.py:984
  21.0 6.7 %shard_map.315.stats_ref.total_ref.refs_15_ = f32[8,1024]{1,0:T(8,128)} custom-call(f32[8,1024]{1,0:T(8,128)} %get-tuple-element.54.sums_ref), custom_call_target="tpu_custom_call" | custom-call | tf_op jit(solution)/shard_map/pallas_call | solution.py:938
  27.6 14.1 %shard_map.316 = (bf16[2,1472,512]{2,1,0:T(8,128)(2,1)}, f32[1472,512]{1,0:T(8,128)}, bf16[2,1472,512]{2,1,0:T(8,128)(2,1)}, f32[1472,512]{1,0:T(8,128)}, f32[8,512]{1,0:T(8,128)}) custom-call(f32[1472,1024]{1,0:T(8,128)} %get-tuple-element.53.z_ref.zp_ref.refs_13_, f32[8,1024]{1,0:T(8,128)} %shard_map.315.stats_ref.total_ref.refs_15_, f32[1,1024]{1,0:T(1,128)} %bitcast.50, ...), custom_call_target="tpu_custom_call" | custom-call | tf_op jit(solution)/shard_map/pallas_call | solution.py:984
  41.8 5.1 %shard_map.317.stats_ref.refs_19_ = f32[8,512]{1,0:T(8,128)} custom-call(f32[8,512]{1,0:T(8,128)} %get-tuple-element.56.sums_ref), custom_call_target="tpu_custom_call" | custom-call | tf_op jit(solution)/shard_map/pallas_call | solution.py:938
  46.9 34.9 %shard_map.318 = (bf16[2,1472,512]{2,1,0:T(8,128)(2,1)}, f32[1472,512]{1,0:T(8,128)}, f32[8,512]{1,0:T(8,128)}) custom-call(f32[1472,512]{1,0:T(8,128)} %get-tuple-element.55.z_ref.refs_11_, f32[8,1024]{1,0:T(8,128)} %shard_map.315.stats_ref.total_ref.refs_15_, f32[8,512]{1,0:T(8,128)} %shard_map.317.stats_ref.refs_19_, f32[1,512]{1,0:T(1,128)} %bitcast.65, ...), custom_call_target="tpu_custom_call" | custom-call | tf_op jit(solution)/shard_map/pallas_call | solution.py:984
  81.8 5.1 %shard_map.319.stats_ref.ss_ref.refs_16_ = f32[8,512]{1,0:T(8,128)} custom-call(f32[8,512]{1,0:T(8,128)} %get-tuple-element.58.sums_ref), custom_call_target="tpu_custom_call" | custom-call | tf_op jit(solution)/shard_map/pallas_call | solution.py:938
  86.9 10.1 %shard_map.320 = (bf16[2,1472,512]{2,1,0:T(8,128)(2,1)}, f32[1472,512]{1,0:T(8,128)}, f32[8,512]{1,0:T(8,128)}) custom-call(f32[1472,512]{1,0:T(8,128)} %get-tuple-element.57.z_ref.zs_ref.refs_10_, f32[8,1024]{1,0:T(8,128)} %shard_map.315.stats_ref.total_ref.refs_15_, f32[8,512]{1,0:T(8,128)} %shard_map.319.stats_ref.ss_ref.refs_16_, f32[1,512]{1,0:T(1,128)} %bitcast.57, ...), custom_call_target="tpu_custom_call" | custom-call | tf_op jit(solution)/shard_map/pallas_call | solution.py:984
  97.0 5.1 %shard_map.321.stats_ref.st_ref = f32[8,512]{1,0:T(8,128)} custom-call(f32[8,512]{1,0:T(8,128)} %get-tuple-element.61.sums_ref), custom_call_target="tpu_custom_call" | custom-call | tf_op jit(solution)/shard_map/pallas_call | solution.py:938
  102.2 15.8 %shard_map.322 = (bf16[2,1472,512]{2,1,0:T(8,128)(2,1)}, f32[1472,1024]{1,0:T(8,128)}, f32[8,1024]{1,0:T(8,128)}) custom-call(f32[1472,512]{1,0:T(8,128)} %get-tuple-element.60.z_ref.zt_ref, f32[8,1024]{1,0:T(8,128)} %shard_map.315.stats_ref.total_ref.refs_15_, f32[8,512]{1,0:T(8,128)} %shard_map.321.stats_ref.st_ref, f32[1,512]{1,0:T(1,128)} %bitcast.60, ...), custom_call_target="tpu_custom_call" | custom-call | tf_op jit(solution)/shard_map/pallas_call | solution.py:984
  117.9 5.6 %shard_map.323.stats_ref.so_ref = f32[8,1024]{1,0:T(8,128)} custom-call(f32[8,1024]{1,0:T(8,128)} %get-tuple-element.64.sums_ref), custom_call_target="tpu_custom_call" | custom-call | tf_op jit(solution)/shard_map/pallas_call | solution.py:938
  123.6 14.1 %shard_map.324 = (f32[361,4,1024]{2,1,0:T(4,128)}, f32[1472,1024]{1,0:T(8,128)}, f32[8,1024]{1,0:T(8,128)}) custom-call(f32[1472,1024]{1,0:T(8,128)} %get-tuple-element.63.z_ref.zo_ref, f32[8,1024]{1,0:T(8,128)} %shard_map.315.stats_ref.total_ref.refs_15_, f32[8,1024]{1,0:T(8,128)} %shard_map.323.stats_ref.so_ref, f32[1,1024]{1,0:T(1,128)} %bitcast.63, ...), custom_call_target="tpu_custom_call" | custom-call | tf_op jit(solution)/shard_map/pallas_call | solution.py:984
  137.6 5.6 %shard_map.325.qo_ref.refs_24_ = f32[8,1024]{1,0:T(8,128)} custom-call(f32[8,1024]{1,0:T(8,128)} %get-tuple-element.72.sums_ref), custom_call_target="tpu_custom_call" | custom-call | tf_op jit(solution)/shard_map/pallas_call | solution.py:938
  143.2 28.8 %shard_map.326 = (bf16[2,1472,1024]{2,1,0:T(8,128)(2,1)}, f32[1472,512]{1,0:T(8,128)}, f32[1472,512]{1,0:T(8,128)}, f32[8,1024]{1,0:T(8,128)}) custom-call(f32[1472,1024]{1,0:T(8,128)} %get-tuple-element.71.dy_ref, f32[1472,1024]{1,0:T(8,128)} %get-tuple-element.63.z_ref.zo_ref, f32[8,1024]{1,0:T(8,128)} %shard_map.323.stats_ref.so_ref, f32[1,1024]{1,0:T(1,128)} %bitcast.64, ...), custom_call_target="tpu_custom_call" | custom-call | tf_op jit(solution)/shard_map/pallas_call | solution.py:984
  172.0 5.5 %shard_map.327.q_ref.refs_25_ = f32[8,1024]{1,0:T(8,128)} custom-call(f32[8,1024]{1,0:T(8,128)} %get-tuple-element.76.sums_ref), custom_call_target="tpu_custom_call" | custom-call | tf_op jit(solution)/shard_map/pallas_call | solution.py:938
  177.5 19.0 %shard_map.328 = (bf16[2,1472,512]{2,1,0:T(8,128)(2,1)}, bf16[2,1472,512]{2,1,0:T(8,128)(2,1)}, f32[1472,512]{1,0:T(8,128)}, f32[1472,512]{1,0:T(8,128)}, f32[8,512]{1,0:T(8,128)}) custom-call(f32[1472,512]{1,0:T(8,128)} %get-tuple-element.74.dyt_ref, f32[1472,512]{1,0:T(8,128)} %get-tuple-element.75.dyp_ref, f32[1472,512]{1,0:T(8,128)} %get-tuple-element.60.z_ref.zt_ref, ...), custom_call_target="tpu_custom_call" | custom-call | tf_op jit(solution)/shard_map/pallas_call | solution.py:984
  196.5 5.1 %shard_map.329.refs_18_ = f32[8,512]{1,0:T(8,128)} custom-call(f32[8,512]{1,0:T(8,128)} %get-tuple-element.81.sums_ref), custom_call_target="tpu_custom_call" | custom-call | tf_op jit(solution)/shard_map/pallas_call | solution.py:938
  201.7 211.7 %shard_map.330 = (f32[1024,1024]{1,0:T(8,128)}, f32[512,512]{1,0:T(8,128)}, f32[9,512,512]{2,1,0:T(8,128)}, f32[512,512]{1,0:T(8,128)}, f32[1024,1024]{1,0:T(8,1...) custom-call(bf16[2,1472,512]{2,1,0:T(8,128)(2,1)} %get-tuple-element.66.refs_0_, ...), custom_call_target="tpu_custom_call" | custom-call | tf_op jit(solution)/shard_map/pallas_call | solution.py:899
  415.4 6.9 %copy.43 = f32[4,19,19,1024]{3,0,2,1:T(4,128)} copy(f32[4,19,19,1024]{3,0,2,1:T(4,128)} %bitcast.47) | data formatting | bytes 11829248
  422.3 4.9 %copy.44 = f32[1024,1024]{1,0:T(8,128)} copy(f32[1024,1024]{1,0:T(8,128)} %get-tuple-element.126) | data formatting | bytes 8388608
  428.2 4.8 %copy.46 = f32[3,3,512,512]{3,2,1,0:T(8,128)} copy(f32[3,3,512,512]{3,2,1,0:T(8,128)S(1)} %bitcast.45) | data formatting | bytes 18874368
  434.5 2.0 copy.48
  (22 shorter events, 5.6 us)
Async XLA Ops:
  415.4 12.8 %slice-start = ((s8[9437184]{0:T(1024)(128)(4,1)}), s8[4194304]{0:T(1024)(128)(4,1)S(1)}, s32[]{:S(2)}) async-start(s8[9437184]{0:T(1024)(128)(4,1)} %bitcast.43), calls=%async_computation | async-start | bytes 8388608
  415.4 12.8 %slice-start.1 = ((s8[9437184]{0:T(1024)(128)(4,1)}), s8[4194304]{0:T(1024)(128)(4,1)S(1)}, s32[]{:S(2)}) async-start(s8[9437184]{0:T(1024)(128)(4,1)} %bitcast.43), calls=%async_computation.1 | async-start | bytes 8388608
  422.3 4.9 %copy-start.2 = (f32[512,512]{1,0:T(8,128)S(1)}, f32[512,512]{1,0:T(8,128)}, u32[]{:S(2)}) copy-start(f32[512,512]{1,0:T(8,128)} %get-tuple-element.129) | copy-start | bytes 3145732
  422.3 5.9 %slice-start.2 = ((s8[9437184]{0:T(1024)(128)(4,1)}), s8[1048576]{0:T(1024)(128)(4,1)S(1)}, s32[]{:S(2)}) async-start(s8[9437184]{0:T(1024)(128)(4,1)} %bitcast.43), calls=%async_computation.2 | async-start | bytes 2097152
  428.2 4.8 %copy-start.1 = (f32[512,512]{1,0:T(8,128)S(1)}, f32[512,512]{1,0:T(8,128)}, u32[]{:S(2)}) copy-start(f32[512,512]{1,0:T(8,128)} %get-tuple-element.135) | copy-start | bytes 3145732
  428.2 6.3 %copy-start = (f32[1024,1024]{1,0:T(8,128)S(1)}, f32[1024,1024]{1,0:T(8,128)}, u32[]{:S(2)}) copy-start(f32[1024,1024]{1,0:T(8,128)} %get-tuple-element.138) | copy-start | bytes 12582916

commit v4 on v3

--- a/solution.py
+++ b/solution.py
@@ -2,6 +2,7 @@
 
 import jax
 import jax.numpy as jnp
+import numpy as np
 from jax import lax
 from jax.experimental import pallas as pl
 from jax.experimental.pallas import tpu as pltpu
@@ -87,7 +88,7 @@
     return jnp.sum(value.reshape(value.shape[0] // 8, 8, value.shape[1]), axis=0)
 
 
-def over_rows(count, body, carry=None, unroll=2):
+def over_rows(count, body, carry=None, unroll=4):
     def step(k, c):
         return body(pl.ds(pl.multiple_of(k * CHUNK, CHUNK), CHUNK), c)
 
@@ -440,6 +441,13 @@
     spread_out(scratch_ref, grad_ref)
 
 
+def features_body(dzp_ref, dzm_ref, w_ref, grad_ref, scratch_ref):
+    half = dzp_ref.shape[2]
+    scratch_ref[...] = product2_t(dzp_ref, (), w_ref[:, :half])
+    scratch_ref[...] += product2_t(dzm_ref, (), w_ref[:, half:])
+    spread_out(scratch_ref, grad_ref)
+
+
 def weight_body(x_ref, dz_ref, dw_ref):
     turned = x_ref[0].T
     value = dot(turned, dz_ref[0]) + dot(turned, dz_ref[1])
@@ -461,22 +469,330 @@
     )(x, dz)
 
 
+SPLIT, INNER, SPREAD, TRANS, OUT, BACK_OUT = range(6)
+
+
+def front_body(side, slots, *refs):
+    (features_hbm, cotangent_hbm, w_split_hbm, w_inner_hbm, w_spread_hbm, w_trans_hbm, w_out_hbm), refs = refs[:7], refs[7:]
+    (g_split, b_split, g_inner, b_inner, g_spread, b_spread, g_trans, b_trans, g_out, b_out, edge_ref, counts_ref, sides_ref), refs = refs[:13], refs[13:]
+    (x_out, zp_out, zm_out, main_out, part_out, zi_out, inner_out, zs_out, joined_out, zt_out, trans_out, result_hbm, dlow_out, dhigh_out, total_ref, mask_ref), refs = refs[:16], refs[16:]
+    (p0, p1, p2, p3, p4, p5, p6, p7, q0, q1, q2, q3, wide_ref, feature_ref, cot_ref, staged_ref), refs = refs[:16], refs[16:]
+    (w_split, w_inner, w_spread, w_trans, w_out, local_ref, shared_ref), refs = refs[:7], refs[7:]
+    weight_sem, feature_sem, cot_sem, staged_sem, out_sem, sum_send, sum_recv = refs
+    count, half = p0.shape
+    pitch = count // TILES
+    places = pitch // slots
+    low, high, everything = slice(0, half), slice(half, 2 * half), slice(None)
+    dp, bn = lax.axis_index("dp"), lax.axis_index("bn")
+    members = shared_ref.shape[1]
+    group = [lax.rem(bn + k, members) for k in range(1, members)]
+
+    weights = [
+        pltpu.make_async_copy(source, target, weight_sem.at[k])
+        for k, (source, target) in enumerate(
+            ((w_split_hbm, w_split), (w_inner_hbm, w_inner), (w_spread_hbm, w_spread), (w_trans_hbm, w_trans), (w_out_hbm, w_out))
+        )
+    ]
+
+    def rows_of(k):
+        return min(places, features_hbm.shape[0] - k * places)
+
+    def feature_load(k):
+        size = rows_of(k)
+        return pltpu.make_async_copy(features_hbm.at[k * places : k * places + size], feature_ref.at[k % 2, 0:size], feature_sem.at[k % 2])
+
+    def cot_load(k):
+        size = rows_of(k)
+        return pltpu.make_async_copy(cotangent_hbm.at[k * places : k * places + size], cot_ref.at[0:size], cot_sem)
+
+    def result_store(k):
+        size = rows_of(k)
+        return pltpu.make_async_copy(staged_ref.at[0:size], result_hbm.at[k * places : k * places + size], staged_sem)
+
+    pending = {}
+
+    def write(name, source, target):
+        copy = pltpu.make_async_copy(source, target, out_sem.at[len(pending)])
+        copy.start()
+        pending[name] = [copy, True]
+
+    def written(name):
+        if pending[name][1]:
+            pending[name][0].wait()
+            pending[name][1] = False
+
+    def sum_copies(which, width):
+        return [
+            pltpu.make_async_remote_copy(
+                src_ref=local_ref.at[which, :, 0:width], dst_ref=shared_ref.at[which, bn, :, 0:width],
+                send_sem=sum_send.at[which, k], recv_sem=sum_recv.at[which, k], device_id={"bn": peer}, device_id_type=MESH,
+            )
+            for k, peer in enumerate(group)
+        ]
+
+    def exchange(which, width, beside=None):
+        copies = sum_copies(which, width)
+        for copy in copies:
+            copy.start()
+        shared_ref[which, bn, :, 0:width] = local_ref[which, :, 0:width]
+        if beside is not None:
+            beside()
+        for copy in copies:
+            copy.wait()
+        value = shared_ref[which, 0, :, 0:width]
+        for k in range(1, members):
+            value = value + shared_ref[which, k, :, 0:width]
+        total_ref[which, :, 0:width] = value
+
+    def stats(which):
+        return total_ref.at[which]
+
+    def affine(which, gain_ref, shift_ref, columns):
+        mean, inverse = moments(stats(which), total_ref[SPLIT, 2:3, 0:1], columns)
+        return mean, gain_ref[0:1, columns] * inverse, shift_ref[0:1, columns]
+
+    def activate(z_ref, r, mean, scale, shift):
+        return mish((z_ref[r, :] - mean) * scale + shift) * mask_ref[r, 0:1]
+
+    feature_load(0).start()
+    for k in (0, 1):
+        weights[k].start()
+    feature_load(1).start()
+    barrier = pltpu.get_barrier_semaphore()
+    for peer in group:
+        pl.semaphore_signal(barrier, inc=1, device_id={"bn": peer}, device_id_type=MESH)
+    local_ref[...] = jnp.zeros_like(local_ref)
+    limits = [jnp.where(k < counts_ref[0], sides_ref[k], 0).astype(F32) for k in range(slots)]
+
+    def mask_rows(r, _):
+        index = (r.start + lax.broadcasted_iota(jnp.int32, (CHUNK, 128), 0)).astype(F32)
+        place = jnp.floor((index + 0.5) * (1.0 / slots))
+        slot = index - place * slots
+        y = jnp.floor((place + 0.5) * (1.0 / side))
+        x = place - y * side
+        limit = jnp.zeros_like(index)
+        for k in range(slots):
+            limit = jnp.where(slot == k, limits[k], limit)
+        mask_ref[r, :] = jnp.where(jnp.maximum(x, y) < limit, 1.0, 0.0)
+
+    over_rows(count, mask_rows)
+    for k in range(TILES):
+        feature_load(k).wait()
+        compact(feature_ref.at[k % 2], wide_ref)
+        if k + 2 < TILES:
+            feature_load(k + 2).start()
+        here = pl.ds(k * pitch, pitch)
+
+        def body(r, _, k=k):
+            q = pl.ds(pl.multiple_of(r.start + k * pitch, CHUNK), CHUNK)
+            for h, columns in enumerate((low, high)):
+                q0[h, q, :] = jnp.where(mask_ref[q, 0:1] > 0.0, wide_ref[r, columns], 0.0).astype(BF16)
+
+        over_rows(pitch, body)
+    for k in (2, 3, 4):
+        weights[k].start()
+    cot_load(0).start()
+    write("x", q0, x_out)
+    weights[0].wait()
+    p0[...] = dot(q0[0], w_split[low, low]) + dot(q0[1], w_split[high, low])
+    p1[0:count, :] = dot(q0[0], w_split[low, high]) + dot(q0[1], w_split[high, high])
+    write("zm", p1.at[0:count], zm_out)
+    write("zp", p0, zp_out)
+
+    def add_squares(which, z_ref, columns, masked=False):
+        def body(r, carry):
+            value = z_ref[r, :]
+            kept = value * mask_ref[r, 0:1] if masked else value
+            return (carry[0] + fold(kept), carry[1] + fold(kept * value))
+
+        zero = jnp.zeros((8, half), F32)
+        add_sums(local_ref.at[which], columns, over_rows(count, body, (zero, zero)))
+
+    add_squares(SPLIT, p0, low)
+    add_squares(SPLIT, p1, high)
+    local_ref[SPLIT, 2:3, 0:128] = jnp.sum(mask_ref[...], axis=0, keepdims=True)
+    pl.semaphore_wait(barrier, members - 1)
+    exchange(SPLIT, 2 * half)
+
+    mean, scale, shift = affine(SPLIT, g_split, b_split, high)
+
+    def main_rows(r, _):
+        act = activate(p1, r, mean, scale, shift)
+        p2[r, :] = act
+        split_store(q2, (r,), act)
+
+    over_rows(count, main_rows)
+    write("main", q2, main_out)
+    weights[1].wait()
+    p3[...] = product2(q2, (), w_inner[...])
+    write("zi", p3, zi_out)
+    add_squares(INNER, p3, low)
+    mean_p, scale_p, shift_p = affine(SPLIT, g_split, b_split, low)
+
+    def part_rows(r, _):
+        split_store(q1, (r,), activate(p0, r, mean_p, scale_p, shift_p))
+
+    exchange(INNER, half, lambda: over_rows(count, part_rows))
+    write("part", q1, part_out)
+
+    written("zm")
+    written("x")
+    mean_i, scale_i, shift_i = affine(INNER, g_inner, b_inner, low)
+    p1[0:GUARD, :] = jnp.zeros((GUARD, half), F32)
+    p1[GUARD + count :, :] = jnp.zeros((GUARD, half), F32)
+
+    def inner_rows(r, _):
+        act = activate(p3, r, mean_i, scale_i, shift_i)
+        p1[pl.ds(r.start + GUARD, CHUNK), :] = act
+        split_store(q0, (r,), act)
+
+    over_rows(count, inner_rows)
+    write("inner", q0, inner_out)
+    weights[2].wait()
+    written("zi")
+    written("main")
+    for tap, (move, dx) in enumerate(taps(side, slots)):
+        if move:
+            pair_ref = (q2, q3)[tap % 2]
+            moved = p1[GUARD + move : GUARD + move + count, :]
+            if dx:
+                moved = moved * edge_ref[:, dx + 1 : dx + 2]
+            split_store(pair_ref, (slice(None),), moved)
+        else:
+            pair_ref = q0
+        part = product2(pair_ref, (), w_spread[tap])
+        if tap == 0:
+            p3[...] = part
+        else:
+            p3[...] += part
+    write("zs", p3, zs_out)
+    add_squares(SPREAD, p3, low, True)
+    exchange(SPREAD, half)
+
+    mean_s, scale_s, shift_s = affine(SPREAD, g_spread, b_spread, low)
+
+    def joined_rows(r, _):
+        split_store(q2, (r,), activate(p3, r, mean_s, scale_s, shift_s) + p2[r, :])
+
+    over_rows(count, joined_rows)
+    write("joined", q2, joined_out)
+    weights[3].wait()
+    p2[...] = product2(q2, (), w_trans[...])
+    write("zt", p2, zt_out)
+    add_squares(TRANS, p2, low)
+    exchange(TRANS, half)
+
+    mean_t, scale_t, shift_t = affine(TRANS, g_trans, b_trans, low)
+
+    def trans_rows(r, _):
+        split_store(q3, (r,), activate(p2, r, mean_t, scale_t, shift_t))
+
+    over_rows(count, trans_rows)
+    write("trans", q3, trans_out)
+    weights[4].wait()
+    for page, columns in ((p4, low), (p5, high)):
+        page[...] = product2(q3, (), w_out[low, columns]) + product2(q1, (), w_out[high, columns])
+        add_squares(OUT, page, columns)
+    exchange(OUT, 2 * half)
+
+    total = total_ref[SPLIT, 2:3, 0:1]
+    for k in range(TILES):
+        cot_load(k).wait()
+        compact(cot_ref, wide_ref)
+        if k + 1 < TILES:
+            cot_load(k + 1).start()
+        for page, slope_page, columns in ((p4, p6, low), (p5, p7, high)):
+            mean_o, inverse_o = moments(stats(OUT), total, columns)
+            gain, shift_o = g_out[0:1, columns], b_out[0:1, columns]
+
+            def body(r, carry, k=k, page=page, slope_page=slope_page, columns=columns):
+                q = pl.ds(pl.multiple_of(r.start + k * pitch, CHUNK), CHUNK)
+                mask = mask_ref[q, 0:1]
+                scaled = (page[q, :] - mean_o) * inverse_o
+                y = scaled * gain + shift_o
+                t = jnp.exp(jnp.minimum(y, 30.0))
+                n = t * (t + 2.0)
+                inv = 1.0 / (n + 2.0)
+                ratio = n * inv
+                slope = ratio + y * (((4.0 * t) * (t + 1.0) * inv) * inv)
+                dy = jnp.where(mask > 0.0, wide_ref[r, columns], 0.0) * slope
+                wide_ref[r, columns] = y * ratio * mask
+                slope_page[q, :] = dy
+                return (carry[0] + fold(dy), carry[1] + fold(dy * scaled))
+
+            zero = jnp.zeros((8, half), F32)
+            add_sums(local_ref.at[BACK_OUT], columns, over_rows(pitch, body, (zero, zero)))
+        if k:
+            result_store(k - 1).wait()
+        spread_out(wide_ref, staged_ref)
+        result_store(k).start()
+    exchange(BACK_OUT, 2 * half)
+
+    def settled(page, z_page, pair_ref, which, back, gain_ref, columns, back_columns):
+        mean_k, inverse_k = moments(stats(which), total, columns)
+        factor = gain_ref[0:1, columns] * inverse_k
+        first, second = total_ref[back, 0:1, back_columns] / total, total_ref[back, 1:2, back_columns] / total
+
+        def body(r, _):
+            split_store(pair_ref, (r,), settle(page[r, :], z_page[r, :], mask_ref[r, 0:1], mean_k, inverse_k, factor, first, second))
+
+        over_rows(count, body)
+
+    written("inner")
+    written("joined")
+    settled(p6, p4, q0, OUT, BACK_OUT, g_out, low, low)
+    settled(p7, p5, q2, OUT, BACK_OUT, g_out, high, high)
+    write("dlow", q0, dlow_out)
+    write("dhigh", q2, dhigh_out)
+    result_store(TILES - 1).wait()
+    for name in list(pending):
+        written(name)
+
+
+def front_call(arrays, constants, scalars, slots, side, count, members):
+    hbm, vmem_spec = pl.BlockSpec(memory_space=pl.ANY), pl.BlockSpec(memory_space=pltpu.VMEM)
+    vmem, dma = pltpu.VMEM, pltpu.SemaphoreType.DMA
+    full = arrays[0].shape[2]
+    half = full // 2
+    pitch = count // TILES
+    pair, page = sds((2, count, half), BF16), sds((count, half))
+    outs = [pair, page, page, pair, pair, page, pair, page, pair, page, pair, sds(arrays[1].shape), pair, pair]
+    scratch = [vmem((count, half), F32), vmem((count + 2 * GUARD, half), F32)] + [vmem((count, half), F32)] * 6
+    scratch += [vmem((2, count, half), BF16)] * 4
+    scratch += [
+        vmem((pitch, full), F32), vmem((2, pitch // slots, slots, full), BF16), vmem((pitch // slots, slots, full), F32), vmem((pitch // slots, slots, full), F32),
+        vmem((full, full), BF16), vmem((half, half), BF16), vmem((9, half, half), BF16), vmem((half, half), BF16), vmem((full, full), BF16),
+        vmem((6, 8, full), F32), vmem((6, members, 8, full), F32),
+        dma((5,)), dma((2,)), dma(()), dma(()), dma((16,)), dma((6, members - 1)), dma((6, members - 1)),
+    ]
+    return pl.pallas_call(
+        functools.partial(front_body, side, slots),
+        in_specs=[hbm] * len(arrays) + [vmem_spec] * len(constants) + [pl.BlockSpec(memory_space=pltpu.SMEM)] * 2,
+        out_specs=[hbm] * len(outs) + [vmem_spec] * 2,
+        out_shape=outs + [sds((6, 8, full)), sds((count, 128))],
+        scratch_shapes=scratch,
+        compiler_params=pltpu.CompilerParams(collective_id=1, has_side_effects=True, vmem_limit_bytes=60 * 1024 * 1024),
+    )(*arrays, *constants, *scalars)
+
+
 LAG = 8
 KEPT = 6
 
 
 def reduce_body(jobs, side, slots, *refs):
-    lefts, rights, refs = refs[:6], refs[6:9], refs[9:]
-    (dys_hbm, zs_hbm, zi_hbm, gj_hbm, zm_hbm, ws_hbm), refs = refs[:6], refs[6:]
-    (s_split, s_spread, g_spread, q_spread, s_inner, g_inner, b_inner, g_split, b_split, q_out, q_mid, mask_ref, edge_ref, wi_ref, w_ref), refs = refs[:15], refs[15:]
-    outs, features_hbm, vectors_ref, refs = refs[:5], refs[5], refs[6], refs[7:]
+    lefts, rights, refs = refs[:6], refs[6:8], refs[8:]
+    (zt_hbm, zp_hbm, zs_hbm, zi_hbm, zm_hbm, ws_hbm), refs = refs[:6], refs[6:]
+    (totals_ref, g_split, b_split, g_inner, b_inner, g_spread, b_spread, g_trans, b_trans, mask_ref, edge_ref, wi_ref, wt_ref, wo_ref), refs = refs[:14], refs[14:]
+    outs, dpart_out, dmain_out, vectors_ref, refs = refs[:5], refs[5], refs[6], refs[7], refs[8:]
     (x_ref, z_ref, turned_ref, own_ref, r0_ref, half_ref, r1_ref, quarter_ref, r2_ref, eighth_ref, r3_ref, full_ref, load_sem, store_sem) = refs[:14]
-    (padded_ref, grad_ref, page_ref, tile_ref, zm_ref, pair_ref, part_ref, wide_ref, staged_ref, tap_ref, sums_ref, shared_ref, small_ref, spread_ref) = refs[14:28]
-    (page_sem, tap_sem, part_sem, staged_sem, sum_send, sum_recv, small_send, small_recv) = refs[28:36]
-    sems = refs[36:]
+    (padded_ref, grad_ref, page_ref, joined_ref, zm_ref, pair_ref, part_ref, wide_ref, tap_ref, sums_ref, shared_ref, small_ref, spread_ref) = refs[14:27]
+    (page_sem, tap_sem, write_sem, sum_send, sum_recv, small_send, small_recv) = refs[27:34]
+    sems = refs[34:]
     count, half = grad_ref.shape
-    pitch = tile_ref.shape[1]
+    pitch = wide_ref.shape[0]
     tiles = count // pitch
+    s_split, q_out = totals_ref.at[SPLIT], totals_ref.at[BACK_OUT]
+    s_spread, s_trans, s_inner = (totals_ref.at[k, :, 0:half] for k in (SPREAD, TRANS, INNER))
     stats_total = s_split[2:3, 0:1]
     block = own_ref.shape[1]
     mid = block // 2
@@ -551,13 +867,12 @@
             copy.wait()
 
     def load(j):
-        (left, left_columns, parts), right, _ = jobs[j]
+        (left, begin_part, parts), right, _ = jobs[j]
         slot = j % 2
-        made = [pltpu.make_async_copy(lefts[left].at[0:parts, :, left_columns], x_ref.at[slot, 0:parts], load_sem.at[slot, 0])]
-        if right == "pair":
-            made.append(pltpu.make_async_copy(pair_ref, z_ref.at[slot], load_sem.at[slot, 1]))
-        elif right is not None:
-            made.append(pltpu.make_async_copy(rights[right[0]].at[:, :, right[1]], z_ref.at[slot], load_sem.at[slot, 1]))
+        made = [pltpu.make_async_copy(lefts[left].at[begin_part : begin_part + parts], x_ref.at[slot, 0:parts], load_sem.at[slot, 0])]
+        source = {"pair": pair_ref, "part": part_ref, 0: rights[0], 1: rights[1]}.get(right)
+        if source is not None:
+            made.append(pltpu.make_async_copy(source, z_ref.at[slot], load_sem.at[slot, 1]))
         return made
 
     def store(j):
@@ -574,20 +889,10 @@
         return pltpu.make_async_copy(ws_hbm.at[tap], tap_ref.at[tap % 2], tap_sem.at[tap % 2])
 
     upper = slice(half, 2 * half)
-    load_dy, load_zs = page(dys_hbm, grad_ref, 0), page(zs_hbm, page_ref, 1)
-    load_zi, load_zm = page(zi_hbm, page_ref, 1), page(zm_hbm.at[:, upper], zm_ref, 2)
-
-    def joined_load(k):
-        return pltpu.make_async_copy(gj_hbm.at[k * pitch : (k + 1) * pitch], tile_ref.at[k % 2], part_sem.at[0, k % 2])
-
-    def part_load(k):
-        return pltpu.make_async_copy(rights[2].at[:, k * pitch : (k + 1) * pitch], part_ref.at[k % 2], part_sem.at[1, k % 2])
-
-    places = staged_ref.shape[0]
-
-    def staged_store(k):
-        size = min(places, features_hbm.shape[0] - k * places)
-        return pltpu.make_async_copy(staged_ref.at[0:size], features_hbm.at[k * places : k * places + size], staged_sem)
+    load_zt, load_zp, load_zs = page(zt_hbm, page_ref, 0), page(zp_hbm, joined_ref, 1), page(zs_hbm, page_ref, 0)
+    load_zi, load_zm = page(zi_hbm, page_ref, 0), page(zm_hbm, zm_ref, 2)
+    write_part = pltpu.make_async_copy(part_ref, dpart_out, write_sem.at[0])
+    write_main = pltpu.make_async_copy(z_ref.at[1], dmain_out, write_sem.at[1])
 
     group = [at(z, x, y, 1 - core), at(z, x, 1 - y, core), to_diagonal]
 
@@ -622,22 +927,69 @@
             for k, peer in enumerate(everyone)
         ]
 
+    def settled(dy_ref, z_page, which, back, gain_ref, columns, keep):
+        mean, inverse = moments(which, stats_total, columns)
+        factor = gain_ref[0:1, columns] * inverse
+        first_sum, second_sum = sums_ref[back, 0:1, :] / stats_total, sums_ref[back, 1:2, :] / stats_total
+
+        def body(r, _):
+            keep(r, settle(dy_ref[r, :], z_page[r, :], mask_ref[r, 0:1], mean, inverse, factor, first_sum, second_sum))
+
+        over_rows(count, body)
+
+    def sloped(grad, target_ref, z_page, which, back, gain_ref, shift_ref, columns):
+        mean, inverse = moments(which, stats_total, columns)
+        gain, shift = gain_ref[0:1, columns], shift_ref[0:1, columns]
+
+        def body(r, carry):
+            dy, sums = norm_slope(z_page, grad[r, :], mask_ref, r, everything, mean, inverse, gain, shift)
+            target_ref[r, :] = dy
+            return (carry[0] + sums[0], carry[1] + sums[1])
+
+        zero = jnp.zeros((8, half), F32)
+        add_sums(sums_ref.at[back], everything, over_rows(count, body, (zero, zero)))
+        sum_start(back)
+
+    own, lower = everything, slice(0, half)
+
+    def stacked(step):
+        columns_k = slice(step * half, (step + 1) * half)
+        for target_ref, rows_k in ((grad_ref, lower), (zm_ref, upper)):
+            value = product2_t(z_ref.at[step % 2], (), wo_ref[rows_k, columns_k])
+            if step == 0:
+                target_ref[...] = value
+            else:
+                target_ref[...] += value
+
+    def middle_slopes():
+        load_zt.wait()
+        load_zp.wait()
+        sloped(grad_ref, grad_ref, page_ref, s_trans, 2, g_trans, b_trans, own)
+        sloped(zm_ref, zm_ref, joined_ref, s_split, 3, g_split, b_split, lower)
+
+    def middle():
+        sum_finish(2)
+        sum_finish(3)
+        settled(grad_ref, page_ref, s_trans, 2, g_trans, own, lambda r, dz: split_store(pair_ref, (r,), dz))
+        load_zs.start()
+        settled(zm_ref, joined_ref, s_split, 3, g_split, lower, lambda r, dz: split_store(part_ref, (r,), dz))
+        load_zm.start()
+        write_part.start()
+        joined_ref[...] = product2_t(pair_ref, (), wt_ref[...])
+        load_zs.wait()
+        sloped(joined_ref, grad_ref, page_ref, s_spread, 4, g_spread, b_spread, own)
+
     def prepare():
-        load_dy.wait()
-        load_zs.wait()
+        sum_finish(4)
         padded_ref[0:GUARD, :] = jnp.zeros((GUARD, half), F32)
         padded_ref[GUARD + count :, :] = jnp.zeros((GUARD, half), F32)
-        mean, inverse = moments(s_spread, stats_total, everything)
-        factor = g_spread[...] * inverse
-        first_sum, second_sum = q_spread[0:1, :] / stats_total, q_spread[1:2, :] / stats_total
-
-        def body(r, _):
-            dz = settle(grad_ref[r, :], page_ref[r, :], mask_ref[r, 0:1], mean, inverse, factor, first_sum, second_sum)
+
+        def keep(r, dz):
             padded_ref[pl.ds(r.start + GUARD, CHUNK), :] = dz
 
-        over_rows(count, body)
+        settled(grad_ref, page_ref, s_spread, 4, g_spread, own, keep)
         load_zi.start()
-        load_zm.start()
+        grad_ref[...] = jnp.zeros_like(grad_ref)
 
     def tap_work(tap):
         move, dx = taps(side, slots)[tap]
@@ -657,20 +1009,7 @@
 
     def inner_slope():
         load_zi.wait()
-        joined_load(0).start()
-        joined_load(1).start()
-        mean, inverse = moments(s_inner, stats_total, everything)
-        gain, shift = g_inner[...], b_inner[...]
-
-        def tail(r, carry):
-            dy, sums = norm_slope(page_ref, grad_ref[r, :], mask_ref, r, everything, mean, inverse, gain, shift)
-            grad_ref[r, :] = dy
-            return (carry[0] + sums[0], carry[1] + sums[1])
-
-        zero = jnp.zeros((8, half), F32)
-        sums_ref[...] = jnp.zeros_like(sums_ref)
-        add_sums(sums_ref.at[0], everything, over_rows(count, tail, (zero, zero)))
-        sum_start(0)
+        sloped(grad_ref, grad_ref, page_ref, s_inner, 0, g_inner, b_inner, own)
 
     def shifted(k):
         return lambda r: pl.ds(pl.multiple_of(r.start + k * pitch, CHUNK), CHUNK)
@@ -688,26 +1027,23 @@
 
         over_rows(pitch, body)
         rows_k = slice(k * pitch, (k + 1) * pitch)
-        wide_ref[:, 0:half] = product2_t(pair_ref, (rows_k,), wi_ref[...])
-        joined_load(k).wait()
+        wide_ref[...] = product2_t(pair_ref, (rows_k,), wi_ref[...])
         mean, inverse = moments(s_split, stats_total, upper)
         gain, shift = g_split[0:1, upper], b_split[0:1, upper]
 
         def tail(r, carry):
             q = here(r)
-            dy, sums = norm_slope(zm_ref, wide_ref[r, 0:half] + tile_ref[k % 2, r, :], mask_ref, q, everything, mean, inverse, gain, shift)
+            dy, sums = norm_slope(zm_ref, wide_ref[r, :] + joined_ref[q, :], mask_ref, q, everything, mean, inverse, gain, shift)
             grad_ref[q, :] = dy
             return (carry[0] + sums[0], carry[1] + sums[1])
 
         zero = jnp.zeros((8, half), F32)
         add_sums(sums_ref.at[1], everything, over_rows(pitch, tail, (zero, zero)))
-        if k + 2 < tiles:
-            joined_load(k + 2).start()
 
     def small_start():
         pieces = [
-            (q_mid, slice(half, 2 * half)), (sums_ref.at[1], everything), (sums_ref.at[0], everything), (q_spread, everything),
-            (q_mid, slice(0, half)), (q_out, slice(0, half)), (q_out, slice(half, 2 * half)),
+            (sums_ref.at[3], everything), (sums_ref.at[1], everything), (sums_ref.at[0], everything), (sums_ref.at[4], everything),
+            (sums_ref.at[2], everything), (q_out, slice(0, half)), (q_out, slice(half, 2 * half)),
         ]
         small_ref[...] = jnp.zeros_like(small_ref)
         for k, (ref, columns_k) in enumerate(pieces):
@@ -725,45 +1061,34 @@
             value = value + spread_ref[k]
         vectors_ref[...] = value
 
-    def split_tile(k):
-        mean, inverse = moments(s_split, stats_total, upper)
-        factor = g_split[0:1, upper] * inverse
-        first_sum, second_sum = sums_ref[1, 0:1, :] / stats_total, sums_ref[1, 1:2, :] / stats_total
-        here = shifted(k)
-
-        def body(r, _):
-            q = here(r)
-            dz = settle(grad_ref[q, :], zm_ref[q, :], mask_ref[q, 0:1], mean, inverse, factor, first_sum, second_sum)
-            split_store(pair_ref, (q,), dz)
-
-        over_rows(pitch, body)
-        part_load(k).wait()
-        wide_ref[...] = dot_t(part_ref[k % 2, 0], w_ref[:, 0:half]) + dot_t(part_ref[k % 2, 1], w_ref[:, 0:half])
-        wide_ref[...] += product2_t(pair_ref, (slice(k * pitch, (k + 1) * pitch),), w_ref[:, half:])
-        if k + 2 < tiles:
-            part_load(k + 2).start()
-        if k:
-            staged_store(k - 1).wait()
-        spread_out(wide_ref, staged_ref)
-        staged_store(k).start()
-
-    def first_parts():
-        part_load(0).start()
-        part_load(1).start()
-
+    def main_settle():
+        def keep(r, dz):
+            high = dz.astype(BF16)
+            rest = (dz - high.astype(F32)).astype(BF16)
+            for slot in (0, 1):
+                z_ref[slot, 0, r, :] = high
+                z_ref[slot, 1, r, :] = rest
+
+        settled(grad_ref, zm_ref, s_split, 1, g_split, upper, keep)
+        write_main.start()
+
+    FIRST_TAP = 4
     hosted = {
-        9: [inner_slope],
-        10: [lambda: (load_zm.wait(), sum_finish(0)), functools.partial(inner_tile, 0), functools.partial(inner_tile, 1)],
-        11: [functools.partial(inner_tile, 2), functools.partial(inner_tile, 3), lambda: sum_start(1)],
-        12: [lambda: sum_finish(1), small_start, first_parts],
-        14: [functools.partial(split_tile, 0), functools.partial(split_tile, 1)],
-        15: [functools.partial(split_tile, 2), functools.partial(split_tile, 3)],
-        16: [lambda: staged_store(3).wait()],
-        18: [small_finish],
+        0: [functools.partial(stacked, 0)],
+        1: [functools.partial(stacked, 1), middle_slopes],
+        2: [middle],
+        3: [prepare],
+        13: [inner_slope],
+        14: [load_zm.wait, lambda: sum_finish(0), functools.partial(inner_tile, 0), functools.partial(inner_tile, 1)],
+        15: [functools.partial(inner_tile, 2), functools.partial(inner_tile, 3), lambda: sum_start(1)],
+        16: [lambda: sum_finish(1), small_start],
+        17: [main_settle],
+        18: [small_finish, write_part.wait, write_main.wait],
     }
 
-    load_dy.start()
-    load_zs.start()
+    sums_ref[...] = jnp.zeros_like(sums_ref)
+    load_zt.start()
+    load_zp.start()
     tap_load(0).start()
     for copy in load(0):
         copy.start()
@@ -772,8 +1097,6 @@
     for peer in peers:
         pl.semaphore_signal(barrier, inc=1, device_id=peer, device_id_type=MESH)
     pl.semaphore_wait(barrier, len(peers))
-    prepare()
-    grad_ref[...] = jnp.zeros_like(grad_ref)
     total = len(jobs)
 
     @pl.loop(0, total + LAG + 1)
@@ -807,6 +1130,24 @@
             def _(c, number=number):
                 finish(number, c)
                 begin(number + 1, c)
+
+        for j in range(total):
+
+            @pl.when(t == j)
+            def _(j=j):
+                for copy in load(j):
+                    copy.wait()
+                for task in hosted.get(j, ()):
+                    task()
+                if j + 1 < total:
+                    for copy in load(j + 1):
+                        copy.start()
+                if 0 <= j - FIRST_TAP < 9:
+                    tap_work(j - FIRST_TAP)
+
+        @pl.when(jnp.logical_and(t >= FIRST_TAP, t < FIRST_TAP + 9))
+        def _():
+            tap_gradient(t % 2)
 
         @stage(3, 4)
         def _(c):
@@ -843,24 +1184,6 @@
             half_ref[slot] = own_ref[slot, part(core * (block // 2), block // 2), :] + r0_ref[slot]
             begin(1, c)
 
-        for j in range(total):
-
-            @pl.when(t == j)
-            def _(j=j):
-                for copy in load(j):
-                    copy.wait()
-                for task in hosted.get(j, ()):
-                    task()
-                if j + 1 < total:
-                    for copy in load(j + 1):
-                        copy.start()
-                if j < 9:
-                    tap_work(j)
-
-        @pl.when(t < 9)
-        def _():
-            tap_gradient(t % 2)
-
         exact = functools.reduce(jnp.logical_or, [t == j for j in range(total) if jobs[j][0][2] == 1])
 
         @stage(None, 0)
@@ -877,7 +1200,7 @@
             begin(0, c)
 
 
-def reduce_call(jobs, lefts, rights, hosted, constants, shapes, side, slots, pixel_shape):
+def reduce_call(jobs, lefts, rights, hosted, constants, shapes, side, slots):
     hbm, vmem_spec = pl.BlockSpec(memory_space=pl.ANY), pl.BlockSpec(memory_space=pltpu.VMEM)
     vmem, dma = pltpu.VMEM, pltpu.SemaphoreType.DMA
     count, block = hosted[0].shape
@@ -888,19 +1211,19 @@
         vmem((2, block // 4, block), F32), vmem((2, block // 4, block), F32), vmem((2, block // 8, block), F32), vmem((2, block // 8, block), F32),
         vmem((2, 3, block // 32, block), F32), vmem((KEPT, block, block), F32),
         dma((2, 2)), dma((KEPT,)),
-        vmem((count + 2 * GUARD, block), F32), vmem((count, block), F32), vmem((count, block), F32), vmem((2, pitch, block), F32),
-        vmem((count, block), F32), vmem((2, count, block), BF16), vmem((2, 2, pitch, block), BF16), vmem((pitch, 2 * block), F32),
-        vmem((pitch // slots, slots, 2 * block), F32), vmem((2, block, block), BF16), vmem((2, 8, block), F32), vmem((2, 4, 8, block), F32),
+        vmem((count + 2 * GUARD, block), F32), vmem((count, block), F32), vmem((count, block), F32), vmem((count, block), F32),
+        vmem((count, block), F32), vmem((2, count, block), BF16), vmem((2, count, block), BF16), vmem((pitch, block), F32),
+        vmem((2, block, block), BF16), vmem((5, 8, block), F32), vmem((5, 4, 8, block), F32),
         vmem((16, block), F32), vmem((8, 16, block), F32),
-        dma((3,)), dma((2,)), dma((2, 2)), dma(()), dma((2, 3)), dma((2, 3)), dma((7,)), dma((7,)),
+        dma((3,)), dma((2,)), dma((2,)), dma((5, 3)), dma((5, 3)), dma((7,)), dma((7,)),
     ]
     for width in (1, 2, 2, 3, 6, 2, 2, 1):
         scratch += [dma((width, 2)), dma((width, 2))]
     return pl.pallas_call(
         functools.partial(reduce_body, jobs, side, slots),
         in_specs=[hbm] * (len(lefts) + len(rights) + len(hosted)) + [vmem_spec] * len(constants),
-        out_specs=[hbm] * (len(shapes) + 1) + [vmem_spec],
-        out_shape=[sds(shape) for shape in shapes] + [sds(pixel_shape), sds((16, block))],
+        out_specs=[hbm] * (len(shapes) + 2) + [vmem_spec],
+        out_shape=[sds(shape) for shape in shapes] + [sds((2, count, block), BF16)] * 2 + [sds((16, block))],
         scratch_shapes=scratch,
         compiler_params=pltpu.CompilerParams(collective_id=3, has_side_effects=True, vmem_limit_bytes=60 * 1024 * 1024),
     )(*lefts, *rights, *hosted, *constants)
@@ -957,14 +1280,9 @@
     pitch = round_up(-(-slots * side * side // TILES), 16)
     count = TILES * pitch
     grid = (TILES,)
-    row = jnp.arange(count)
-    slot, place = row % slots, row // slots
-    y, x = place // side, place % side
-    sides = map_sides[slot]
-    keep = (slot < image_counts[0]) & (y < sides) & (x < sides) & (place < side * side)
-    mask = jnp.broadcast_to(keep.astype(F32)[:, None], (count, 128))
-    lane = jnp.arange(128)[None, :]
-    edges = jnp.where(lane == 0, (x > 0)[:, None], jnp.where(lane == 2, (x < side - 1)[:, None], True)).astype(F32)
+    columns = np.arange(count)[:, None] // slots % side
+    lanes = np.arange(128)[None, :]
+    edges = jnp.asarray(np.where(lanes == 0, columns > 0, np.where(lanes == 2, columns < side - 1, True)).astype(np.float32))
     features = features.transpose(1, 2, 0, 3).reshape(side * side, slots, full)
     cotangent = cotangent.transpose(1, 2, 0, 3).reshape(side * side, slots, full)
     (split_gain, split_shift, inner_gain, inner_shift, spread_gain, spread_shift, transition_gain, transition_shift, output_gain, output_shift) = (
@@ -994,95 +1312,114 @@
     def fixed(array):
         return (array, whole(array))
 
-    x0, z_split, s_split = call(
-        split_kernel_body,
-        [(features, pixels(pitch, features.shape)), (mask, r_mask), fixed(split_kernel)],
-        [(sds((count, full), BF16), r_full), (sds((count, full)), r_full), (sds((8, full)), sums_full)],
-        [pltpu.VMEM((pitch, full), F32)],
-    )
-    s_split = group(s_split)
-    part2, main, main2, z_inner, s_inner = call(
-        inner_body,
-        [(z_split, r_full), fixed(s_split), fixed(split_gain), fixed(split_shift), (mask, r_mask), fixed(inner_kernel)],
-        [
-            (sds((2, count, half), BF16), pair_half), (sds((count, half)), r_half), (sds((2, count, half), BF16), pair_half),
-            (sds((count, half)), r_half), (sds((8, half)), sums_half),
-        ],
-    )
-    s_inner = group(s_inner)
-    tap_spec = pl.BlockSpec((1, half, half), lambda i: (i, 0, 0))
-    inner2, z_spread, s_spread = call(
-        functools.partial(spread_body, side, slots),
-        [fixed(z_inner), fixed(s_split), fixed(s_inner), fixed(inner_gain), fixed(inner_shift), fixed(mask), fixed(edges), (spread_weight, tap_spec)],
-        [(sds((2, count, half), BF16), out_whole((2, count, half))), (sds((count, half)), out_whole((count, half))), (sds((8, half)), sums_half)],
-        [pltpu.VMEM((count + 2 * GUARD, half), F32), pltpu.VMEM((2, count, half), BF16)],
-        (9,),
-    )
-    s_spread = group(s_spread)
-    joined2, z_trans, s_trans = call(
-        transition_body,
-        [(z_spread, r_half), fixed(s_split), fixed(s_spread), fixed(spread_gain), fixed(spread_shift), (mask, r_mask), (main, r_half), fixed(transition_kernel)],
-        [(sds((2, count, half), BF16), pair_half), (sds((count, half)), r_half), (sds((8, half)), sums_half)],
-    )
-    s_trans = group(s_trans)
-    trans2, z_out, s_out = call(
-        output_body,
-        [(z_trans, r_half), fixed(s_split), fixed(s_trans), fixed(transition_gain), fixed(transition_shift), (mask, r_mask), (part2, pair_half), fixed(output_kernel)],
-        [(sds((2, count, half), BF16), pair_half), (sds((count, full)), r_full), (sds((8, full)), sums_full)],
-    )
-    s_out = group(s_out)
-    result, dy_out, q_out = call(
-        result_body,
-        [(z_out, r_full), fixed(s_split), fixed(s_out), fixed(output_gain), fixed(output_shift), (mask, r_mask), (cotangent, pixels(pitch, cotangent.shape))],
-        [(sds(cotangent.shape), pixels(pitch, cotangent.shape)), (sds((count, full)), r_full), (sds((8, full)), sums_full)],
-        [pltpu.VMEM((pitch, full), F32)],
-    )
-    q_out = group(q_out)
-    dz_out, dy_trans, dy_part, q_mid = call(
-        output_back_body,
-        [
-            (dy_out, r_full), (z_out, r_full), fixed(s_out), fixed(output_gain), fixed(q_out), fixed(s_split), (mask, r_mask), fixed(output_kernel),
-            (z_trans, r_half), fixed(s_trans), fixed(transition_gain), fixed(transition_shift), (z_split, rows(pitch, half, 0)), fixed(split_gain), fixed(split_shift),
-        ],
-        [(sds((2, count, full), BF16), pair_full), (sds((count, half)), r_half), (sds((count, half)), r_half), (sds((8, full)), sums_full)],
-        [pltpu.VMEM((pitch, full), F32)],
-    )
-    q_mid = group(q_mid)
-    dz_trans, dz_part, grad_joined, dy_spread, q_spread = call(
-        transition_back_body,
-        [
-            (dy_trans, r_half), (dy_part, r_half), (z_trans, r_half), fixed(s_trans), fixed(transition_gain), fixed(q_mid), fixed(s_split), (mask, r_mask), fixed(transition_kernel),
-            (z_split, rows(pitch, half, 0)), fixed(split_gain), (z_spread, r_half), fixed(s_spread), fixed(spread_gain), fixed(spread_shift),
-        ],
-        [
-            (sds((2, count, half), BF16), pair_half), (sds((2, count, half), BF16), pair_half), (sds((count, half)), r_half),
-            (sds((count, half)), r_half), (sds((8, half)), sums_half),
-        ],
-    )
-    q_spread = group(q_spread)
     if shape == (8, 4):
         low, high = slice(0, half), slice(half, full)
         every = slice(None)
-        jobs = [((4, every, 2), None, (2, (tap,))) for tap in range(9)]
-        jobs += [((0, every, 2), (0, low), (4, (low, low))), ((0, every, 2), (0, high), (4, (low, high)))]
-        jobs += [((1, every, 2), (0, low), (4, (high, low))), ((1, every, 2), (0, high), (4, (high, high)))]
-        jobs += [((5, every, 2), "pair", (1, (every, every))), ((2, every, 2), (1, every), (3, (every, every)))]
-        jobs += [((3, low, 1), (2, every), (0, (low, low))), ((3, high, 1), (2, every), (0, (high, low)))]
-        jobs += [((3, low, 1), "pair", (0, (low, high))), ((3, high, 1), "pair", (0, (high, high)))]
-        grad_split, grad_inner, grad_spread, grad_transition, grad_output, grad_features, vectors = reduce_call(
+        (x0, z_part, z_main, main2, part2, z_inner, inner2, z_spread, joined2, z_trans, trans2, result, dz_low, dz_high, totals, mask) = front_call(
+            [features, cotangent, split_kernel, inner_kernel, spread_weight, transition_kernel, output_kernel],
+            [split_gain, split_shift, inner_gain, inner_shift, spread_gain, spread_shift, transition_gain, transition_shift, output_gain, output_shift, edges],
+            [image_counts, map_sides],
+            slots, side, count, shape[1],
+        )
+        jobs = [((0, 0, 2), 0, (4, (low, low))), ((0, 0, 2), 1, (4, (low, high)))]
+        jobs += [((1, 0, 2), 0, (4, (high, low))), ((1, 0, 2), 1, (4, (high, high)))]
+        jobs += [((4, 0, 2), None, (2, (tap,))) for tap in range(9)]
+        jobs += [((2, 0, 2), "pair", (3, (every, every)))]
+        jobs += [((3, 0, 1), "part", (0, (low, low))), ((3, 1, 1), "part", (0, (high, low)))]
+        jobs += [((5, 0, 2), "pair", (1, (every, every)))]
+        jobs += [((3, 0, 1), None, (0, (low, high))), ((3, 1, 1), None, (0, (high, high)))]
+        grad_split, grad_inner, grad_spread, grad_transition, grad_output, dz_part, dz_main, vectors = reduce_call(
             jobs,
-            [trans2, part2, joined2, x0[None], inner2, main2],
-            [dz_out, dz_trans, dz_part],
-            [dy_spread, z_spread, z_inner, grad_joined, z_split, spread_weight],
+            [trans2, part2, joined2, x0, inner2, main2],
+            [dz_low, dz_high],
+            [z_trans, z_part, z_spread, z_inner, z_main, spread_weight],
             [
-                s_split, s_spread, spread_gain, q_spread, s_inner, inner_gain, inner_shift, split_gain, split_shift, q_out, q_mid,
-                mask, edges, inner_kernel, split_kernel,
+                totals, split_gain, split_shift, inner_gain, inner_shift, spread_gain, spread_shift, transition_gain, transition_shift,
+                mask, edges, inner_kernel, transition_kernel, output_kernel,
             ],
             [(full, full), (half, half), (9, half, half), (half, half), (full, full)],
-            side, slots, cotangent.shape,
+            side, slots,
+        )
+        (grad_features,) = call(
+            features_body,
+            [(dz_part, pair_half), (dz_main, pair_half), fixed(split_kernel)],
+            [(sds(cotangent.shape), pixels(pitch, cotangent.shape))],
+            [pltpu.VMEM((pitch, full), F32)],
         )
         small = vectors.reshape(2, 8 * half)
     else:
+        row = jnp.arange(count)[:, None] + jnp.zeros((1, 128), jnp.int32)
+        slot, place = row % slots, row // slots
+        y, x = place // side, place % side
+        sides = sum(jnp.where(slot == k, map_sides[k], 0) for k in range(slots))
+        keep = (slot < image_counts[0]) & (y < sides) & (x < sides) & (place < side * side)
+        mask = keep.astype(F32)
+        x0, z_split, s_split = call(
+            split_kernel_body,
+            [(features, pixels(pitch, features.shape)), (mask, r_mask), fixed(split_kernel)],
+            [(sds((count, full), BF16), r_full), (sds((count, full)), r_full), (sds((8, full)), sums_full)],
+            [pltpu.VMEM((pitch, full), F32)],
+        )
+        s_split = group(s_split)
+        part2, main, main2, z_inner, s_inner = call(
+            inner_body,
+            [(z_split, r_full), fixed(s_split), fixed(split_gain), fixed(split_shift), (mask, r_mask), fixed(inner_kernel)],
+            [
+                (sds((2, count, half), BF16), pair_half), (sds((count, half)), r_half), (sds((2, count, half), BF16), pair_half),
+                (sds((count, half)), r_half), (sds((8, half)), sums_half),
+            ],
+        )
+        s_inner = group(s_inner)
+        tap_spec = pl.BlockSpec((1, half, half), lambda i: (i, 0, 0))
+        inner2, z_spread, s_spread = call(
+            functools.partial(spread_body, side, slots),
+            [fixed(z_inner), fixed(s_split), fixed(s_inner), fixed(inner_gain), fixed(inner_shift), fixed(mask), fixed(edges), (spread_weight, tap_spec)],
+            [(sds((2, count, half), BF16), out_whole((2, count, half))), (sds((count, half)), out_whole((count, half))), (sds((8, half)), sums_half)],
+            [pltpu.VMEM((count + 2 * GUARD, half), F32), pltpu.VMEM((2, count, half), BF16)],
+            (9,),
+        )
+        s_spread = group(s_spread)
+        joined2, z_trans, s_trans = call(
+            transition_body,
+            [(z_spread, r_half), fixed(s_split), fixed(s_spread), fixed(spread_gain), fixed(spread_shift), (mask, r_mask), (main, r_half), fixed(transition_kernel)],
+            [(sds((2, count, half), BF16), pair_half), (sds((count, half)), r_half), (sds((8, half)), sums_half)],
+        )
+        s_trans = group(s_trans)
+        trans2, z_out, s_out = call(
+            output_body,
+            [(z_trans, r_half), fixed(s_split), fixed(s_trans), fixed(transition_gain), fixed(transition_shift), (mask, r_mask), (part2, pair_half), fixed(output_kernel)],
+            [(sds((2, count, half), BF16), pair_half), (sds((count, full)), r_full), (sds((8, full)), sums_full)],
+        )
+        s_out = group(s_out)
+        result, dy_out, q_out = call(
+            result_body,
+            [(z_out, r_full), fixed(s_split), fixed(s_out), fixed(output_gain), fixed(output_shift), (mask, r_mask), (cotangent, pixels(pitch, cotangent.shape))],
+            [(sds(cotangent.shape), pixels(pitch, cotangent.shape)), (sds((count, full)), r_full), (sds((8, full)), sums_full)],
+            [pltpu.VMEM((pitch, full), F32)],
+        )
+        q_out = group(q_out)
+        dz_out, dy_trans, dy_part, q_mid = call(
+            output_back_body,
+            [
+                (dy_out, r_full), (z_out, r_full), fixed(s_out), fixed(output_gain), fixed(q_out), fixed(s_split), (mask, r_mask), fixed(output_kernel),
+                (z_trans, r_half), fixed(s_trans), fixed(transition_gain), fixed(transition_shift), (z_split, rows(pitch, half, 0)), fixed(split_gain), fixed(split_shift),
+            ],
+            [(sds((2, count, full), BF16), pair_full), (sds((count, half)), r_half), (sds((count, half)), r_half), (sds((8, full)), sums_full)],
+            [pltpu.VMEM((pitch, full), F32)],
+        )
+        q_mid = group(q_mid)
+        dz_trans, dz_part, grad_joined, dy_spread, q_spread = call(
+            transition_back_body,
+            [
+                (dy_trans, r_half), (dy_part, r_half), (z_trans, r_half), fixed(s_trans), fixed(transition_gain), fixed(q_mid), fixed(s_split), (mask, r_mask), fixed(transition_kernel),
+                (z_split, rows(pitch, half, 0)), fixed(split_gain), (z_spread, r_half), fixed(s_spread), fixed(spread_gain), fixed(spread_shift),
+            ],
+            [
+                (sds((2, count, half), BF16), pair_half), (sds((2, count, half), BF16), pair_half), (sds((count, half)), r_half),
+                (sds((count, half)), r_half), (sds((8, half)), sums_half),
+            ],
+        )
+        q_spread = group(q_spread)
         moved_spec = pl.BlockSpec((1, 2, count, half), lambda i: (i, 0, 0, 0))
         moved, dy_inner, q_inner = call(
             functools.partial(spread_back_body, side, slots),

time: 437 us -> 344 us (0.79); the launches traced: 436 us -> 339 us
  Pallas kernels: 405 us -> 315 us
  other arithmetic: 4.38 us -> 0.01 us
    pallas_call x8 -> x1, Pallas kernels: 150 us -> 10.7 us  [call(): pl.pallas_call(body, grid=steps, in_specs=[spec for _, spec in ins], out_...]
    pallas_call x8 -> x1, Pallas kernels: 43.8 us -> 86.4 us  [front_call(): pl.pallas_call(functools.partial(front_body, side, slots), in_specs=[hbm]...]
    pallas_call x1, Pallas kernels: 212 us -> 218 us  [reduce_call(): pl.pallas_call(functools.partial(reduce_body, jobs, side, slots), in_spec...]
    unnamed x18 -> x20, local copies, waits for them, and re-layouts: 21.1 us -> 21.1 us
where the time goes in v4:
time: 344 us; the launch traced here: 339 us
  Pallas kernels  315 us (92%)
  local copies, waits for them, and re-layouts  22.3 us (6%)
    pallas_call x1, Pallas kernels, reduce_call(): pl.pallas_call(functools.partial(reduce_body, jobs, side, slots), in_spec...  218 us
    pallas_call x1, Pallas kernels, front_call(): pl.pallas_call(functools.partial(front_body, side, slots), in_specs=[hbm]...  86.4 us
    unnamed x20, local copies, waits for them, and re-layouts  21.1 us
    pallas_call x1, Pallas kernels, call(): pl.pallas_call(body, grid=steps, in_specs=[spec for _, spec in ins], out_...  10.7 us

profile of v4, /device:TPU:0, one launch (start us, length us, event | category | flops | bytes accessed | tf_op | source)
XLA Modules:
  0.0 339.0 jit_solution(5069314942967747124)
XLA Ops:
  1.3 86.4 %shard_map.323 = (bf16[2,1472,512]{2,1,0:T(8,128)(2,1)}, f32[1472,512]{1,0:T(8,128)}, f32[1472,512]{1,0:T(8,128)}, bf16[2,1472,512]{2,1,0:T(8,128)(2,1)}, bf16[2...) custom-call(bf16[361,4,1024]{2,1,0:T(4,128)(2,1)} %bitcast.42, ...), custom_call_target="tpu_custom_call" | custom-call | tf_op jit(solution)/shard_map/pallas_call | solution.py:768
  87.7 218.1 %shard_map.324 = (f32[1024,1024]{1,0:T(8,128)}, f32[512,512]{1,0:T(8,128)}, f32[9,512,512]{2,1,0:T(8,128)}, f32[512,512]{1,0:T(8,128)}, f32[1024,1024]{1,0:T(8,1...) custom-call(bf16[2,1472,512]{2,1,0:T(8,128)(2,1)} %get-tuple-element.42.refs_0_, ...), custom_call_target="tpu_custom_call" | custom-call | tf_op jit(solution)/shard_map/pallas_call | solution.py:1222
  305.7 0.0 copy-start.3
  305.8 10.7 %shard_map.325 = f32[361,4,1024]{2,1,0:T(4,128)} custom-call(bf16[2,1472,512]{2,1,0:T(8,128)(2,1)} %get-tuple-element.57.dzp_ref, bf16[2,1472,512]{2,1,0:T(8,128)(2,1)} %get-tuple-element.58.dzm_ref, bf16[1024,1024]{1,0:T(8,128)(2,1)} %w_ref.1), custom_call_target="tpu_custom_call" | custom-call | tf_op jit(solution)/shard_map/pallas_call | solution.py:1302
  316.4 0.0 copy-done.3
  316.5 0.6 fusion.1
  317.1 0.6 fusion
  317.7 0.0 slice-start
  317.7 0.0 slice-start.1
  317.7 6.9 %copy.44 = f32[4,19,19,1024]{3,0,2,1:T(4,128)} copy(f32[4,19,19,1024]{3,0,2,1:T(4,128)} %bitcast.41) | data formatting | bytes 11829248
  324.6 0.0 copy-start.2
  324.6 4.9 %copy.45 = f32[1024,1024]{1,0:T(8,128)} copy(f32[1024,1024]{1,0:T(8,128)} %get-tuple-element.94) | data formatting | bytes 8388608
  329.5 0.0 copy-done.2
  329.5 1.0 copy.46
  330.5 0.0 slice-done
  330.5 0.0 slice-done.1
  330.5 0.0 slice-done.2
  330.5 0.0 copy-start.1
  330.5 0.0 copy-start
  330.5 4.8 %copy.47 = f32[3,3,512,512]{3,2,1,0:T(8,128)} copy(f32[3,3,512,512]{3,2,1,0:T(8,128)S(1)} %bitcast.38) | data formatting | bytes 18874368
  335.3 0.0 copy-done.1
  335.3 1.0 copy.48
  336.3 0.5 copy-done
  336.8 2.0 copy.49
  (3 shorter events, 0.0 us)
Async XLA Ops:
  305.7 10.7 %copy-start.3 = (f32[16,512]{1,0:T(8,128)S(1)}, f32[16,512]{1,0:T(8,128)}, u32[]{:S(2)}) copy-start(f32[16,512]{1,0:T(8,128)} %get-tuple-element.60) | copy-start | bytes 98308
  317.7 12.8 %slice-start = ((s8[9437184]{0:T(1024)(128)(4,1)}), s8[4194304]{0:T(1024)(128)(4,1)S(1)}, s32[]{:S(2)}) async-start(s8[9437184]{0:T(1024)(128)(4,1)} %bitcast.36), calls=%async_computation | async-start | bytes 8388608
  317.7 12.8 %slice-start.1 = ((s8[9437184]{0:T(1024)(128)(4,1)}), s8[4194304]{0:T(1024)(128)(4,1)S(1)}, s32[]{:S(2)}) async-start(s8[9437184]{0:T(1024)(128)(4,1)} %bitcast.36), calls=%async_computation.1 | async-start | bytes 8388608
  324.6 4.9 %copy-start.2 = (f32[512,512]{1,0:T(8,128)S(1)}, f32[512,512]{1,0:T(8,128)}, u32[]{:S(2)}) copy-start(f32[512,512]{1,0:T(8,128)} %get-tuple-element.97) | copy-start | bytes 3145732
  324.6 5.9 %slice-start.2 = ((s8[9437184]{0:T(1024)(128)(4,1)}), s8[1048576]{0:T(1024)(128)(4,1)S(1)}, s32[]{:S(2)}) async-start(s8[9437184]{0:T(1024)(128)(4,1)} %bitcast.36), calls=%async_computation.2 | async-start | bytes 2097152
  330.5 4.8 %copy-start.1 = (f32[512,512]{1,0:T(8,128)S(1)}, f32[512,512]{1,0:T(8,128)}, u32[]{:S(2)}) copy-start(f32[512,512]{1,0:T(8,128)} %get-tuple-element.103) | copy-start | bytes 3145732
  330.5 6.3 %copy-start = (f32[1024,1024]{1,0:T(8,128)S(1)}, f32[1024,1024]{1,0:T(8,128)}, u32[]{:S(2)}) copy-start(f32[1024,1024]{1,0:T(8,128)} %get-tuple-element.106) | copy-start | bytes 12582916

commit v5 on v4

--- a/solution.py
+++ b/solution.py
@@ -441,11 +441,90 @@
     spread_out(scratch_ref, grad_ref)
 
 
-def features_body(dzp_ref, dzm_ref, w_ref, grad_ref, scratch_ref):
+def final_body(pieces, *refs):
+    count = len(pieces)
+    sources, dzp_hbm, dzm_hbm, w_hbm, refs = refs[:count], refs[count], refs[count + 1], refs[count + 2], refs[count + 3 :]
+    targets, grad_hbm, refs = refs[:count], refs[count], refs[count + 1 :]
+    buffers, (dzp_ref, dzm_ref, w_ref, wide_ref, staged_ref, load_sem, store_sem, own_sem, grad_sem) = refs[:count], refs[count:]
     half = dzp_ref.shape[2]
-    scratch_ref[...] = product2_t(dzp_ref, (), w_ref[:, :half])
-    scratch_ref[...] += product2_t(dzm_ref, (), w_ref[:, half:])
-    spread_out(scratch_ref, grad_ref)
+    pitch = wide_ref.shape[0]
+    places = staged_ref.shape[1]
+    tiles = dzp_ref.shape[1] // pitch
+    own = [pltpu.make_async_copy(w_hbm, w_ref, own_sem.at[0])]
+    for k in range(tiles):
+        rows_k = slice(k * pitch, (k + 1) * pitch)
+        own.append(pltpu.make_async_copy(dzp_hbm.at[:, rows_k], dzp_ref.at[:, rows_k], own_sem.at[1 + 2 * k]))
+        own.append(pltpu.make_async_copy(dzm_hbm.at[:, rows_k], dzm_ref.at[:, rows_k], own_sem.at[2 + 2 * k]))
+    loads, stores = [], []
+    for source, buffer, target, cuts in zip(sources, buffers, targets, pieces):
+        for begin, end in cuts:
+            k = len(loads)
+            loads.append(pltpu.make_async_copy(source.at[begin:end], buffer.at[begin:end], load_sem.at[k]))
+            stores.append(pltpu.make_async_copy(buffer.at[begin:end], target.at[begin:end], store_sem.at[k]))
+    for copy in own[:3]:
+        copy.start()
+    ahead = len(loads) // 2
+    for copy in loads[:ahead]:
+        copy.start()
+    for copy in own[3:]:
+        copy.start()
+    for copy in loads[ahead:]:
+        copy.start()
+
+    def forward(begin, end):
+        for k in range(begin, end):
+            loads[k].wait()
+            stores[k].start()
+
+    def grad_store(k):
+        size = min(places, grad_hbm.shape[0] - k * places)
+        return pltpu.make_async_copy(staged_ref.at[k % 2, 0:size], grad_hbm.at[k * places : k * places + size], grad_sem.at[k % 2])
+
+    own[0].wait()
+    step = -(-len(loads) // (tiles + 1))
+    for k in range(tiles):
+        own[1 + 2 * k].wait()
+        own[2 + 2 * k].wait()
+        rows_k = slice(k * pitch, (k + 1) * pitch)
+        wide_ref[...] = product2_t(dzp_ref, (rows_k,), w_ref[:, :half]) + product2_t(dzm_ref, (rows_k,), w_ref[:, half:])
+        if k >= 2:
+            grad_store(k - 2).wait()
+        spread_out(wide_ref, staged_ref.at[k % 2])
+        grad_store(k).start()
+        forward(min(k * step, len(loads)), min((k + 1) * step, len(loads)))
+    forward(min(tiles * step, len(loads)), len(loads))
+    for k in range(max(0, tiles - 2), tiles):
+        grad_store(k).wait()
+    for copy in stores:
+        copy.wait()
+
+
+def final_call(arrays, dzp, dzm, weight, slots):
+    hbm = pl.BlockSpec(memory_space=pl.ANY)
+    vmem, dma = pltpu.VMEM, pltpu.SemaphoreType.DMA
+    full, count = weight.shape[0], dzp.shape[1]
+    pitch = count // TILES
+    pieces = []
+    for array in arrays:
+        length = array.shape[0]
+        row_bytes = 4 * array.size // length
+        step = min(length, max(1, (1 << 20) // row_bytes))
+        pieces.append([(begin, min(begin + step, length)) for begin in range(0, length, step)])
+    number = sum(len(cuts) for cuts in pieces)
+    pixel_shape = arrays[0].shape
+    scratch = [vmem(array.shape, F32) for array in arrays]
+    scratch += [
+        vmem(dzp.shape, BF16), vmem(dzm.shape, BF16), vmem(weight.shape, BF16), vmem((pitch, full), F32), vmem((2, pitch // slots, slots, full), F32),
+        dma((number,)), dma((number,)), dma((1 + 2 * TILES,)), dma((2,)),
+    ]
+    return pl.pallas_call(
+        functools.partial(final_body, pieces),
+        in_specs=[hbm] * (len(arrays) + 3),
+        out_specs=[hbm] * (len(arrays) + 1),
+        out_shape=[sds(array.shape) for array in arrays] + [sds(pixel_shape)],
+        scratch_shapes=scratch,
+        compiler_params=params(60),
+    )(*arrays, dzp, dzm, weight)
 
 
 def weight_body(x_ref, dz_ref, dw_ref):
@@ -477,7 +556,7 @@
     (g_split, b_split, g_inner, b_inner, g_spread, b_spread, g_trans, b_trans, g_out, b_out, edge_ref, counts_ref, sides_ref), refs = refs[:13], refs[13:]
     (x_out, zp_out, zm_out, main_out, part_out, zi_out, inner_out, zs_out, joined_out, zt_out, trans_out, result_hbm, dlow_out, dhigh_out, total_ref, mask_ref), refs = refs[:16], refs[16:]
     (p0, p1, p2, p3, p4, p5, p6, p7, q0, q1, q2, q3, wide_ref, feature_ref, cot_ref, staged_ref), refs = refs[:16], refs[16:]
-    (w_split, w_inner, w_spread, w_trans, w_out, local_ref, shared_ref), refs = refs[:7], refs[7:]
+    (w_split, w_inner, w_spread, w_trans, w_out, local_ref, packed_ref, shared_ref), refs = refs[:8], refs[8:]
     weight_sem, feature_sem, cot_sem, staged_sem, out_sem, sum_send, sum_recv = refs
     count, half = p0.shape
     pitch = count // TILES
@@ -521,28 +600,39 @@
             pending[name][0].wait()
             pending[name][1] = False
 
-    def sum_copies(which, width):
-        return [
+    def sum_copies(which):
+        wide = slice(0, 384 if which == SPLIT else 256)
+        return wide, [
             pltpu.make_async_remote_copy(
-                src_ref=local_ref.at[which, :, 0:width], dst_ref=shared_ref.at[which, bn, :, 0:width],
+                src_ref=packed_ref.at[which, :, wide], dst_ref=shared_ref.at[which, bn, :, wide],
                 send_sem=sum_send.at[which, k], recv_sem=sum_recv.at[which, k], device_id={"bn": peer}, device_id_type=MESH,
             )
             for k, peer in enumerate(group)
         ]
 
     def exchange(which, width, beside=None):
-        copies = sum_copies(which, width)
+        wide, copies = sum_copies(which)
+        pieces = [(j, slice(j * 128, (j + 1) * 128)) for j in range(width // 128)]
+        for j, piece in pieces:
+            packed_ref[which, j : j + 1, 0:128] = local_ref[which, 0:1, piece]
+            packed_ref[which, j : j + 1, 128:256] = local_ref[which, 1:2, piece]
+        if which == SPLIT:
+            packed_ref[which, 0:1, 256:384] = local_ref[which, 2:3, 0:128]
         for copy in copies:
             copy.start()
-        shared_ref[which, bn, :, 0:width] = local_ref[which, :, 0:width]
+        shared_ref[which, bn, :, wide] = packed_ref[which, :, wide]
         if beside is not None:
             beside()
         for copy in copies:
             copy.wait()
-        value = shared_ref[which, 0, :, 0:width]
+        value = shared_ref[which, 0, :, wide]
         for k in range(1, members):
-            value = value + shared_ref[which, k, :, 0:width]
-        total_ref[which, :, 0:width] = value
+            value = value + shared_ref[which, k, :, wide]
+        for j, piece in pieces:
+            total_ref[which, 0:1, piece] = value[j : j + 1, 0:128]
+            total_ref[which, 1:2, piece] = value[j : j + 1, 128:256]
+        if which == SPLIT:
+            total_ref[which, 2:3, 0:128] = value[0:1, 256:384]
 
     def stats(which):
         return total_ref.at[which]
@@ -562,6 +652,8 @@
     for peer in group:
         pl.semaphore_signal(barrier, inc=1, device_id={"bn": peer}, device_id_type=MESH)
     local_ref[...] = jnp.zeros_like(local_ref)
+    packed_ref[...] = jnp.zeros_like(packed_ref)
+    total_ref[...] = jnp.zeros_like(total_ref)
     limits = [jnp.where(k < counts_ref[0], sides_ref[k], 0).astype(F32) for k in range(slots)]
 
     def mask_rows(r, _):
@@ -762,7 +854,7 @@
     scratch += [
         vmem((pitch, full), F32), vmem((2, pitch // slots, slots, full), BF16), vmem((pitch // slots, slots, full), F32), vmem((pitch // slots, slots, full), F32),
         vmem((full, full), BF16), vmem((half, half), BF16), vmem((9, half, half), BF16), vmem((half, half), BF16), vmem((full, full), BF16),
-        vmem((6, 8, full), F32), vmem((6, members, 8, full), F32),
+        vmem((6, 8, full), F32), vmem((6, 8, 384), F32), vmem((6, members, 8, 384), F32),
         dma((5,)), dma((2,)), dma(()), dma(()), dma((16,)), dma((6, members - 1)), dma((6, members - 1)),
     ]
     return pl.pallas_call(
@@ -867,6 +959,8 @@
             copy.wait()
 
     def load(j):
+        if jobs[j] is None:
+            return []
         (left, begin_part, parts), right, _ = jobs[j]
         slot = j % 2
         made = [pltpu.make_async_copy(lefts[left].at[begin_part : begin_part + parts], x_ref.at[slot, 0:parts], load_sem.at[slot, 0])]
@@ -1072,18 +1166,18 @@
         settled(grad_ref, zm_ref, s_split, 1, g_split, upper, keep)
         write_main.start()
 
-    FIRST_TAP = 4
+    FIRST_TAP = 6
     hosted = {
-        0: [functools.partial(stacked, 0)],
-        1: [functools.partial(stacked, 1), middle_slopes],
-        2: [middle],
-        3: [prepare],
-        13: [inner_slope],
-        14: [load_zm.wait, lambda: sum_finish(0), functools.partial(inner_tile, 0), functools.partial(inner_tile, 1)],
-        15: [functools.partial(inner_tile, 2), functools.partial(inner_tile, 3), lambda: sum_start(1)],
-        16: [lambda: sum_finish(1), small_start],
-        17: [main_settle],
-        18: [small_finish, write_part.wait, write_main.wait],
+        2: [functools.partial(stacked, 0)],
+        3: [functools.partial(stacked, 1), middle_slopes],
+        4: [middle],
+        5: [prepare],
+        15: [inner_slope],
+        16: [load_zm.wait, lambda: sum_finish(0), functools.partial(inner_tile, 0), functools.partial(inner_tile, 1)],
+        17: [functools.partial(inner_tile, 2), functools.partial(inner_tile, 3), lambda: sum_start(1)],
+        18: [lambda: sum_finish(1), small_start],
+        19: [main_settle],
+        20: [small_finish, write_part.wait, write_main.wait],
     }
 
     sums_ref[...] = jnp.zeros_like(sums_ref)
@@ -1098,10 +1192,12 @@
         pl.semaphore_signal(barrier, inc=1, device_id=peer, device_id_type=MESH)
     pl.semaphore_wait(barrier, len(peers))
     total = len(jobs)
+    taken = [j for j in range(total) if jobs[j] is not None]
+    empty = [j for j in range(total) if jobs[j] is None]
 
     @pl.loop(0, total + LAG + 1)
     def _(t):
-        for j in range(total):
+        for j in taken:
 
             @pl.when(t == j + LAG + 1)
             def _(j=j):
@@ -1110,7 +1206,10 @@
         def stage(number, lag):
             def wrap(body):
                 c = t - lag
-                pl.when(jnp.logical_and(c >= 0, c < total))(lambda: body(c))
+                valid = jnp.logical_and(c >= 0, c < total)
+                if empty:
+                    valid = jnp.logical_and(valid, jnp.logical_or(c < empty[0], c > empty[-1]))
+                pl.when(valid)(lambda: body(c))
 
             return wrap
 
@@ -1118,7 +1217,7 @@
         def _(c):
             finish(7, c)
 
-        for j in range(total):
+        for j in taken:
 
             @pl.when(t == j + LAG)
             def _(j=j):
@@ -1184,7 +1283,7 @@
             half_ref[slot] = own_ref[slot, part(core * (block // 2), block // 2), :] + r0_ref[slot]
             begin(1, c)
 
-        exact = functools.reduce(jnp.logical_or, [t == j for j in range(total) if jobs[j][0][2] == 1])
+        exact = functools.reduce(jnp.logical_or, [t == j for j in taken if jobs[j][0][2] == 1])
 
         @stage(None, 0)
         def _(c):
@@ -1323,6 +1422,7 @@
         )
         jobs = [((0, 0, 2), 0, (4, (low, low))), ((0, 0, 2), 1, (4, (low, high)))]
         jobs += [((1, 0, 2), 0, (4, (high, low))), ((1, 0, 2), 1, (4, (high, high)))]
+        jobs += [None, None]
         jobs += [((4, 0, 2), None, (2, (tap,))) for tap in range(9)]
         jobs += [((2, 0, 2), "pair", (3, (every, every)))]
         jobs += [((3, 0, 1), "part", (0, (low, low))), ((3, 1, 1), "part", (0, (high, low)))]
@@ -1340,11 +1440,8 @@
             [(full, full), (half, half), (9, half, half), (half, half), (full, full)],
             side, slots,
         )
-        (grad_features,) = call(
-            features_body,
-            [(dz_part, pair_half), (dz_main, pair_half), fixed(split_kernel)],
-            [(sds(cotangent.shape), pixels(pitch, cotangent.shape))],
-            [pltpu.VMEM((pitch, full), F32)],
+        result, grad_split, grad_inner, grad_spread, grad_transition, grad_output, grad_features = final_call(
+            [result, grad_split, grad_inner, grad_spread, grad_transition, grad_output], dz_part, dz_main, split_kernel, slots
         )
         small = vectors.reshape(2, 8 * half)
     else:

time: 344 us -> 333 us (0.968)
  local copies, waits for them, and re-layouts: 22.3 us -> 1.25 us
  Pallas kernels: 315 us -> 326 us
    unnamed x20 -> x2, local copies, waits for them, and re-layouts: 21.1 us -> 0.01 us
    pallas_call x1, Pallas kernels: 10.7 us -> 20.1 us  [final_call(): pl.pallas_call(functools.partial(final_body, pieces), in_specs=[hbm] * (l...]
where the time goes in v5:
time: 333 us; the launch traced here: 329 us
  Pallas kernels  326 us (98%)
    pallas_call x1, Pallas kernels, reduce_call(): pl.pallas_call(functools.partial(reduce_body, jobs, side, slots), in_spec...  221 us
    pallas_call x1, Pallas kernels, front_call(): pl.pallas_call(functools.partial(front_body, side, slots), in_specs=[hbm]...  85.2 us
    pallas_call x1, Pallas kernels, final_call(): pl.pallas_call(functools.partial(final_body, pieces), in_specs=[hbm] * (l...  20.1 us

profile of v5, /device:TPU:0, one launch (start us, length us, event | category | flops | bytes accessed | tf_op | source)
XLA Modules:
  0.0 328.8 jit_solution(14530627367181806170)
XLA Ops:
  1.3 85.2 %shard_map.323 = (bf16[2,1472,512]{2,1,0:T(8,128)(2,1)}, f32[1472,512]{1,0:T(8,128)}, f32[1472,512]{1,0:T(8,128)}, bf16[2,1472,512]{2,1,0:T(8,128)(2,1)}, bf16[2...) custom-call(bf16[361,4,1024]{2,1,0:T(4,128)(2,1)} %bitcast.37, ...), custom_call_target="tpu_custom_call" | custom-call | tf_op jit(solution)/shard_map/pallas_call | solution.py:860
  86.5 220.7 %shard_map.324 = (f32[1024,1024]{1,0:T(8,128)}, f32[512,512]{1,0:T(8,128)}, f32[9,512,512]{2,1,0:T(8,128)}, f32[512,512]{1,0:T(8,128)}, f32[1024,1024]{1,0:T(8,1...) custom-call(bf16[2,1472,512]{2,1,0:T(8,128)(2,1)} %get-tuple-element.49.refs_0_, ...), custom_call_target="tpu_custom_call" | custom-call | tf_op jit(solution)/shard_map/pallas_call | solution.py:1321
  307.2 0.0 copy-start
  307.2 20.1 %shard_map.325 = (f32[361,4,1024]{2,1,0:T(4,128)}, f32[1024,1024]{1,0:T(8,128)}, f32[512,512]{1,0:T(8,128)}, f32[9,512,512]{2,1,0:T(8,128)}, f32[512,512]{1,0:T(...) custom-call(f32[361,4,1024]{2,1,0:T(4,128)} %get-tuple-element.48.refs_0_, ...), custom_call_target="tpu_custom_call" | custom-call | tf_op jit(solution)/shard_map/pallas_call | solution.py:520
  327.3 0.0 copy-done
  327.3 0.6 fusion.1
  327.9 0.6 fusion
  (1 shorter events, 0.0 us)
Async XLA Ops:
  307.2 20.1 %copy-start = (f32[16,512]{1,0:T(8,128)S(1)}, f32[16,512]{1,0:T(8,128)}, u32[]{:S(2)}) copy-start(f32[16,512]{1,0:T(8,128)} %get-tuple-element.74) | copy-start | bytes 98308

commit v6 on v5

--- a/solution.py
+++ b/solution.py
@@ -867,7 +867,8 @@
     )(*arrays, *constants, *scalars)
 
 
-LAG = 8
+LAGS = (1, 2, 3, 4, 5, 6, 7, 8)
+LAG = LAGS[-1]
 KEPT = 6
 
 
@@ -876,10 +877,10 @@
     (zt_hbm, zp_hbm, zs_hbm, zi_hbm, zm_hbm, ws_hbm), refs = refs[:6], refs[6:]
     (totals_ref, g_split, b_split, g_inner, b_inner, g_spread, b_spread, g_trans, b_trans, mask_ref, edge_ref, wi_ref, wt_ref, wo_ref), refs = refs[:14], refs[14:]
     outs, dpart_out, dmain_out, vectors_ref, refs = refs[:5], refs[5], refs[6], refs[7], refs[8:]
-    (x_ref, z_ref, turned_ref, own_ref, r0_ref, half_ref, r1_ref, quarter_ref, r2_ref, eighth_ref, r3_ref, full_ref, load_sem, store_sem) = refs[:14]
-    (padded_ref, grad_ref, page_ref, joined_ref, zm_ref, pair_ref, part_ref, wide_ref, tap_ref, sums_ref, shared_ref, small_ref, spread_ref) = refs[14:27]
-    (page_sem, tap_sem, write_sem, sum_send, sum_recv, small_send, small_recv) = refs[27:34]
-    sems = refs[34:]
+    (x_ref, z_ref, turned_ref, own_ref, r0_ref, half_ref, r1_ref, quarter_ref, r2_ref, eighth_ref, r3_ref, gathered_ref, full_ref, load_sem, store_sem) = refs[:15]
+    (padded_ref, grad_ref, page_ref, joined_ref, zm_ref, pair_ref, part_ref, wide_ref, tap_ref, sums_ref, shared_ref, small_ref, spread_ref) = refs[15:28]
+    (page_sem, tap_sem, write_sem, sum_send, sum_recv, small_send, small_recv) = refs[28:35]
+    sems = refs[35:]
     count, half = grad_ref.shape
     pitch = wide_ref.shape[0]
     tiles = count // pitch
@@ -904,10 +905,10 @@
     def part(start, size):
         return pl.ds(pl.multiple_of(start, size), size)
 
-    def far(stage, k, slot, source, target, peer):
+    def far(stage, k, turn, source, target, peer):
         send, recv = sems[2 * stage], sems[2 * stage + 1]
         return pltpu.make_async_remote_copy(
-            src_ref=source, dst_ref=target, send_sem=send.at[k, slot], recv_sem=recv.at[k, slot], device_id=peer, device_id_type=MESH
+            src_ref=source, dst_ref=target, send_sem=send.at[k, turn], recv_sem=recv.at[k, turn], device_id=peer, device_id_type=MESH
         )
 
     first = (x, y)
@@ -915,39 +916,39 @@
     sides = (to_x, to_y)
 
     def copies(stage, c):
-        slot, keep = c % 2, c % KEPT
+        slot, turn, keep = c % 2, c % 4, c % KEPT
         base = core * (block // 2)
         if stage == 0:
-            return [far(0, 0, slot, own_ref.at[slot, part((1 - core) * (block // 2), block // 2)], r0_ref.at[slot], to_core)]
+            return [far(0, 0, turn, own_ref.at[slot, part((1 - core) * (block // 2), block // 2)], r0_ref.at[slot], to_core)]
         if stage == 1:
             return [
-                far(1, k, slot, half_ref.at[slot, part((1 - first[k]) * (block // 4), block // 4), columns[k]], r1_ref.at[slot, :, columns[k]], sides[k])
+                far(1, k, turn, half_ref.at[slot, part((1 - first[k]) * (block // 4), block // 4), columns[k]], r1_ref.at[turn, :, columns[k]], sides[k])
                 for k in (0, 1)
             ]
         if stage == 2:
             return [
-                far(2, k, slot, quarter_ref.at[slot, part((1 - second[k]) * (block // 8), block // 8), columns[k]], r2_ref.at[slot, :, columns[k]], sides[1 - k])
+                far(2, k, turn, quarter_ref.at[slot, part((1 - second[k]) * (block // 8), block // 8), columns[k]], r2_ref.at[turn, :, columns[k]], sides[1 - k])
                 for k in (0, 1)
             ]
         if stage == 3:
             return [
-                far(3, k, slot, eighth_ref.at[slot, part(depth[k] * (block // 32), block // 32)], r3_ref.at[slot, k], to_z[k]) for k in (0, 1, 2)
+                far(3, k, turn, eighth_ref.at[slot, part(depth[k] * (block // 32), block // 32)], r3_ref.at[slot, k], to_z[k]) for k in (0, 1, 2)
             ]
+        if stage == 4:
+            spot = gathered_ref.at[slot, part(z * (block // 32), block // 32)]
+            return [far(4, k, turn, spot, spot, to_z[k]) for k in (0, 1, 2)]
         made = []
         for k in (0, 1):
             eighth = base + first[k] * (block // 4) + second[k] * (block // 8)
-            if stage == 4:
-                spot = full_ref.at[keep, part(eighth + z * (block // 32), block // 32), columns[k]]
-                made += [far(4, 3 * k + d, slot, spot, spot, to_z[d]) for d in (0, 1, 2)]
-            elif stage == 5:
+            if stage == 5:
                 spot = full_ref.at[keep, part(eighth, block // 8), columns[k]]
-                made.append(far(5, k, slot, spot, spot, sides[1 - k]))
+                made.append(far(5, k, turn, spot, spot, sides[1 - k]))
             elif stage == 6:
                 spot = full_ref.at[keep, part(base + first[k] * (block // 4), block // 4), columns[k]]
-                made.append(far(6, k, slot, spot, spot, sides[k]))
+                made.append(far(6, k, turn, spot, spot, sides[k]))
         if stage == 7:
             spot = full_ref.at[keep, part(base, block // 2)]
-            made.append(far(7, 0, slot, spot, spot, to_core))
+            made.append(far(7, 0, turn, spot, spot, to_core))
         return made
 
     def begin(stage, c):
@@ -963,7 +964,9 @@
             return []
         (left, begin_part, parts), right, _ = jobs[j]
         slot = j % 2
-        made = [pltpu.make_async_copy(lefts[left].at[begin_part : begin_part + parts], x_ref.at[slot, 0:parts], load_sem.at[slot, 0])]
+        made = []
+        if j < 2 or jobs[j - 2] is None or jobs[j - 2][0] != jobs[j][0]:
+            made.append(pltpu.make_async_copy(lefts[left].at[begin_part : begin_part + parts], x_ref.at[slot, 0:parts], load_sem.at[slot, 0]))
         source = {"pair": pair_ref, "part": part_ref, 0: rights[0], 1: rights[1]}.get(right)
         if source is not None:
             made.append(pltpu.make_async_copy(source, z_ref.at[slot], load_sem.at[slot, 1]))
@@ -1166,18 +1169,18 @@
         settled(grad_ref, zm_ref, s_split, 1, g_split, upper, keep)
         write_main.start()
 
-    FIRST_TAP = 6
+    FIRST_TAP = 4
     hosted = {
-        2: [functools.partial(stacked, 0)],
-        3: [functools.partial(stacked, 1), middle_slopes],
-        4: [middle],
-        5: [prepare],
-        15: [inner_slope],
-        16: [load_zm.wait, lambda: sum_finish(0), functools.partial(inner_tile, 0), functools.partial(inner_tile, 1)],
-        17: [functools.partial(inner_tile, 2), functools.partial(inner_tile, 3), lambda: sum_start(1)],
-        18: [lambda: sum_finish(1), small_start],
-        19: [main_settle],
-        20: [small_finish, write_part.wait, write_main.wait],
+        0: [functools.partial(stacked, 0)],
+        1: [functools.partial(stacked, 1), middle_slopes],
+        2: [middle],
+        3: [prepare],
+        13: [inner_slope],
+        14: [load_zm.wait, lambda: sum_finish(0), functools.partial(inner_tile, 0), functools.partial(inner_tile, 1)],
+        15: [functools.partial(inner_tile, 2), functools.partial(inner_tile, 3), lambda: sum_start(1)],
+        16: [lambda: sum_finish(1), small_start],
+        17: [main_settle],
+        18: [small_finish, write_part.wait, write_main.wait],
     }
 
     sums_ref[...] = jnp.zeros_like(sums_ref)
@@ -1213,7 +1216,7 @@
 
             return wrap
 
-        @stage(7, 8)
+        @stage(7, LAGS[7])
         def _(c):
             finish(7, c)
 
@@ -1225,9 +1228,13 @@
 
         for number in (6, 5, 4):
 
-            @stage(number, number + 1)
+            @stage(number, LAGS[number])
             def _(c, number=number):
                 finish(number, c)
+                if number == 4:
+                    for k in (0, 1):
+                        row = core * (block // 2) + first[k] * (block // 4) + second[k] * (block // 8)
+                        full_ref[c % KEPT, part(row, block // 8), columns[k]] = gathered_ref[c % 2, :, columns[k]]
                 begin(number + 1, c)
 
         for j in range(total):
@@ -1248,35 +1255,33 @@
         def _():
             tap_gradient(t % 2)
 
-        @stage(3, 4)
+        @stage(3, LAGS[3])
         def _(c):
             finish(3, c)
-            slot, keep = c % 2, c % KEPT
+            slot = c % 2
             value = eighth_ref[slot, part(z * (block // 32), block // 32), :]
             for k in (0, 1, 2):
                 value = value + r3_ref[slot, k]
-            for k in (0, 1):
-                row = core * (block // 2) + first[k] * (block // 4) + second[k] * (block // 8) + z * (block // 32)
-                full_ref[keep, part(row, block // 32), k * mid : (k + 1) * mid] = value[:, k * mid : (k + 1) * mid]
+            gathered_ref[slot, part(z * (block // 32), block // 32), :] = value
             begin(4, c)
 
-        @stage(2, 3)
+        @stage(2, LAGS[2])
         def _(c):
             finish(2, c)
             slot = c % 2
             for k in (0, 1):
-                eighth_ref[slot, :, columns[k]] = quarter_ref[slot, part(second[k] * (block // 8), block // 8), columns[k]] + r2_ref[slot, :, columns[k]]
+                eighth_ref[slot, :, columns[k]] = quarter_ref[slot, part(second[k] * (block // 8), block // 8), columns[k]] + r2_ref[c % 4, :, columns[k]]
             begin(3, c)
 
-        @stage(1, 2)
+        @stage(1, LAGS[1])
         def _(c):
             finish(1, c)
             slot = c % 2
             for k in (0, 1):
-                quarter_ref[slot, :, columns[k]] = half_ref[slot, part(first[k] * (block // 4), block // 4), columns[k]] + r1_ref[slot, :, columns[k]]
+                quarter_ref[slot, :, columns[k]] = half_ref[slot, part(first[k] * (block // 4), block // 4), columns[k]] + r1_ref[c % 4, :, columns[k]]
             begin(2, c)
 
-        @stage(0, 1)
+        @stage(0, LAGS[0])
         def _(c):
             finish(0, c)
             slot = c % 2
@@ -1307,8 +1312,8 @@
     scratch = [
         vmem((2, 2, count, block), BF16), vmem((2, 2, count, block), BF16), vmem((block, count), BF16),
         vmem((2, block, block), F32), vmem((2, block // 2, block), F32), vmem((2, block // 2, block), F32),
-        vmem((2, block // 4, block), F32), vmem((2, block // 4, block), F32), vmem((2, block // 8, block), F32), vmem((2, block // 8, block), F32),
-        vmem((2, 3, block // 32, block), F32), vmem((KEPT, block, block), F32),
+        vmem((4, block // 4, block), F32), vmem((2, block // 4, block), F32), vmem((4, block // 8, block), F32), vmem((2, block // 8, block), F32),
+        vmem((2, 3, block // 32, block), F32), vmem((2, block // 8, block), F32), vmem((KEPT, block, block), F32),
         dma((2, 2)), dma((KEPT,)),
         vmem((count + 2 * GUARD, block), F32), vmem((count, block), F32), vmem((count, block), F32), vmem((count, block), F32),
         vmem((count, block), F32), vmem((2, count, block), BF16), vmem((2, count, block), BF16), vmem((pitch, block), F32),
@@ -1316,8 +1321,8 @@
         vmem((16, block), F32), vmem((8, 16, block), F32),
         dma((3,)), dma((2,)), dma((2,)), dma((5, 3)), dma((5, 3)), dma((7,)), dma((7,)),
     ]
-    for width in (1, 2, 2, 3, 6, 2, 2, 1):
-        scratch += [dma((width, 2)), dma((width, 2))]
+    for width in (1, 2, 2, 3, 3, 2, 2, 1):
+        scratch += [dma((width, 4)), dma((width, 4))]
     return pl.pallas_call(
         functools.partial(reduce_body, jobs, side, slots),
         in_specs=[hbm] * (len(lefts) + len(rights) + len(hosted)) + [vmem_spec] * len(constants),
@@ -1422,7 +1427,6 @@
         )
         jobs = [((0, 0, 2), 0, (4, (low, low))), ((0, 0, 2), 1, (4, (low, high)))]
         jobs += [((1, 0, 2), 0, (4, (high, low))), ((1, 0, 2), 1, (4, (high, high)))]
-        jobs += [None, None]
         jobs += [((4, 0, 2), None, (2, (tap,))) for tap in range(9)]
         jobs += [((2, 0, 2), "pair", (3, (every, every)))]
         jobs += [((3, 0, 1), "part", (0, (low, low))), ((3, 1, 1), "part", (0, (high, low)))]

time: 333 us -> 331 us (level)
  no operation moved by 1% of the time
where the time goes in v6:
time: 331 us; the launch traced here: 326 us
  Pallas kernels  323 us (98%)
    pallas_call x1, Pallas kernels, reduce_call(): pl.pallas_call(functools.partial(reduce_body, jobs, side, slots), in_spec...  218 us
    pallas_call x1, Pallas kernels, front_call(): pl.pallas_call(functools.partial(front_body, side, slots), in_specs=[hbm]...  85.2 us
    pallas_call x1, Pallas kernels, final_call(): pl.pallas_call(functools.partial(final_body, pieces), in_specs=[hbm] * (l...  20.1 us

profile of v6, /device:TPU:0, one launch (start us, length us, event | category | flops | bytes accessed | tf_op | source)
XLA Modules:
  0.0 326.2 jit_solution(14158485783754736367)
XLA Ops:
  1.3 85.2 %shard_map.323 = (bf16[2,1472,512]{2,1,0:T(8,128)(2,1)}, f32[1472,512]{1,0:T(8,128)}, f32[1472,512]{1,0:T(8,128)}, bf16[2,1472,512]{2,1,0:T(8,128)(2,1)}, bf16[2...) custom-call(bf16[361,4,1024]{2,1,0:T(4,128)(2,1)} %bitcast.37, ...), custom_call_target="tpu_custom_call" | custom-call | tf_op jit(solution)/shard_map/pallas_call | solution.py:860
  86.5 218.1 %shard_map.324 = (f32[1024,1024]{1,0:T(8,128)}, f32[512,512]{1,0:T(8,128)}, f32[9,512,512]{2,1,0:T(8,128)}, f32[512,512]{1,0:T(8,128)}, f32[1024,1024]{1,0:T(8,1...) custom-call(bf16[2,1472,512]{2,1,0:T(8,128)(2,1)} %get-tuple-element.49.refs_0_, ...), custom_call_target="tpu_custom_call" | custom-call | tf_op jit(solution)/shard_map/pallas_call | solution.py:1326
  304.6 0.0 copy-start
  304.7 20.1 %shard_map.325 = (f32[361,4,1024]{2,1,0:T(4,128)}, f32[1024,1024]{1,0:T(8,128)}, f32[512,512]{1,0:T(8,128)}, f32[9,512,512]{2,1,0:T(8,128)}, f32[512,512]{1,0:T(...) custom-call(f32[361,4,1024]{2,1,0:T(4,128)} %get-tuple-element.48.refs_0_, ...), custom_call_target="tpu_custom_call" | custom-call | tf_op jit(solution)/shard_map/pallas_call | solution.py:520
  324.7 0.0 copy-done
  324.8 0.6 fusion.1
  325.4 0.6 fusion
  (1 shorter events, 0.0 us)
Async XLA Ops:
  304.6 20.1 %copy-start = (f32[16,512]{1,0:T(8,128)S(1)}, f32[16,512]{1,0:T(8,128)}, u32[]{:S(2)}) copy-start(f32[16,512]{1,0:T(8,128)} %get-tuple-element.74) | copy-start | bytes 98308

commit v7 on v6

--- a/solution.py
+++ b/solution.py
@@ -548,7 +548,7 @@
     )(x, dz)
 
 
-SPLIT, INNER, SPREAD, TRANS, OUT, BACK_OUT = range(6)
+SPLIT, INNER, SPREAD, TRANS, OUT, BACK_OUT, SPLIT_LOW = range(7)
 
 
 def front_body(side, slots, *refs):
@@ -610,12 +610,13 @@
             for k, peer in enumerate(group)
         ]
 
-    def exchange(which, width, beside=None):
+    def exchange(which, width, beside=None, start=0, target=None):
         wide, copies = sum_copies(which)
-        pieces = [(j, slice(j * 128, (j + 1) * 128)) for j in range(width // 128)]
+        pieces = [(j, slice(start + j * 128, start + (j + 1) * 128)) for j in range(width // 128)]
+        kept = which if target is None else target
         for j, piece in pieces:
-            packed_ref[which, j : j + 1, 0:128] = local_ref[which, 0:1, piece]
-            packed_ref[which, j : j + 1, 128:256] = local_ref[which, 1:2, piece]
+            packed_ref[which, j : j + 1, 0:128] = local_ref[kept, 0:1, piece]
+            packed_ref[which, j : j + 1, 128:256] = local_ref[kept, 1:2, piece]
         if which == SPLIT:
             packed_ref[which, 0:1, 256:384] = local_ref[which, 2:3, 0:128]
         for copy in copies:
@@ -629,8 +630,8 @@
         for k in range(1, members):
             value = value + shared_ref[which, k, :, wide]
         for j, piece in pieces:
-            total_ref[which, 0:1, piece] = value[j : j + 1, 0:128]
-            total_ref[which, 1:2, piece] = value[j : j + 1, 128:256]
+            total_ref[kept, 0:1, piece] = value[j : j + 1, 0:128]
+            total_ref[kept, 1:2, piece] = value[j : j + 1, 128:256]
         if which == SPLIT:
             total_ref[which, 2:3, 0:128] = value[0:1, 256:384]
 
@@ -686,10 +687,8 @@
     cot_load(0).start()
     write("x", q0, x_out)
     weights[0].wait()
-    p0[...] = dot(q0[0], w_split[low, low]) + dot(q0[1], w_split[high, low])
     p1[0:count, :] = dot(q0[0], w_split[low, high]) + dot(q0[1], w_split[high, high])
     write("zm", p1.at[0:count], zm_out)
-    write("zp", p0, zp_out)
 
     def add_squares(which, z_ref, columns, masked=False):
         def body(r, carry):
@@ -700,25 +699,33 @@
         zero = jnp.zeros((8, half), F32)
         add_sums(local_ref.at[which], columns, over_rows(count, body, (zero, zero)))
 
-    add_squares(SPLIT, p0, low)
     add_squares(SPLIT, p1, high)
     local_ref[SPLIT, 2:3, 0:128] = jnp.sum(mask_ref[...], axis=0, keepdims=True)
     pl.semaphore_wait(barrier, members - 1)
-    exchange(SPLIT, 2 * half)
-
-    mean, scale, shift = affine(SPLIT, g_split, b_split, high)
-
-    def main_rows(r, _):
-        act = activate(p1, r, mean, scale, shift)
-        p2[r, :] = act
-        split_store(q2, (r,), act)
-
-    over_rows(count, main_rows)
-    write("main", q2, main_out)
-    weights[1].wait()
-    p3[...] = product2(q2, (), w_inner[...])
-    write("zi", p3, zi_out)
-    add_squares(INNER, p3, low)
+
+    def split_low():
+        p0[...] = dot(q0[0], w_split[low, low]) + dot(q0[1], w_split[high, low])
+        write("zp", p0, zp_out)
+        add_squares(SPLIT, p0, low)
+
+    exchange(SPLIT, half, split_low, half)
+
+    def inner():
+        mean, scale, shift = affine(SPLIT, g_split, b_split, high)
+
+        def main_rows(r, _):
+            act = activate(p1, r, mean, scale, shift)
+            p2[r, :] = act
+            split_store(q2, (r,), act)
+
+        over_rows(count, main_rows)
+        write("main", q2, main_out)
+        weights[1].wait()
+        p3[...] = product2(q2, (), w_inner[...])
+        write("zi", p3, zi_out)
+        add_squares(INNER, p3, low)
+
+    exchange(SPLIT_LOW, half, inner, 0, SPLIT)
     mean_p, scale_p, shift_p = affine(SPLIT, g_split, b_split, low)
 
     def part_rows(r, _):
@@ -854,8 +861,8 @@
     scratch += [
         vmem((pitch, full), F32), vmem((2, pitch // slots, slots, full), BF16), vmem((pitch // slots, slots, full), F32), vmem((pitch // slots, slots, full), F32),
         vmem((full, full), BF16), vmem((half, half), BF16), vmem((9, half, half), BF16), vmem((half, half), BF16), vmem((full, full), BF16),
-        vmem((6, 8, full), F32), vmem((6, 8, 384), F32), vmem((6, members, 8, 384), F32),
-        dma((5,)), dma((2,)), dma(()), dma(()), dma((16,)), dma((6, members - 1)), dma((6, members - 1)),
+        vmem((6, 8, full), F32), vmem((7, 8, 384), F32), vmem((7, members, 8, 384), F32),
+        dma((5,)), dma((2,)), dma(()), dma(()), dma((16,)), dma((7, members - 1)), dma((7, members - 1)),
     ]
     return pl.pallas_call(
         functools.partial(front_body, side, slots),

time: 331 us -> 328 us (level)
  no operation moved by 1% of the time
where the time goes in v7:
time: 328 us; the launch traced here: 324 us
  Pallas kernels  321 us (98%)
    pallas_call x1, Pallas kernels, reduce_call(): pl.pallas_call(functools.partial(reduce_body, jobs, side, slots), in_spec...  218 us
    pallas_call x1, Pallas kernels, front_call(): pl.pallas_call(functools.partial(front_body, side, slots), in_specs=[hbm]...  83.3 us
    pallas_call x1, Pallas kernels, final_call(): pl.pallas_call(functools.partial(final_body, pieces), in_specs=[hbm] * (l...  20.1 us

profile of v7, /device:TPU:0, one launch (start us, length us, event | category | flops | bytes accessed | tf_op | source)
XLA Modules:
  0.0 323.8 jit_solution(4037439580862595650)
XLA Ops:
  1.3 83.3 %shard_map.323 = (bf16[2,1472,512]{2,1,0:T(8,128)(2,1)}, f32[1472,512]{1,0:T(8,128)}, f32[1472,512]{1,0:T(8,128)}, bf16[2,1472,512]{2,1,0:T(8,128)(2,1)}, bf16[2...) custom-call(bf16[361,4,1024]{2,1,0:T(4,128)(2,1)} %bitcast.37, ...), custom_call_target="tpu_custom_call" | custom-call | tf_op jit(solution)/shard_map/pallas_call | solution.py:867
  84.6 217.6 %shard_map.324 = (f32[1024,1024]{1,0:T(8,128)}, f32[512,512]{1,0:T(8,128)}, f32[9,512,512]{2,1,0:T(8,128)}, f32[512,512]{1,0:T(8,128)}, f32[1024,1024]{1,0:T(8,1...) custom-call(bf16[2,1472,512]{2,1,0:T(8,128)(2,1)} %get-tuple-element.49.refs_0_, ...), custom_call_target="tpu_custom_call" | custom-call | tf_op jit(solution)/shard_map/pallas_call | solution.py:1333
  302.2 0.0 copy-start
  302.2 20.1 %shard_map.325 = (f32[361,4,1024]{2,1,0:T(4,128)}, f32[1024,1024]{1,0:T(8,128)}, f32[512,512]{1,0:T(8,128)}, f32[9,512,512]{2,1,0:T(8,128)}, f32[512,512]{1,0:T(...) custom-call(f32[361,4,1024]{2,1,0:T(4,128)} %get-tuple-element.48.refs_0_, ...), custom_call_target="tpu_custom_call" | custom-call | tf_op jit(solution)/shard_map/pallas_call | solution.py:520
  322.3 0.0 copy-done
  322.4 0.6 fusion.1
  323.0 0.6 fusion
  (1 shorter events, 0.0 us)
Async XLA Ops:
  302.2 20.1 %copy-start = (f32[16,512]{1,0:T(8,128)S(1)}, f32[16,512]{1,0:T(8,128)}, u32[]{:S(2)}) copy-start(f32[16,512]{1,0:T(8,128)} %get-tuple-element.74) | copy-start | bytes 98308
